TPU v7x, 512 devices: a whole 4x8x8 slice. The times are simulated.
512 devices in a mesh: gx: 8 (over y), gy: 4 (over z_lo, core), gz: 16 (over x, z_hi).
Axes of the slice: x: 4, y: 8, z: 8 (z_hi: 4, z_lo: 2; z = z_hi * 2 + z_lo), core: 2. Of those that a mesh axis runs over, the one named last changes fastest.
Arguments:
- features: bfloat16 [393216, 256], P(('gx', 'gy', 'gz')), may hold values from -6 to 6
- tile_values: bfloat16 [7168, 8, 128, 128], P(('gx', 'gy', 'gz')), as said below
- tile_columns: int32 [7168, 8], P(('gx', 'gy', 'gz')), may hold values from 0 to 13
- tile_present: int32 [7168, 8], P(('gx', 'gy', 'gz')), may hold values 0 or 1
- host_root: int32 [4096], P(('gx', 'gy')), may hold values from 0 to 15, as said below
- host_block: int32 [4096], P(('gx', 'gy')), may hold values from 0 to 1
- self_one: bfloat16 [256, 256], replicated, may hold values from -0.375 to 0.375
- neigh_one: bfloat16 [256, 256], replicated, may hold values from -0.375 to 0.375
- scale_one: float32 [256], replicated, may hold values from 0.25 to 1.75
- shift_one: float32 [256], replicated, may hold values from -3 to 3
- self_two: bfloat16 [256, 256], replicated, may hold values from -0.375 to 0.375
- neigh_two: bfloat16 [256, 256], replicated, may hold values from -0.375 to 0.375
Outputs:
- embedding: bfloat16 [393216, 256], P(('gx', 'gy', 'gz'))
Inputs may be any that keep to these rules, and one draw needn't show every extreme that they name: `host_root`: never the holder's own gz index; the 8 replica slots of one device name 8 different devices. `tile_values`: entries lie in 0 to 1.8 / sqrt(1024).
All inputs are finite; a program needn't handle non-finite values. No bound on the sum of `tile_present` on one device may be relied on, other than what follows from the above.
Results may differ from a plain program's by a relative error of at most 0.012.
Values may be sent and summed in bfloat16 or wider, within the bound.
No kernel may reach another device: no remote copies, remote signals or barrier semaphores. Data moves between devices by JAX's collectives and lax.ppermute only.
A program may use at most 64 MiB of HBM per device.

v0:
```python
import jax
import jax.numpy as jnp
from jax import lax
from jax.sharding import Mesh
from jax.sharding import PartitionSpec as P

OWN = 4
SPLIT = 2
GZ = ("gz_0", "gz_1")
GX_GY_GZ = ("gx", "gy_0", "gy_1", "gz_0", "gz_1")
GY = ("gy_0", "gy_1")
GX_GY = ("gx", "gy_0", "gy_1")


def over_axes(value, axes):
    for axis in axes:
        value = lax.psum(value, axis)
    return value


def per_device(
    features,
    tile_values,
    tile_columns,
    tile_present,
    host_root,
    host_block,
    self_one,
    neigh_one,
    scale_one,
    shift_one,
    self_two,
    neigh_two,
):
    tile = tile_values.shape[2]
    width = features.shape[1]
    rooted = features.shape[0] // tile
    slots = tile_values.shape[0]
    hosts = slots - rooted
    group = lax.axis_size(GZ)
    mine = lax.axis_index(GZ)
    root_table = host_root.reshape(group, hosts)
    block_table = host_block.reshape(group, hosts)
    my_roots = lax.dynamic_index_in_dim(root_table, mine, 0, keepdims=False)
    peers = jnp.arange(group, dtype=jnp.int32)
    splits = jnp.arange(SPLIT, dtype=jnp.int32)
    matched = (root_table == mine)[:, :, None] & (block_table[:, :, None] == splits[None, None, :])
    holders = jnp.sum(matched.astype(jnp.int32), axis=1).astype(jnp.bfloat16)
    routing = (my_roots[:, None] == peers[None, :]).astype(jnp.bfloat16)

    def spread(rows):
        split_rows = rows.reshape(rooted, tile, width)[OWN:]
        outgoing = jnp.einsum(
            "qs,sif->qif", holders, split_rows, preferred_element_type=jnp.float32
        ).astype(jnp.bfloat16)
        incoming = lax.all_to_all(outgoing, GZ, split_axis=0, concat_axis=0, tiled=True)
        return incoming[my_roots]

    def collect(replica_partial):
        outgoing = jnp.einsum(
            "hq,hif->qif", routing, replica_partial, preferred_element_type=jnp.float32
        ).astype(jnp.bfloat16)
        incoming = lax.all_to_all(outgoing, GZ, split_axis=0, concat_axis=0, tiled=True)
        return jnp.einsum("qs,qif->sif", holders, incoming, preferred_element_type=jnp.float32)

    def aggregate(view):
        picked = view[tile_columns]
        picked = jnp.where(tile_present[:, :, None, None] > 0, picked, jnp.zeros_like(picked))
        return jnp.einsum("bkij,bkjf->bif", tile_values, picked, preferred_element_type=jnp.float32)

    def layer(rows, w_self, w_neigh):
        hosted = spread(rows)
        view = jnp.concatenate([rows.reshape(rooted, tile, width), hosted], axis=0)
        partial_value = aggregate(view)
        remote = collect(partial_value[rooted:].astype(jnp.bfloat16))
        total = partial_value[:rooted].at[OWN:].add(remote)
        neighbours = total.astype(jnp.bfloat16).reshape(-1, width)
        return jnp.dot(rows, w_self, preferred_element_type=jnp.float32) + jnp.dot(
            neighbours, w_neigh, preferred_element_type=jnp.float32
        )

    first = layer(features, self_one, neigh_one)
    sums, squares = (
        over_axes(jnp.sum(first, axis=0), GX_GY_GZ),
        over_axes(jnp.sum(first * first, axis=0), GX_GY_GZ),
    )
    count = first.shape[0] * lax.axis_size("gx") * lax.axis_size(GY) * group
    mean = sums / count
    var = squares / count - mean * mean
    hidden = jax.nn.relu((first - mean) * lax.rsqrt(var + 1e-05) * scale_one + shift_one).astype(
        jnp.bfloat16
    )
    second = layer(hidden, self_two, neigh_two)
    return second.astype(jnp.bfloat16)


def solution(mesh):
    finer = Mesh(
        mesh.devices.reshape(mesh.shape["gx"], 2, 2, 4, 4), ("gx", "gy_0", "gy_1", "gz_0", "gz_1")
    )
    return jax.shard_map(
        per_device,
        mesh=finer,
        in_specs=(
            P(GX_GY_GZ, None),
            P(GX_GY_GZ, None, None, None),
            P(GX_GY_GZ, None),
            P(GX_GY_GZ, None),
            P(GX_GY),
            P(GX_GY),
            P(),
            P(),
            P(),
            P(),
            P(),
            P(),
        ),
        out_specs=P(GX_GY_GZ, None),
        check_vma=False,
    )
```

profile of v0, /device:TPU:64, one launch (start us, length us, event | category | flops | bytes accessed | tf_op | source)
XLA Modules:
  0.0 216.8 jit_solution(8671801710749799438)
XLA Ops:
  0.0 0.8 reshape.121
  0.9 0.7 eq.42
  1.8 0.9 slice.76
  3.2 1.3 copy.47
  4.5 12.0 %all-to-all-start = ((bf16[16,128,256]{2,1,0:T(8,128)(2,1)}), bf16[16,128,256]{2,1,0:T(8,128)(2,1)S(1)}, u32[]{:S(2)}, u32[]{:S(2)}) async-start(bf16[16,128,256]{2,1,0:T(8,128)(2,1)} %copy.47), calls=%async_computation | async-start | bytes 2097152 | tf_op jit(solution)/shard_map/all_to_all | solution.py:56
  16.9 29.5 %all-to-all-done = bf16[16,128,256]{2,1,0:T(8,128)(2,1)S(1)} async-done(((bf16[16,128,256]{2,1,0:T(8,128)(2,1)}), bf16[16,128,256]{2,1,0:T(8,128)(2,1)S(1)}, u32[]{:S(2)}, u32[]{:S(2)}) %all-to-all-start) | async-done | bytes 1048608 | tf_op jit(solution)/shard_map/all_to_all | solution.py:56
  46.4 0.6 gather_fusion
  47.0 6.3 %gather_fusion.1 = bf16[112,128,256]{2,1,0:T(8,128)(2,1)} fusion(bf16[14,128,256]{2,1,0:T(8,128)(2,1)S(1)} %pad_maximum_fusion, s32[1024]{0:T(1024)S(1)} %pad_clamp_fusion), kind=kCustom, calls=%fused_computation.1 | custom fusion | bytes 14680512 | tf_op jit(solution)/shard_map/gather | solution.py:67
  53.3 5.7 %fusion.8 = f32[14,128,256]{2,1,0:T(8,128)S(1)} fusion(bf16[14,8,128,128]{3,2,1,0:T(8,128)(2,1)} %param.17, bf16[14,8,128,256]{3,2,1,0:T(8,128)(2,1)} %bitcast.48, pred[14,8]{1,0:T(8,128)(4,1)S(1)} %copy.43), kind=kOutput, calls=%fused_computation.12 | convolution fusion | flops 943194112 | bytes 12845168 | tf_op jit(solution)/shard_map/bkij,bkjf->bif/dot_general | solution.py:69
  59.7 0.6 copy-done.3
  60.3 1.3 copy.50
  61.6 3.7 %all-to-all-start.1 = ((bf16[16,128,256]{2,1,0:T(8,128)(2,1)}), bf16[16,128,256]{2,1,0:T(8,128)(2,1)S(1)}, u32[]{:S(2)}, u32[]{:S(2)}) async-start(bf16[16,128,256]{2,1,0:T(8,128)(2,1)} %copy.50), calls=%async_computation.1 | async-start | bytes 2097152 | tf_op jit(solution)/shard_map/all_to_all | solution.py:63
  65.7 1.2 slice.94
  66.9 25.8 %all-to-all-done.1 = bf16[16,128,256]{2,1,0:T(8,128)(2,1)S(1)} async-done(((bf16[16,128,256]{2,1,0:T(8,128)(2,1)}), bf16[16,128,256]{2,1,0:T(8,128)(2,1)S(1)}, u32[]{:S(2)}, u32[]{:S(2)}) %all-to-all-start.1) | async-done | bytes 1048608 | tf_op jit(solution)/shard_map/all_to_all | solution.py:63
  92.6 0.7 fusion.17
  93.3 1.0 fusion.22
  94.6 17.6 %all-reduce = (f32[256]{0:T(256)S(1)}, f32[256]{0:T(256)S(1)}) all-reduce(f32[256]{0:T(256)S(1)} %get-tuple-element.30, f32[256]{0:T(256)S(1)} %get-tuple-element.29), channel_id=1, replica_groups=mesh['gx'=8,'gy_0'=2,'gy_1'=2,'gz_0'=4,'gz_1'=4] {'gx'}, use_global_device_ids=true, to_apply=%region_8.9 | all-reduce | flops 512 | bytes 4096 | tf_op jit(solution)/shard_map/psum | solution.py:17
  112.2 4.9 %all-reduce.4 = (f32[256]{0:T(256)S(1)}, f32[256]{0:T(256)S(1)}) all-reduce(f32[256]{0:T(256)S(1)} %get-tuple-element.31, f32[256]{0:T(256)S(1)} %get-tuple-element.32), channel_id=1, replica_groups=mesh['gx'=8,'gy_0'=2,'gy_1'=2,'gz_0'=4,'gz_1'=4] {'gy_0'}, use_global_device_ids=true, to_apply=%region_9.10 | all-reduce | flops 512 | bytes 4096 | tf_op jit(solution)/shard_map/psum | solution.py:17
  117.1 2.4 %all-reduce.3 = (f32[256]{0:T(256)S(1)}, f32[256]{0:T(256)S(1)}) all-reduce(f32[256]{0:T(256)S(1)} %get-tuple-element.39, f32[256]{0:T(256)S(1)} %get-tuple-element.40), channel_id=1, replica_groups=mesh['gx'=8,'gy_0'=2,'gy_1'=2,'gz_0'=4,'gz_1'=4] {'gy_1'}, use_global_device_ids=true, to_apply=%region_10.11 | all-reduce | flops 512 | bytes 4096 | tf_op jit(solution)/shard_map/psum | solution.py:17
  119.6 8.6 %all-reduce.2 = (f32[256]{0:T(256)S(1)}, f32[256]{0:T(256)S(1)}) all-reduce(f32[256]{0:T(256)S(1)} %get-tuple-element.37, f32[256]{0:T(256)S(1)} %get-tuple-element.38), channel_id=1, replica_groups=mesh['gx'=8,'gy_0'=2,'gy_1'=2,'gz_0'=4,'gz_1'=4] {'gz_0'}, use_global_device_ids=true, to_apply=%region_11.12 | all-reduce | flops 512 | bytes 4096 | tf_op jit(solution)/shard_map/psum | solution.py:17
  128.2 10.2 %all-reduce.1 = (f32[256]{0:T(256)S(1)}, f32[256]{0:T(256)S(1)}) all-reduce(f32[256]{0:T(256)S(1)} %get-tuple-element.35, f32[256]{0:T(256)S(1)} %get-tuple-element.36), channel_id=1, replica_groups=mesh['gx'=8,'gy_0'=2,'gy_1'=2,'gz_0'=4,'gz_1'=4] {'gz_1'}, use_global_device_ids=true, to_apply=%region_12.13 | all-reduce | flops 512 | bytes 4096 | tf_op jit(solution)/shard_map/psum | solution.py:17
  139.4 29.4 %all_to_all.20 = bf16[16,128,256]{2,1,0:T(8,128)(2,1)S(1)} all-to-all(bf16[16,128,256]{2,1,0:T(8,128)(2,1)S(1)} %copy.54), channel_id=1, replica_groups=mesh['gx'=8,'gy_0'=2,'gy_1'=2,'gz_0'=4,'gz_1'=4] {'gz_0','gz_1'}, dimensions={0} | all-to-all | bytes 2097152 | tf_op jit(solution)/shard_map/all_to_all | solution.py:56
  169.5 6.3 %gather_fusion.3 = bf16[112,128,256]{2,1,0:T(8,128)(2,1)} fusion(bf16[14,128,256]{2,1,0:T(8,128)(2,1)S(1)} %pad_maximum_fusion.1, s32[1024]{0:T(1024)S(1)} %pad_clamp_fusion), kind=kCustom, calls=%fused_computation.3 | custom fusion | bytes 14680512 | tf_op jit(solution)/shard_map/gather | solution.py:67
  175.8 5.7 %fusion.11 = f32[14,128,256]{2,1,0:T(8,128)S(1)} fusion(bf16[14,8,128,128]{3,2,1,0:T(8,128)(2,1)} %param.17, bf16[14,8,128,256]{3,2,1,0:T(8,128)(2,1)} %bitcast.47, pred[14,8]{1,0:T(8,128)(4,1)S(1)} %copy.43), kind=kOutput, calls=%fused_computation.13 | convolution fusion | flops 943194112 | bytes 12845168 | tf_op jit(solution)/shard_map/bkij,bkjf->bif/dot_general | solution.py:69
  182.2 0.6 copy-done.2
  182.8 1.3 copy.56
  184.1 3.9 %all-to-all-start.3 = ((bf16[16,128,256]{2,1,0:T(8,128)(2,1)}), bf16[16,128,256]{2,1,0:T(8,128)(2,1)S(1)}, u32[]{:S(2)}, u32[]{:S(2)}) async-start(bf16[16,128,256]{2,1,0:T(8,128)(2,1)} %copy.56), calls=%async_computation.3 | async-start | bytes 2097152 | tf_op jit(solution)/shard_map/all_to_all | solution.py:63
  188.2 1.2 slice.98
  189.4 24.7 %all-to-all-done.3 = bf16[16,128,256]{2,1,0:T(8,128)(2,1)S(1)} async-done(((bf16[16,128,256]{2,1,0:T(8,128)(2,1)}), bf16[16,128,256]{2,1,0:T(8,128)(2,1)S(1)}, u32[]{:S(2)}, u32[]{:S(2)}) %all-to-all-start.3) | async-done | bytes 1048608 | tf_op jit(solution)/shard_map/all_to_all | solution.py:63
  214.2 0.7 fusion.15
  214.8 1.0 fusion.21
  215.8 1.0 fusion.14
  (50 shorter events, 4.9 us)
Async XLA Ops:
  0.0 94.3 %copy-start = (bf16[256,256]{1,0:T(8,128)(2,1)S(1)}, bf16[256,256]{1,0:T(8,128)(2,1)}, u32[]{:S(2)}) copy-start(bf16[256,256]{1,0:T(8,128)(2,1)} %param.23) | copy-start | bytes 393220
  0.0 46.9 %copy-start.1 = (bf16[768,256]{1,0:T(8,128)(2,1)S(1)}, bf16[768,256]{1,0:T(8,128)(2,1)}, u32[]{:S(2)}) copy-start(bf16[768,256]{1,0:T(8,128)(2,1)} %param.16) | copy-start | bytes 1179652
  0.0 16.5 %copy-start.8 = (s32[14,8]{0,1:T(8,128)S(1)}, s32[14,8]{0,1:T(8,128)}, u32[]{:S(2)}) copy-start(s32[14,8]{0,1:T(8,128)} %param.18) | copy-start | bytes 1348
  0.0 16.7 %copy-start.7 = (s32[14,8]{0,1:T(8,128)S(1)}, s32[14,8]{0,1:T(8,128)}, u32[]{:S(2)}) copy-start(s32[14,8]{0,1:T(8,128)} %param.19) | copy-start | bytes 1348
  4.5 41.8 %all-to-all-start = ((bf16[16,128,256]{2,1,0:T(8,128)(2,1)}), bf16[16,128,256]{2,1,0:T(8,128)(2,1)S(1)}, u32[]{:S(2)}, u32[]{:S(2)}) async-start(bf16[16,128,256]{2,1,0:T(8,128)(2,1)} %copy.47), calls=%async_computation | async-start | bytes 2097152 | tf_op jit(solution)/shard_map/all_to_all | solution.py:56
  59.0 1.3 copy-start.3
  59.0 6.3 %copy-start.4 = (bf16[256,256]{1,0:T(8,128)(2,1)S(1)}, bf16[256,256]{1,0:T(8,128)(2,1)}, u32[]{:S(2)}) copy-start(bf16[256,256]{1,0:T(8,128)(2,1)} %param.22) | copy-start | bytes 393220
  61.6 31.0 %all-to-all-start.1 = ((bf16[16,128,256]{2,1,0:T(8,128)(2,1)}), bf16[16,128,256]{2,1,0:T(8,128)(2,1)S(1)}, u32[]{:S(2)}, u32[]{:S(2)}) async-start(bf16[16,128,256]{2,1,0:T(8,128)(2,1)} %copy.50), calls=%async_computation.1 | async-start | bytes 2097152 | tf_op jit(solution)/shard_map/all_to_all | solution.py:63
  65.4 73.0 %copy-start.9 = (f32[256]{0:T(256)S(1)}, f32[256]{0:T(256)}, u32[]{:S(2)}) copy-start(f32[256]{0:T(256)} %param.25) | copy-start | bytes 3076
  65.4 73.0 %copy-start.10 = (f32[256]{0:T(256)S(1)}, f32[256]{0:T(256)}, u32[]{:S(2)}) copy-start(f32[256]{0:T(256)} %param.24) | copy-start | bytes 3076
  181.5 1.3 copy-start.2
  181.5 6.5 %copy-start.5 = (bf16[256,256]{1,0:T(8,128)(2,1)S(1)}, bf16[256,256]{1,0:T(8,128)(2,1)}, u32[]{:S(2)}) copy-start(bf16[256,256]{1,0:T(8,128)(2,1)} %param.26) | copy-start | bytes 393220
  184.1 31.7 %copy-start.6 = (bf16[256,256]{1,0:T(8,128)(2,1)S(1)}, bf16[256,256]{1,0:T(8,128)(2,1)}, u32[]{:S(2)}) copy-start(bf16[256,256]{1,0:T(8,128)(2,1)} %param.27) | copy-start | bytes 393220
  184.1 30.1 %all-to-all-start.3 = ((bf16[16,128,256]{2,1,0:T(8,128)(2,1)}), bf16[16,128,256]{2,1,0:T(8,128)(2,1)S(1)}, u32[]{:S(2)}, u32[]{:S(2)}) async-start(bf16[16,128,256]{2,1,0:T(8,128)(2,1)} %copy.56), calls=%async_computation.3 | async-start | bytes 2097152 | tf_op jit(solution)/shard_map/all_to_all | solution.py:63
where the time goes:
time: 217 us
  waiting for transfers between devices  80 us (37%)
  blocking collectives  73.2 us (34%)
  local copies, waits for them, and re-layouts  24.7 us (11%)
  starting transfers between devices  19.6 us (9%)
  matrix products  16.7 us (8%)
  other arithmetic  2.34 us (1%)
    all_to_all x2, waiting for transfers between devices, collect(): lax.all_to_all(outgoing, GZ, split_axis=0, concat_axis=0, tiled=True)  50.5 us
    psum x5, blocking collectives, over_axes(): value = lax.psum(value, axis)  43.7 us
    all_to_all x1, waiting for transfers between devices, spread(): lax.all_to_all(outgoing, GZ, split_axis=0, concat_axis=0, tiled=True)  29.5 us
    all_to_all x1, blocking collectives, spread(): lax.all_to_all(outgoing, GZ, split_axis=0, concat_axis=0, tiled=True)  29.4 us
    gather x2, local copies, waits for them, and re-layouts, aggregate(): picked = view[tile_columns]  12.6 us
    all_to_all x1, starting transfers between devices, spread(): lax.all_to_all(outgoing, GZ, split_axis=0, concat_axis=0, tiled=True)  12 us
    dot_general x2, matrix products, aggregate(): jnp.einsum('bkij,bkjf->bif', tile_values, picked, preferred_element_type=...  11.3 us
    all_to_all x2, starting transfers between devices, collect(): lax.all_to_all(outgoing, GZ, split_axis=0, concat_axis=0, tiled=True)  7.59 us
  transfers between devices with their start and end apart: 3, of which 3 were waited for; matrix products, arithmetic and copies ran while one was open for 1% of the time, Pallas kernels for 0%

commit v1 on v0

v1 whole, which is shorter than its diff:
```python
import functools

import jax
import jax.numpy as jnp
from jax import lax
from jax.experimental import pallas as pl
from jax.experimental.pallas import tpu as pltpu
from jax.sharding import Mesh
from jax.sharding import PartitionSpec as P

OWN = 4
SPLIT = 2
ROOTED = 6
HOST = 8
SLOTS = 14
K = 8
TILE = 128
F = 256
GROUP = 16
CENTER_ROWS = 16
VMEM_BYTES = 12 << 20
GZ = ("gz_0", "gz_1")
GX_GY_GZ = ("gx", "gy_0", "gy_1", "gz_0", "gz_1")
GX_GY = ("gx", "gy_0", "gy_1")

f32 = jnp.float32
bf16 = jnp.bfloat16

ANY = pl.BlockSpec(memory_space=pl.ANY)
VMEM = pl.BlockSpec(memory_space=pltpu.VMEM)
SMEM = pl.BlockSpec(memory_space=pltpu.SMEM)
DMA = pltpu.SemaphoreType.DMA


def shape(dims, dtype):
    return jax.ShapeDtypeStruct(dims, dtype)


def call(body, name, flops, size, **kw):
    return pl.pallas_call(
        body,
        name=name,
        compiler_params=pltpu.CompilerParams(vmem_limit_bytes=VMEM_BYTES),
        cost_estimate=pl.CostEstimate(flops=flops, bytes_accessed=size, transcendentals=0),
        **kw,
    )


def dot(a, b):
    return jnp.dot(a, b, preferred_element_type=f32)


def my_place():
    return lax.axis_index("gz_0") * 4 + lax.axis_index("gz_1")


def send_selected(sel, blocks, out, sems):
    copies = [
        pltpu.make_async_copy(blocks.at[jnp.maximum(sel(q) - 1, 0)], out.at[q], sems.at[q])
        for q in range(GROUP)
    ]
    for c in copies:
        c.start()
    for c in copies:
        c.wait()


def outgoing_kernel(root, block, rows, out, sel, split, sem, sems):
    load = pltpu.make_async_copy(rows.at[pl.ds(OWN, SPLIT)], split, sem)
    load.start()
    mine = my_place()
    for q in range(GROUP):
        held = jnp.int32(0)
        for j in range(HOST):
            held = jnp.where(root[q * HOST + j] == mine, block[q * HOST + j] + 1, held)
        sel[q] = held
    load.wait()
    send_selected(lambda q: sel[q], split, out, sems)


def tile_row(cols, present, b, tiles, view):
    acc = None
    for k in range(K):
        slot = jnp.where(present[b, k] > 0, cols[b, k], SLOTS)
        term = dot(tiles[k], view[slot])
        acc = term if acc is None else acc + term
    return acc


def replica_rows(root, cols, present, tiles, out, view, tbuf, obuf, tsem, osem):
    mine = my_place()

    def send(h):
        return pltpu.make_async_copy(obuf.at[h], out.at[root[mine * HOST + h]], osem.at[h])

    def step(h, carry):
        pltpu.make_async_copy(tiles.at[ROOTED + h], tbuf.at[h], tsem.at[h]).wait()
        obuf[h] = tile_row(cols, present, ROOTED + h, tbuf.at[h], view).astype(bf16)

        @pl.when(h > 0)
        def _():
            send(h - 1).start()

        return carry

    lax.fori_loop(0, HOST, step, 0)
    send(HOST - 1).start()
    lax.fori_loop(0, HOST, lambda h, c: (send(h).wait(), c)[1], 0)


def load_tiles(tiles, first, count, tbuf, tsem):
    def step(i, carry):
        pltpu.make_async_copy(tiles.at[first + i], tbuf.at[i], tsem.at[i]).start()
        return carry

    lax.fori_loop(0, count, step, 0)


def load_view(root, rows, incoming, view, vsem):
    mine = my_place()
    copies = [pltpu.make_async_copy(rows, view.at[pl.ds(0, ROOTED)], vsem.at[0])]
    for h in range(HOST):
        copies.append(
            pltpu.make_async_copy(
                incoming.at[root[mine * HOST + h]], view.at[ROOTED + h], vsem.at[1 + h]
            )
        )
    for c in copies:
        c.start()
    return copies


def replica_kernel(root, cols, present, rows, incoming, tiles, out, view, tbuf, obuf, vsem, tsem, osem):
    copies = load_view(root, rows, incoming, view, vsem)
    load_tiles(tiles, ROOTED, HOST, tbuf, tsem)
    view[SLOTS] = jnp.zeros((TILE, F), bf16)
    for c in copies:
        c.wait()
    replica_rows(root, cols, present, tiles, out, view, tbuf, obuf, tsem, osem)


def own_kernel(
    root, cols, present, rows, incoming, tiles, w_self, w_neigh,
    first_own, self_split, part_split, sums, view, tbuf, vsem, tsem,
):
    copies = load_view(root, rows, incoming, view, vsem)
    load_tiles(tiles, 0, ROOTED, tbuf, tsem)
    view[SLOTS] = jnp.zeros((TILE, F), bf16)
    sums[...] = jnp.zeros((2, F), f32)
    for c in copies:
        c.wait()

    def partial(b):
        pltpu.make_async_copy(tiles.at[b], tbuf.at[b], tsem.at[b]).wait()
        return tile_row(cols, present, b, tbuf.at[b], view)

    def own(b, carry):
        neighbours = partial(b).astype(bf16)
        first = dot(view[b], w_self[...]) + dot(neighbours, w_neigh[...])
        first_own[b] = first
        sums[0:1] += jnp.sum(first, axis=0, keepdims=True)
        sums[1:2] += jnp.sum(first * first, axis=0, keepdims=True)
        return carry

    def split(s, carry):
        part_split[s] = partial(OWN + s)
        self_split[s] = dot(view[OWN + s], w_self[...])
        return carry

    lax.fori_loop(0, OWN, own, 0)
    lax.fori_loop(0, SPLIT, split, 0)


def add_replicas(sel, incoming, total):
    for q in range(GROUP):
        s = sel[q]

        @pl.when(s > 0)
        def _(q=q, s=s):
            total[s - 1] += incoming[q].astype(f32)


def split_kernel(sel, incoming, part_split, self_split, own_sums, w_neigh, first_split, out, sums, total, pay, sems):
    total[...] = part_split[...]
    add_replicas(sel, incoming, total)
    all_sums = own_sums[...]
    firsts = []
    for s in range(SPLIT):
        first = self_split[s] + dot(total[s].astype(bf16), w_neigh[...])
        first_split[s] = first
        firsts.append(first)
    s1, s2 = all_sums[0:1], all_sums[1:2]
    for first in firsts:
        s1 += jnp.sum(first, axis=0, keepdims=True)
        s2 += jnp.sum(first * first, axis=0, keepdims=True)
    sums[0:1] = s1
    sums[1:2] = s2
    center = (s1 * (1.0 / (ROOTED * TILE))).astype(bf16)
    shift = center.astype(f32)
    for s in range(SPLIT):
        pay[s, pl.ds(0, TILE)] = (firsts[s] - shift).astype(bf16)
        pay[s, pl.ds(TILE, CENTER_ROWS)] = jnp.broadcast_to(center, (CENTER_ROWS, F))
    send_selected(lambda q: sel[q], pay, out, sems)


def hidden_kernel(
    count, root, cols, present, sums, scale, shift, first_own, first_split, incoming, tiles,
    out, hidden, view, tbuf, obuf, tsem, osem, hsem,
):
    load_tiles(tiles, ROOTED, HOST, tbuf, tsem)
    mine = my_place()
    mean = sums[0:1] * (1.0 / count)
    var = sums[1:2] * (1.0 / count) - mean * mean
    inv = lax.rsqrt(var + 1e-5)

    def norm(first, less):
        return jax.nn.relu((first - less) * inv * scale[...] + shift[...]).astype(bf16)

    def own(b, carry):
        view[b] = norm(first_own[b], mean)
        return carry

    def split(s, carry):
        view[OWN + s] = norm(first_split[s], mean)
        return carry

    def hosted(h, carry):
        q = root[mine * HOST + h]
        centered = incoming[q, pl.ds(0, TILE)].astype(f32)
        center = incoming[q, pl.ds(TILE, CENTER_ROWS)].astype(f32)[0:1]
        view[ROOTED + h] = norm(centered, mean - center)
        return carry

    lax.fori_loop(0, OWN, own, 0)
    lax.fori_loop(0, SPLIT, split, 0)
    lax.fori_loop(0, HOST, hosted, 0)
    view[SLOTS] = jnp.zeros((TILE, F), bf16)
    replica_rows(root, cols, present, tiles, out, view, tbuf, obuf, tsem, osem)
    keep = pltpu.make_async_copy(view, hidden, hsem)
    keep.start()
    keep.wait()


def own_two_kernel(cols, present, hidden, tiles, w_self, w_neigh, out, self_split, part_split, view, tbuf, vsem, tsem):
    load = pltpu.make_async_copy(hidden, view, vsem)
    load.start()
    load_tiles(tiles, 0, ROOTED, tbuf, tsem)
    load.wait()

    def partial(b):
        pltpu.make_async_copy(tiles.at[b], tbuf.at[b], tsem.at[b]).wait()
        return tile_row(cols, present, b, tbuf.at[b], view)

    def own(b, carry):
        neighbours = partial(b).astype(bf16)
        second = dot(view[b], w_self[...]) + dot(neighbours, w_neigh[...])
        out[b] = second.astype(bf16)
        return carry

    def split(s, carry):
        part_split[s] = partial(OWN + s)
        self_split[s] = dot(view[OWN + s], w_self[...])
        return carry

    lax.fori_loop(0, OWN, own, 0)
    lax.fori_loop(0, SPLIT, split, 0)


def last_kernel(sel, incoming, part_split, self_split, w_neigh, begun, out, total, done, sem):
    total[...] = part_split[...]
    add_replicas(sel, incoming, total)
    for s in range(SPLIT):
        done[s] = (self_split[s] + dot(total[s].astype(bf16), w_neigh[...])).astype(bf16)
    put = pltpu.make_async_copy(done, out.at[pl.ds(OWN, SPLIT)], sem)
    put.start()
    put.wait()


MAC = 2 * TILE * TILE * F


def per_device(
    features, tile_values, tile_columns, tile_present, host_root, host_block,
    self_one, neigh_one, scale_one, shift_one, self_two, neigh_two,
):
    rows = features.reshape(ROOTED, TILE, F)
    scale, shift = scale_one.reshape(1, F), shift_one.reshape(1, F)
    count = features.shape[0] * lax.axis_size(GX_GY_GZ)
    wire = shape((GROUP, TILE, F), bf16)
    split_f32 = shape((SPLIT, TILE, F), f32)

    def exchange(blocks):
        return lax.all_to_all(blocks, GZ, split_axis=0, concat_axis=0, tiled=True)

    view_scratch = pltpu.VMEM((SLOTS + 1, TILE, F), bf16)

    def tile_scratch(n):
        return pltpu.VMEM((n, K, TILE, TILE), bf16)

    outgoing, sel = call(
        outgoing_kernel, "outgoing", 0, 2 << 20,
        out_shape=(wire, shape((GROUP,), jnp.int32)),
        in_specs=[SMEM, SMEM, ANY],
        out_specs=(ANY, SMEM),
        scratch_shapes=[pltpu.VMEM((SPLIT, TILE, F), bf16), DMA, DMA((GROUP,))],
    )(host_root, host_block, rows)
    incoming = exchange(outgoing)

    outgoing = call(
        replica_kernel, "replicas", 64 * MAC, 4 << 20,
        out_shape=wire,
        in_specs=[SMEM] * 3 + [ANY] * 3,
        out_specs=ANY,
        scratch_shapes=[
            view_scratch, tile_scratch(HOST), pltpu.VMEM((HOST, TILE, F), bf16),
            DMA((1 + HOST,)), DMA((HOST,)), DMA((HOST,)),
        ],
    )(host_root, tile_columns, tile_present, rows, incoming, tile_values)
    returned = exchange(outgoing)

    first_own, self_split, part_split, own_sums = call(
        own_kernel, "own_rows", 60 * MAC, 5 << 20,
        out_shape=(shape((OWN, TILE, F), f32), split_f32, split_f32, shape((2, F), f32)),
        in_specs=[SMEM] * 3 + [ANY] * 3 + [VMEM] * 2,
        out_specs=(VMEM,) * 4,
        scratch_shapes=[view_scratch, tile_scratch(ROOTED), DMA((1 + HOST,)), DMA((ROOTED,))],
    )(host_root, tile_columns, tile_present, rows, incoming, tile_values, self_one, neigh_one)

    first_split, outgoing, sums = call(
        split_kernel, "split_rows", 4 * MAC, 3 << 20,
        out_shape=(split_f32, shape((GROUP, TILE + CENTER_ROWS, F), bf16), shape((2, F), f32)),
        in_specs=[SMEM] + [VMEM] * 5,
        out_specs=(VMEM, ANY, VMEM),
        scratch_shapes=[
            pltpu.VMEM((SPLIT, TILE, F), f32),
            pltpu.VMEM((SPLIT, TILE + CENTER_ROWS, F), bf16),
            DMA((GROUP,)),
        ],
    )(sel, returned, part_split, self_split, own_sums, neigh_one)
    incoming = exchange(outgoing)
    for axes in (("gy_0", "gy_1"), "gz_0", "gz_1", "gx"):
        sums = lax.psum(sums, axes)

    outgoing, hidden = call(
        functools.partial(hidden_kernel, count), "hidden_replicas", 64 * MAC, 5 << 20,
        out_shape=(wire, shape((SLOTS + 1, TILE, F), bf16)),
        in_specs=[SMEM] * 3 + [VMEM] * 6 + [ANY],
        out_specs=(ANY, ANY),
        scratch_shapes=[
            view_scratch, tile_scratch(HOST), pltpu.VMEM((HOST, TILE, F), bf16),
            DMA((HOST,)), DMA((HOST,)), DMA,
        ],
    )(
        host_root, tile_columns, tile_present, sums, scale, shift,
        first_own, first_split, incoming, tile_values,
    )
    returned = exchange(outgoing)

    begun, self_split, part_split = call(
        own_two_kernel, "own_rows_two", 60 * MAC, 5 << 20,
        out_shape=(shape((ROOTED, TILE, F), bf16), split_f32, split_f32),
        in_specs=[SMEM] * 2 + [ANY] * 2 + [VMEM] * 2,
        out_specs=(VMEM,) * 3,
        scratch_shapes=[view_scratch, tile_scratch(ROOTED), DMA, DMA((ROOTED,))],
    )(tile_columns, tile_present, hidden, tile_values, self_two, neigh_two)

    embedding = call(
        last_kernel, "split_rows_two", 4 * MAC, 3 << 20,
        out_shape=shape((ROOTED, TILE, F), bf16),
        in_specs=[SMEM] + [VMEM] * 4 + [ANY],
        out_specs=ANY,
        input_output_aliases={5: 0},
        scratch_shapes=[pltpu.VMEM((SPLIT, TILE, F), f32), pltpu.VMEM((SPLIT, TILE, F), bf16), DMA],
    )(sel, returned, part_split, self_split, neigh_two, begun)
    return embedding.reshape(ROOTED * TILE, F)


def solution(mesh):
    finer = Mesh(
        mesh.devices.reshape(mesh.shape["gx"], 2, 2, 4, 4), ("gx", "gy_0", "gy_1", "gz_0", "gz_1")
    )
    return jax.shard_map(
        per_device,
        mesh=finer,
        in_specs=(
            P(GX_GY_GZ, None),
            P(GX_GY_GZ, None, None, None),
            P(GX_GY_GZ, None),
            P(GX_GY_GZ, None),
            P(GX_GY),
            P(GX_GY),
            P(),
            P(),
            P(),
            P(),
            P(),
            P(),
        ),
        out_specs=P(GX_GY_GZ, None),
        check_vma=False,
    )
```

time: 217 us -> 195 us (0.90)
  Pallas kernels: 0 us -> 25.5 us
  waiting for transfers between devices: 80 us -> 61.6 us
  matrix products: 16.7 us -> 0 us
  local copies, waits for them, and re-layouts: 24.7 us -> 15.3 us
  blocking collectives: 73.2 us -> 64.9 us
  starting transfers between devices: 19.6 us -> 26.5 us
  other arithmetic: 2.34 us -> 0 us
    all_to_all x1 -> x0, blocking collectives: 29.4 us -> none  [spread(): lax.all_to_all(outgoing, GZ, split_axis=0, concat_axis=0, tiled=True)]
    pallas_call x0 -> x7, Pallas kernels: none -> 25.5 us  [the longest x1 5.1 us: per_device(): call(replica_kernel, 'replicas', 64 * MAC, 4 << 20, out_shape=wire, in_sp...]
    psum x5 -> x4, blocking collectives: 43.7 us -> 64.9 us  [per_device(): sums = lax.psum(sums, axes)]
    all_to_all x3 -> x4, waiting for transfers between devices: 80 us -> 61.6 us  [exchange(): return lax.all_to_all(blocks, GZ, split_axis=0, concat_axis=0, tiled=True)]
    dot_general x12 -> x0, matrix products: 16.7 us -> none  [the longest x2 11.3 us: aggregate(): jnp.einsum('bkij,bkjf->bif', tile_values, picked, preferred_element_type=...]
    unnamed x22 -> x54, local copies, waits for them, and re-layouts: 1.26 us -> 15.3 us
    gather x4 -> x0, local copies, waits for them, and re-layouts: 13.8 us -> none  [the longest x2 12.6 us: aggregate(): picked = view[tile_columns]]
    all_to_all x3 -> x4, starting transfers between devices: 19.6 us -> 26.5 us  [exchange(): return lax.all_to_all(blocks, GZ, split_axis=0, concat_axis=0, tiled=True)]
  transfers between devices with their start and end apart: 3 -> 4, of which waited for: 3 -> 3; matrix products, arithmetic and copies ran while one was open for 1% -> 0% of each run, Pallas kernels for 0% -> 5%
where the time goes in v1:
time: 195 us; the launch traced here: 194 us
  blocking collectives  64.9 us (33%)
  waiting for transfers between devices  61.6 us (32%)
  starting transfers between devices  26.5 us (14%)
  Pallas kernels  25.5 us (13%)
  local copies, waits for them, and re-layouts  15.3 us (8%)
    psum x4, blocking collectives, per_device(): sums = lax.psum(sums, axes)  64.9 us
    all_to_all x4, waiting for transfers between devices, exchange(): return lax.all_to_all(blocks, GZ, split_axis=0, concat_axis=0, tiled=True)  61.6 us
    all_to_all x4, starting transfers between devices, exchange(): return lax.all_to_all(blocks, GZ, split_axis=0, concat_axis=0, tiled=True)  26.5 us
    unnamed x54, local copies, waits for them, and re-layouts  15.3 us
    pallas_call x1, Pallas kernels, per_device(): call(replica_kernel, 'replicas', 64 * MAC, 4 << 20, out_shape=wire, in_sp...  5.1 us
    pallas_call x1, Pallas kernels, per_device(): call(functools.partial(hidden_kernel, count), 'hidden_replicas', 64 * MAC...  4.96 us
    pallas_call x1, Pallas kernels, per_device(): call(own_kernel, 'own_rows', 60 * MAC, 5 << 20, out_shape=(shape((OWN, TI...  4.59 us
    pallas_call x1, Pallas kernels, per_device(): call(own_two_kernel, 'own_rows_two', 60 * MAC, 5 << 20, out_shape=(shape(...  4.44 us
  transfers between devices with their start and end apart: 4, of which 3 were waited for; matrix products, arithmetic and copies ran while one was open for 0% of the time, Pallas kernels for 5%

profile of v1, /device:TPU:64, one launch (start us, length us, event | category | flops | bytes accessed | tf_op | source)
XLA Modules:
  0.0 194.0 jit_solution(2148763775263289271)
XLA Ops:
  0.0 1.0 copy-done.4
  1.0 0.7 copy-done.12
  1.7 0.7 copy-done.23
  2.3 2.7 %outgoing.1 = (bf16[16,128,256]{2,1,0:T(8,128)(2,1)}, s32[16]{0:T(128)S(1)}) custom-call(s32[128]{0:T(128)S(1)} %copy-done.12, s32[128]{0:T(128)S(1)} %copy-done.23, bf16[6,128,256]{2,1,0:T(8,128)(2,1)S(1)} %bitcast.4), custom_call_target="tpu_custom_call" | custom-call | bytes 2097152 | tf_op jit(solution)/shard_map/outgoing/pallas_call | solution.py:300
  5.0 0.5 copy-done.18
  5.5 12.0 %all-to-all-start = ((bf16[16,128,256]{2,1,0:T(8,128)(2,1)}), bf16[16,128,256]{2,1,0:T(8,128)(2,1)S(1)}, u32[]{:S(2)}, u32[]{:S(2)}) async-start(bf16[16,128,256]{2,1,0:T(8,128)(2,1)} %get-tuple-element.20), calls=%async_computation | async-start | bytes 2097152 | tf_op jit(solution)/shard_map/all_to_all | solution.py:293
  17.6 29.7 %all-to-all-done.incoming = bf16[16,128,256]{2,1,0:T(8,128)(2,1)S(1)} async-done(((bf16[16,128,256]{2,1,0:T(8,128)(2,1)}), bf16[16,128,256]{2,1,0:T(8,128)(2,1)S(1)}, u32[]{:S(2)}, u32[]{:S(2)}) %all-to-all-start) | async-done | bytes 1048608 | tf_op jit(solution)/shard_map/all_to_all | solution.py:293
  47.3 2.0 %copy-done = bf16[14,8,128,128]{3,2,1,0:T(8,128)(2,1)S(1)} copy-done((bf16[14,8,128,128]{3,2,1,0:T(8,128)(2,1)S(1)}, bf16[14,8,128,128]{3,2,1,0:T(8,128)(2,1)}, u32[]{:S(2)}) %copy-start) | copy-done | bytes 3670040
  49.3 5.1 %replicas.1 = bf16[16,128,256]{2,1,0:T(8,128)(2,1)} custom-call(s32[128]{0:T(128)S(1)} %copy-done.13, s32[14,8]{1,0:T(8,128)S(1)} %copy.18.cols, s32[14,8]{1,0:T(8,128)S(1)} %copy.19.present, bf16[6,128,256]{2,1,0:T(8,128)(2,1)S(1)} %bitcast.5, bf16[16,128,256]{2,1,0:T(8,128)(2,1)S(1)} %all-to-all-done.incoming, bf16[14,8,128,128]{3,2,1,0:T(8,128)(2,1)S(1)} %copy-done), custom_call_target="tpu_custom_call" | custom-call | flops 536870912 | bytes 4194304 | tf_op jit(solution)/shard_map/replicas/pallas_call | solution.py:309
  54.5 3.9 %all-to-all-start.1 = ((bf16[16,128,256]{2,1,0:T(8,128)(2,1)}), bf16[16,128,256]{2,1,0:T(8,128)(2,1)S(1)}, u32[]{:S(2)}, u32[]{:S(2)}) async-start(bf16[16,128,256]{2,1,0:T(8,128)(2,1)} %replicas.1), calls=%async_computation.1 | async-start | bytes 2097152 | tf_op jit(solution)/shard_map/all_to_all | solution.py:293
  58.4 2.0 %copy-done.1 = bf16[14,8,128,128]{3,2,1,0:T(8,128)(2,1)S(1)} copy-done((bf16[14,8,128,128]{3,2,1,0:T(8,128)(2,1)S(1)}, bf16[14,8,128,128]{3,2,1,0:T(8,128)(2,1)}, u32[]{:S(2)}) %copy-start.1) | copy-done | bytes 3670040
  60.4 0.7 copy-done.14
  61.1 4.6 %own_rows.1 = (f32[4,128,256]{2,1,0:T(8,128)S(1)}, f32[2,128,256]{2,1,0:T(8,128)S(1)}, f32[2,128,256]{2,1,0:T(8,128)S(1)}, f32[2,256]{1,0:T(2,128)S(1)}) custom-call(s32[128]{0:T(128)S(1)} %copy-done.14, s32[14,8]{1,0:T(8,128)S(1)} %copy.18.cols, s32[14,8]{1,0:T(8,128)S(1)} %copy.19.present, bf16[6,128,256]{2,1,0:T(8,128)(2,1)S(1)} %bitcast.6, ...), custom_call_target="tpu_custom_call" | custom-call | flops 503316480 | bytes 5242880 | tf_op jit(solution)/shard_map/own_rows/pallas_call | solution.py:321
  65.7 0.7 copy-done.8
  66.4 0.6 copy-done.16
  67.0 18.6 %all-to-all-done.1.incoming = bf16[16,128,256]{2,1,0:T(8,128)(2,1)S(1)} async-done(((bf16[16,128,256]{2,1,0:T(8,128)(2,1)}), bf16[16,128,256]{2,1,0:T(8,128)(2,1)S(1)}, u32[]{:S(2)}, u32[]{:S(2)}) %all-to-all-start.1) | async-done | bytes 1048608 | tf_op jit(solution)/shard_map/all_to_all | solution.py:293
  85.6 0.9 copy-done.9
  86.5 0.7 copy-done.17
  87.2 0.6 copy-done.19
  87.8 2.2 %split_rows.1 = (f32[2,128,256]{2,1,0:T(8,128)S(1)}, bf16[16,144,256]{2,1,0:T(8,128)(2,1)}, f32[2,256]{1,0:T(2,128)S(1)}) custom-call(s32[16]{0:T(128)S(1)} %copy-done.19, bf16[16,128,256]{2,1,0:T(8,128)(2,1)S(1)} %all-to-all-done.1.incoming, f32[2,128,256]{2,1,0:T(8,128)S(1)} %copy-done.9, f32[2,128,256]{2,1,0:T(8,128)S(1)} %get-tuple-element.22.self_split, ...), custom_call_target="tpu_custom_call" | custom-call | flops 33554432 | bytes 3145728 | tf_op jit(solution)/shard_map/split_rows/pallas_call | solution.py:329
  90.0 4.1 %all-to-all-start.2 = ((bf16[16,144,256]{2,1,0:T(8,128)(2,1)}), bf16[16,144,256]{2,1,0:T(8,128)(2,1)S(1)}, u32[]{:S(2)}, u32[]{:S(2)}) async-start(bf16[16,144,256]{2,1,0:T(8,128)(2,1)} %get-tuple-element.27), calls=%async_computation.2 | async-start | bytes 2359296 | tf_op jit(solution)/shard_map/all_to_all | solution.py:293
  94.1 24.9 %psum.28 = f32[2,256]{1,0:T(2,128)S(1)} all-reduce(f32[2,256]{1,0:T(2,128)S(1)} %get-tuple-element.24), channel_id=1, replica_groups=mesh['gx'=8,'gy_0'=2,'gy_1'=2,'gz_0'=4,'gz_1'=4] {'gy_0','gy_1'}, use_global_device_ids=true, to_apply=%region_0.0 | all-reduce | flops 512 | bytes 4096 | tf_op jit(solution)/shard_map/psum | solution.py:342
  119.0 10.8 %psum.29 = f32[2,256]{1,0:T(2,128)S(1)} all-reduce(f32[2,256]{1,0:T(2,128)S(1)} %psum.28), channel_id=1, replica_groups=mesh['gx'=8,'gy_0'=2,'gy_1'=2,'gz_0'=4,'gz_1'=4] {'gz_0'}, use_global_device_ids=true, to_apply=%region_1.0 | all-reduce | flops 512 | bytes 4096 | tf_op jit(solution)/shard_map/psum | solution.py:342
  129.8 11.6 %psum.30 = f32[2,256]{1,0:T(2,128)S(1)} all-reduce(f32[2,256]{1,0:T(2,128)S(1)} %psum.29), channel_id=1, replica_groups=mesh['gx'=8,'gy_0'=2,'gy_1'=2,'gz_0'=4,'gz_1'=4] {'gz_1'}, use_global_device_ids=true, to_apply=%region_2.0 | all-reduce | flops 512 | bytes 4096 | tf_op jit(solution)/shard_map/psum | solution.py:342
  141.4 17.6 %psum.31.sums = f32[2,256]{1,0:T(2,128)S(1)} all-reduce(f32[2,256]{1,0:T(2,128)S(1)} %psum.30), channel_id=1, replica_groups=mesh['gx'=8,'gy_0'=2,'gy_1'=2,'gz_0'=4,'gz_1'=4] {'gx'}, use_global_device_ids=true, to_apply=%region_3.0 | all-reduce | flops 512 | bytes 4096 | tf_op jit(solution)/shard_map/psum | solution.py:342
  159.0 2.0 %copy-done.2 = bf16[14,8,128,128]{3,2,1,0:T(8,128)(2,1)S(1)} copy-done((bf16[14,8,128,128]{3,2,1,0:T(8,128)(2,1)S(1)}, bf16[14,8,128,128]{3,2,1,0:T(8,128)(2,1)}, u32[]{:S(2)}) %copy-start.2) | copy-done | bytes 3670040
  161.1 5.0 %hidden_replicas.1 = (bf16[16,128,256]{2,1,0:T(8,128)(2,1)}, bf16[15,128,256]{2,1,0:T(8,128)(2,1)S(1)}) custom-call(s32[128]{0:T(128)S(1)} %copy-done.15, s32[14,8]{1,0:T(8,128)S(1)} %copy.18.cols, s32[14,8]{1,0:T(8,128)S(1)} %copy.19.present, f32[2,256]{1,0:T(2,128)S(1)} %psum.31.sums, f32[1,256]{1,0:T(1,128)S(1)} %bitcast.7, f32[1,256]{1,0:T(1,128)S(1)} %bitcast.8, ...), custom_call_target="tpu_custom_call" | custom-call | flops 536870912 | bytes 5242880 | tf_op jit(solution)/shard_map/hidden_replicas/pallas_call | solution.py:344
  166.1 6.5 %all-to-all-start.3 = ((bf16[16,128,256]{2,1,0:T(8,128)(2,1)}), bf16[16,128,256]{2,1,0:T(8,128)(2,1)S(1)}, u32[]{:S(2)}, u32[]{:S(2)}) async-start(bf16[16,128,256]{2,1,0:T(8,128)(2,1)} %get-tuple-element.28), calls=%async_computation.3 | async-start | bytes 2097152 | tf_op jit(solution)/shard_map/all_to_all | solution.py:293
  172.6 2.0 %copy-done.3 = bf16[14,8,128,128]{3,2,1,0:T(8,128)(2,1)S(1)} copy-done((bf16[14,8,128,128]{3,2,1,0:T(8,128)(2,1)S(1)}, bf16[14,8,128,128]{3,2,1,0:T(8,128)(2,1)}, u32[]{:S(2)}) %copy-start.3) | copy-done | bytes 3670040
  174.7 4.4 %own_rows_two.1 = (bf16[6,128,256]{2,1,0:T(8,128)(2,1)}, f32[2,128,256]{2,1,0:T(8,128)S(1)}, f32[2,128,256]{2,1,0:T(8,128)S(1)}) custom-call(s32[14,8]{1,0:T(8,128)S(1)} %copy.18.cols, s32[14,8]{1,0:T(8,128)S(1)} %copy.19.present, bf16[15,128,256]{2,1,0:T(8,128)(2,1)S(1)} %get-tuple-element.29.hidden, bf16[14,8,128,128]{3,2,1,0:T(8,128)(2,1)S(1)} %copy-done.3, ...), custom_call_target="tpu_custom_call" | custom-call | flops 503316480 | bytes 5242880 | tf_op jit(solution)/shard_map/own_rows_two/pallas_call | solution.py:359
  179.1 13.3 %all-to-all-done.3.incoming = bf16[16,128,256]{2,1,0:T(8,128)(2,1)S(1)} async-done(((bf16[16,128,256]{2,1,0:T(8,128)(2,1)}), bf16[16,128,256]{2,1,0:T(8,128)(2,1)S(1)}, u32[]{:S(2)}, u32[]{:S(2)}) %all-to-all-start.3) | async-done | bytes 1048608 | tf_op jit(solution)/shard_map/all_to_all | solution.py:293
  192.4 1.6 split_rows_two.1
  (41 shorter events, 0.3 us)
Async XLA Ops:
  0.0 1.0 copy-start.4
  1.0 0.7 copy-start.12
  1.7 0.7 copy-start.23
  2.3 15.1 %copy-start.24 = (s32[14,8]{0,1:T(8,128)S(1)}, s32[14,8]{0,1:T(8,128)}, u32[]{:S(2)}) copy-start(s32[14,8]{0,1:T(8,128)} %param.14) | copy-start | bytes 1348
  2.3 15.2 %copy-start.25 = (s32[14,8]{0,1:T(8,128)S(1)}, s32[14,8]{0,1:T(8,128)}, u32[]{:S(2)}) copy-start(s32[14,8]{0,1:T(8,128)} %param.15) | copy-start | bytes 1348
  2.3 45.0 %copy-start.5 = (bf16[768,256]{1,0:T(8,128)(2,1)S(1)}, bf16[768,256]{1,0:T(8,128)(2,1)}, u32[]{:S(2)}) copy-start(bf16[768,256]{1,0:T(8,128)(2,1)} %param.12) | copy-start | bytes 1179652
  2.3 45.0 %copy-start.13 = (s32[128]{0:T(128)S(1)}, s32[128]{0:T(128)}, u32[]{:S(2)}) copy-start(s32[128]{0:T(128)} %root.7) | copy-start | bytes 1540
  5.0 0.5 copy-start.18
  5.5 41.8 %all-to-all-start = ((bf16[16,128,256]{2,1,0:T(8,128)(2,1)}), bf16[16,128,256]{2,1,0:T(8,128)(2,1)S(1)}, u32[]{:S(2)}, u32[]{:S(2)}) async-start(bf16[16,128,256]{2,1,0:T(8,128)(2,1)} %get-tuple-element.20), calls=%async_computation | async-start | bytes 2097152 | tf_op jit(solution)/shard_map/all_to_all | solution.py:293
  47.3 2.0 %copy-start = (bf16[14,8,128,128]{3,2,1,0:T(8,128)(2,1)S(1)}, bf16[14,8,128,128]{3,2,1,0:T(8,128)(2,1)}, u32[]{:S(2)}) copy-start(bf16[14,8,128,128]{3,2,1,0:T(8,128)(2,1)} %tiles.7) | copy-start | bytes 11010052
  54.4 3.9 %copy-start.6 = (bf16[256,256]{1,0:T(8,128)(2,1)S(1)}, bf16[256,256]{1,0:T(8,128)(2,1)}, u32[]{:S(2)}) copy-start(bf16[256,256]{1,0:T(8,128)(2,1)} %w_neigh.5) | copy-start | bytes 393220
  54.5 3.9 %copy-start.10 = (bf16[256,256]{1,0:T(8,128)(2,1)S(1)}, bf16[256,256]{1,0:T(8,128)(2,1)}, u32[]{:S(2)}) copy-start(bf16[256,256]{1,0:T(8,128)(2,1)} %w_self.2) | copy-start | bytes 393220
  54.5 31.1 %all-to-all-start.1 = ((bf16[16,128,256]{2,1,0:T(8,128)(2,1)}), bf16[16,128,256]{2,1,0:T(8,128)(2,1)S(1)}, u32[]{:S(2)}, u32[]{:S(2)}) async-start(bf16[16,128,256]{2,1,0:T(8,128)(2,1)} %replicas.1), calls=%async_computation.1 | async-start | bytes 2097152 | tf_op jit(solution)/shard_map/all_to_all | solution.py:293
  58.4 2.0 %copy-start.1 = (bf16[14,8,128,128]{3,2,1,0:T(8,128)(2,1)S(1)}, bf16[14,8,128,128]{3,2,1,0:T(8,128)(2,1)}, u32[]{:S(2)}) copy-start(bf16[14,8,128,128]{3,2,1,0:T(8,128)(2,1)} %tiles.7) | copy-start | bytes 11010052
  60.4 0.7 copy-start.14
  65.7 0.7 copy-start.8
  66.4 0.6 copy-start.16
  85.6 1.0 copy-start.9
  86.5 0.7 copy-start.17
  87.2 0.6 copy-start.19
  89.9 69.1 %copy-start.15 = (s32[128]{0:T(128)S(1)}, s32[128]{0:T(128)}, u32[]{:S(2)}) copy-start(s32[128]{0:T(128)} %root.7) | copy-start | bytes 1540
  90.0 69.1 %copy-start.21 = (f32[256]{0:T(256)S(1)}, f32[256]{0:T(256)}, u32[]{:S(2)}) copy-start(f32[256]{0:T(256)} %param.20) | copy-start | bytes 3076
  90.0 69.0 %copy-start.22 = (f32[256]{0:T(256)S(1)}, f32[256]{0:T(256)}, u32[]{:S(2)}) copy-start(f32[256]{0:T(256)} %param.21) | copy-start | bytes 3076
  90.0 69.0 %all-to-all-start.2 = ((bf16[16,144,256]{2,1,0:T(8,128)(2,1)}), bf16[16,144,256]{2,1,0:T(8,128)(2,1)S(1)}, u32[]{:S(2)}, u32[]{:S(2)}) async-start(bf16[16,144,256]{2,1,0:T(8,128)(2,1)} %get-tuple-element.27), calls=%async_computation.2 | async-start | bytes 2359296 | tf_op jit(solution)/shard_map/all_to_all | solution.py:293
  159.0 2.0 %copy-start.2 = (bf16[14,8,128,128]{3,2,1,0:T(8,128)(2,1)S(1)}, bf16[14,8,128,128]{3,2,1,0:T(8,128)(2,1)}, u32[]{:S(2)}) copy-start(bf16[14,8,128,128]{3,2,1,0:T(8,128)(2,1)} %tiles.7) | copy-start | bytes 11010052
  166.0 6.6 %copy-start.7 = (bf16[256,256]{1,0:T(8,128)(2,1)S(1)}, bf16[256,256]{1,0:T(8,128)(2,1)}, u32[]{:S(2)}) copy-start(bf16[256,256]{1,0:T(8,128)(2,1)} %w_neigh.7) | copy-start | bytes 393220
  166.0 6.6 %copy-start.11 = (bf16[256,256]{1,0:T(8,128)(2,1)S(1)}, bf16[256,256]{1,0:T(8,128)(2,1)}, u32[]{:S(2)}) copy-start(bf16[256,256]{1,0:T(8,128)(2,1)} %w_self.3) | copy-start | bytes 393220
  166.1 26.3 %all-to-all-start.3 = ((bf16[16,128,256]{2,1,0:T(8,128)(2,1)}), bf16[16,128,256]{2,1,0:T(8,128)(2,1)S(1)}, u32[]{:S(2)}, u32[]{:S(2)}) async-start(bf16[16,128,256]{2,1,0:T(8,128)(2,1)} %get-tuple-element.28), calls=%async_computation.3 | async-start | bytes 2097152 | tf_op jit(solution)/shard_map/all_to_all | solution.py:293
  172.6 2.0 %copy-start.3 = (bf16[14,8,128,128]{3,2,1,0:T(8,128)(2,1)S(1)}, bf16[14,8,128,128]{3,2,1,0:T(8,128)(2,1)}, u32[]{:S(2)}) copy-start(bf16[14,8,128,128]{3,2,1,0:T(8,128)(2,1)} %tiles.7) | copy-start | bytes 11010052
  174.7 17.7 %copy-start.20 = (s32[16]{0:T(128)S(1)}, s32[16]{0:T(128)}, u32[]{:S(2)}) copy-start(s32[16]{0:T(128)} %copy-done.18) | copy-start | bytes 196

commit v2 on v1

v2 whole, which is shorter than its diff:
```python
import functools

import jax
import jax.numpy as jnp
from jax import lax
from jax.experimental import pallas as pl
from jax.experimental.pallas import tpu as pltpu
from jax.sharding import Mesh
from jax.sharding import PartitionSpec as P

OWN = 4
SPLIT = 2
ROOTED = 6
HOST = 8
SLOTS = 14
K = 8
TILE = 128
F = 256
GROUP = 16
CENTER_ROWS = 16
VMEM_BYTES = 50 << 20
GZ = ("gz_0", "gz_1")
GX_GY_GZ = ("gx", "gy_0", "gy_1", "gz_0", "gz_1")
GX_GY = ("gx", "gy_0", "gy_1")
REST = ("gy_0", "gz_0", "gz_1")
ROOTS_AT = 112
SEL_AT = 120

f32 = jnp.float32
bf16 = jnp.bfloat16

HBM = pl.BlockSpec(memory_space=pltpu.HBM)
ANY = pl.BlockSpec(memory_space=pl.ANY)
VMEM = pl.BlockSpec(memory_space=pltpu.VMEM)
SMEM = pl.BlockSpec(memory_space=pltpu.SMEM)
DMA = pltpu.SemaphoreType.DMA


def shape(dims, dtype):
    return jax.ShapeDtypeStruct(dims, dtype)


def call(body, name, flops, size, room=VMEM_BYTES, **kw):
    return pl.pallas_call(
        body,
        name=name,
        compiler_params=pltpu.CompilerParams(vmem_limit_bytes=room),
        cost_estimate=pl.CostEstimate(flops=flops, bytes_accessed=size, transcendentals=0),
        **kw,
    )


def dot(a, b):
    return jnp.dot(a, b, preferred_element_type=f32)


def my_place():
    return lax.axis_index("gz_0") * 4 + lax.axis_index("gz_1")


def send_selected(sel, blocks, out, sems):
    copies = [
        pltpu.make_async_copy(blocks.at[jnp.maximum(sel(q) - 1, 0)], out.at[q], sems.at[q])
        for q in range(GROUP)
    ]
    for c in copies:
        c.start()
    for c in copies:
        c.wait()


def outgoing_kernel(root, block, rows, out, sel, split, root_s, block_s, sem, sems):
    loads = [
        pltpu.make_async_copy(root, root_s, sem.at[0]),
        pltpu.make_async_copy(block, block_s, sem.at[1]),
        pltpu.make_async_copy(rows.at[pl.ds(OWN, SPLIT)], split, sem.at[2]),
    ]
    for c in loads:
        c.start()
    for c in loads:
        c.wait()
    mine = my_place()
    for q in range(GROUP):
        held = jnp.int32(0)
        for j in range(HOST):
            held = jnp.where(root_s[q * HOST + j] == mine, block_s[q * HOST + j] + 1, held)
        sel[q] = held
    send_selected(lambda q: sel[q], split, out, sems)


def tables_kernel(root, cols, present, sel, rows, table, rows_v, sem):
    load_rows = pltpu.make_async_copy(rows, rows_v, sem)
    load_rows.start()
    mine = my_place()

    def slots(b, carry):
        for k in range(K):
            table[b * K + k] = jnp.where(present[b, k] > 0, cols[b, k], SLOTS)
        return carry

    lax.fori_loop(0, SLOTS, slots, 0)
    for h in range(HOST):
        table[ROOTS_AT + h] = root[mine * HOST + h]
    for q in range(GROUP):
        table[SEL_AT + q] = sel[q]
    load_rows.wait()


def tile_copy(tiles, tbuf, tsem, first, i):
    return pltpu.make_async_copy(tiles.at[first + i], tbuf.at[i], tsem.at[i])


def load_tiles(tiles, tbuf, tsem, first, count):
    lax.fori_loop(0, count, lambda i, c: (tile_copy(tiles, tbuf, tsem, first, i).start(), c)[1], 0)


def tile_row(table, tiles, tbuf, tsem, first, i, view):
    tile_copy(tiles, tbuf, tsem, first, i).wait()
    b = first + i
    acc = None
    for k in range(0, K, 2):
        left = jnp.concatenate([tbuf[i, k], tbuf[i, k + 1]], axis=1)
        right = jnp.concatenate([view[table[b * K + k]], view[table[b * K + k + 1]]], axis=0)
        term = dot(left, right)
        acc = term if acc is None else acc + term
    return acc


def replica_rows(table, tiles, out, view, tbuf, obuf, tsem, osem):
    def send(h):
        return pltpu.make_async_copy(obuf.at[h], out.at[table[ROOTS_AT + h]], osem.at[h])

    def step(h, carry):
        obuf[h] = tile_row(table, tiles, tbuf, tsem, ROOTED, h, view).astype(bf16)

        @pl.when(h > 0)
        def _():
            send(h - 1).start()

        return carry

    lax.fori_loop(0, HOST, step, 0)
    send(HOST - 1).start()
    lax.fori_loop(0, HOST, lambda h, c: (send(h).wait(), c)[1], 0)


def replica_kernel(table, rows, incoming, tiles, out, view, tbuf, obuf, tsem, osem):
    load_tiles(tiles, tbuf, tsem, ROOTED, HOST)

    def own(b, carry):
        view[b] = rows[b]
        return carry

    def hosted(h, carry):
        view[ROOTED + h] = incoming[table[ROOTS_AT + h]]
        return carry

    lax.fori_loop(0, ROOTED, own, 0)
    lax.fori_loop(0, HOST, hosted, 0)
    view[SLOTS] = jnp.zeros((TILE, F), bf16)
    replica_rows(table, tiles, out, view, tbuf, obuf, tsem, osem)


def own_kernel(table, view, tiles, w_self, w_neigh, first_own, self_split, part_split, sums, tbuf, tsem):
    load_tiles(tiles, tbuf, tsem, 0, ROOTED)
    sums[...] = jnp.zeros((2, F), f32)

    def own(b, carry):
        neighbours = tile_row(table, tiles, tbuf, tsem, 0, b, view).astype(bf16)
        first = dot(view[b], w_self[...]) + dot(neighbours, w_neigh[...])
        first_own[b] = first
        sums[0:1] += jnp.sum(first, axis=0, keepdims=True)
        sums[1:2] += jnp.sum(first * first, axis=0, keepdims=True)
        return carry

    def split(s, carry):
        part_split[s] = tile_row(table, tiles, tbuf, tsem, 0, OWN + s, view)
        self_split[s] = dot(view[OWN + s], w_self[...])
        return carry

    lax.fori_loop(0, OWN, own, 0)
    lax.fori_loop(0, SPLIT, split, 0)


def add_replicas(table, incoming, total):
    for q in range(GROUP):
        s = table[SEL_AT + q]

        @pl.when(s > 0)
        def _(q=q, s=s):
            total[s - 1] += incoming[q].astype(f32)


def split_kernel(
    table, incoming, part_split, self_split, own_sums, w_neigh, first_split, out, sums, total, pay, sems
):
    total[...] = part_split[...]
    add_replicas(table, incoming, total)
    for s in range(SPLIT):
        first_split[s] = self_split[s] + dot(total[s].astype(bf16), w_neigh[...])
    s1, s2 = own_sums[0:1], own_sums[1:2]
    for s in range(SPLIT):
        first = first_split[s]
        s1 += jnp.sum(first, axis=0, keepdims=True)
        s2 += jnp.sum(first * first, axis=0, keepdims=True)
    sums[0:1] = s1
    sums[1:2] = s2
    center = (s1 * (1.0 / (ROOTED * TILE))).astype(bf16)
    shift = center.astype(f32)
    for s in range(SPLIT):
        pay[s, pl.ds(0, TILE)] = (first_split[s] - shift).astype(bf16)
        pay[s, pl.ds(TILE, CENTER_ROWS)] = jnp.broadcast_to(center, (CENTER_ROWS, F))
    send_selected(lambda q: table[SEL_AT + q], pay, out, sems)


def hidden_kernel(
    count, table, sums, scale, shift, first_own, first_split, incoming, tiles,
    out, view, tbuf, obuf, tsem, osem,
):
    load_tiles(tiles, tbuf, tsem, ROOTED, HOST)
    total = jnp.sum(sums[...], axis=0)
    mean = total[0:1] * (1.0 / count)
    var = total[1:2] * (1.0 / count) - mean * mean
    inv = lax.rsqrt(var + 1e-5)

    def norm(first, less):
        return jax.nn.relu((first - less) * inv * scale[...] + shift[...]).astype(bf16)

    def own(b, carry):
        view[b] = norm(first_own[b], mean)
        return carry

    def split(s, carry):
        view[OWN + s] = norm(first_split[s], mean)
        return carry

    def hosted(h, carry):
        q = table[ROOTS_AT + h]
        centered = incoming[q, pl.ds(0, TILE)].astype(f32)
        center = incoming[q, pl.ds(TILE, CENTER_ROWS)].astype(f32)[0:1]
        view[ROOTED + h] = norm(centered, mean - center)
        return carry

    lax.fori_loop(0, OWN, own, 0)
    lax.fori_loop(0, SPLIT, split, 0)
    lax.fori_loop(0, HOST, hosted, 0)
    view[SLOTS] = jnp.zeros((TILE, F), bf16)
    replica_rows(table, tiles, out, view, tbuf, obuf, tsem, osem)


def own_two_kernel(table, view, tiles, w_self, w_neigh, out, self_split, part_split, tbuf, tsem):
    load_tiles(tiles, tbuf, tsem, 0, ROOTED)

    def own(b, carry):
        neighbours = tile_row(table, tiles, tbuf, tsem, 0, b, view).astype(bf16)
        second = dot(view[b], w_self[...]) + dot(neighbours, w_neigh[...])
        out[b] = second.astype(bf16)
        return carry

    def split(s, carry):
        part_split[s] = tile_row(table, tiles, tbuf, tsem, 0, OWN + s, view)
        self_split[s] = dot(view[OWN + s], w_self[...])
        return carry

    lax.fori_loop(0, OWN, own, 0)
    lax.fori_loop(0, SPLIT, split, 0)


def last_kernel(table, incoming, part_split, self_split, w_neigh, begun, out, total, done, sem):
    total[...] = part_split[...]
    add_replicas(table, incoming, total)
    for s in range(SPLIT):
        done[s] = (self_split[s] + dot(total[s].astype(bf16), w_neigh[...])).astype(bf16)
    put = pltpu.make_async_copy(done, out.at[pl.ds(OWN, SPLIT)], sem)
    put.start()
    put.wait()


MAC = 2 * TILE * TILE * F


def per_device(
    features, tile_values, tile_columns, tile_present, host_root, host_block,
    self_one, neigh_one, scale_one, shift_one, self_two, neigh_two,
):
    rows = features.reshape(ROOTED, TILE, F)
    scale, shift = scale_one.reshape(1, F), shift_one.reshape(1, F)
    count = features.shape[0] * lax.axis_size(GX_GY_GZ)
    wire = pltpu.HBM((GROUP, TILE, F), bf16)
    split_f32 = pltpu.VMEM((SPLIT, TILE, F), f32)
    view_v = pltpu.VMEM((SLOTS + 1, TILE, F), bf16)
    row_buffer = pltpu.VMEM((HOST, TILE, F), bf16)

    def tile_rows(n):
        return pltpu.VMEM((n, K, TILE, TILE), bf16)

    def exchange(blocks, axes=GZ):
        return lax.all_to_all(blocks, axes, split_axis=0, concat_axis=0, tiled=True)

    outgoing, sel = call(
        outgoing_kernel, "outgoing", 0, 2 << 20, room=60 << 20,
        out_shape=(wire, shape((GROUP,), jnp.int32)),
        in_specs=[HBM] * 3,
        out_specs=(HBM, SMEM),
        scratch_shapes=[
            pltpu.VMEM((SPLIT, TILE, F), bf16),
            pltpu.SMEM((GROUP * HOST,), jnp.int32),
            pltpu.SMEM((GROUP * HOST,), jnp.int32),
            DMA((3,)), DMA((GROUP,)),
        ],
    )(host_root, host_block, rows)
    incoming = exchange(outgoing)

    table, rows_v = call(
        tables_kernel, "tables", 0, 8 << 20,
        out_shape=(
            shape((SEL_AT + GROUP,), jnp.int32),
            pltpu.VMEM((ROOTED, TILE, F), bf16),
        ),
        in_specs=[SMEM] * 4 + [HBM],
        out_specs=(SMEM, VMEM),
        scratch_shapes=[DMA],
    )(host_root, tile_columns, tile_present, sel, rows)

    outgoing, view = call(
        replica_kernel, "replicas", 64 * MAC, 4 << 20,
        out_shape=(wire, view_v),
        in_specs=[SMEM] + [VMEM] * 2 + [HBM],
        out_specs=(HBM, VMEM),
        scratch_shapes=[tile_rows(HOST), row_buffer, DMA((HOST,)), DMA((HOST,))],
    )(table, rows_v, incoming, tile_values)
    returned = exchange(outgoing)

    first_own, self_split, part_split, own_sums = call(
        own_kernel, "own_rows", 60 * MAC, 5 << 20,
        out_shape=(pltpu.VMEM((OWN, TILE, F), f32), split_f32, split_f32, pltpu.VMEM((2, F), f32)),
        in_specs=[SMEM, VMEM, HBM, VMEM, VMEM],
        out_specs=(VMEM,) * 4,
        scratch_shapes=[tile_rows(ROOTED), DMA((ROOTED,))],
    )(table, view, tile_values, self_one, neigh_one)

    first_split, outgoing, sums = call(
        split_kernel, "split_rows", 4 * MAC, 3 << 20,
        out_shape=(
            split_f32,
            pltpu.HBM((GROUP, TILE + CENTER_ROWS, F), bf16),
            pltpu.VMEM((2, F), f32),
        ),
        in_specs=[SMEM] + [VMEM] * 5,
        out_specs=(VMEM, HBM, VMEM),
        scratch_shapes=[
            pltpu.VMEM((SPLIT, TILE, F), f32),
            pltpu.VMEM((SPLIT, TILE + CENTER_ROWS, F), bf16),
            DMA((GROUP,)),
        ],
    )(table, returned, part_split, self_split, own_sums, neigh_one)
    incoming = exchange(outgoing)
    sums = lax.psum(lax.psum(sums, "gx"), "gy_1")
    incoming, sums = lax.optimization_barrier((incoming, sums))
    sums = exchange(jnp.broadcast_to(sums, (2 * GROUP, 2, F)), REST)

    outgoing, view = call(
        functools.partial(hidden_kernel, count), "hidden_replicas", 64 * MAC, 5 << 20,
        out_shape=(wire, view_v),
        in_specs=[SMEM] + [VMEM] * 6 + [HBM],
        out_specs=(HBM, VMEM),
        scratch_shapes=[tile_rows(HOST), row_buffer, DMA((HOST,)), DMA((HOST,))],
    )(table, sums, scale, shift, first_own, first_split, incoming, tile_values)
    returned = exchange(outgoing)

    begun, self_split, part_split = call(
        own_two_kernel, "own_rows_two", 60 * MAC, 5 << 20,
        out_shape=(shape((ROOTED, TILE, F), bf16), split_f32, split_f32),
        in_specs=[SMEM, VMEM, HBM, VMEM, VMEM],
        out_specs=(VMEM,) * 3,
        scratch_shapes=[tile_rows(ROOTED), DMA((ROOTED,))],
    )(table, view, tile_values, self_two, neigh_two)

    embedding = call(
        last_kernel, "split_rows_two", 4 * MAC, 3 << 20,
        out_shape=shape((ROOTED, TILE, F), bf16),
        in_specs=[SMEM] + [VMEM] * 4 + [ANY],
        out_specs=ANY,
        input_output_aliases={5: 0},
        scratch_shapes=[pltpu.VMEM((SPLIT, TILE, F), f32), pltpu.VMEM((SPLIT, TILE, F), bf16), DMA],
    )(table, returned, part_split, self_split, neigh_two, begun)
    return embedding.reshape(ROOTED * TILE, F)


def solution(mesh):
    finer = Mesh(
        mesh.devices.reshape(mesh.shape["gx"], 2, 2, 4, 4), ("gx", "gy_0", "gy_1", "gz_0", "gz_1")
    )
    return jax.shard_map(
        per_device,
        mesh=finer,
        in_specs=(
            P(GX_GY_GZ, None),
            P(GX_GY_GZ, None, None, None),
            P(GX_GY_GZ, None),
            P(GX_GY_GZ, None),
            P(GX_GY),
            P(GX_GY),
            P(),
            P(),
            P(),
            P(),
            P(),
            P(),
        ),
        out_specs=P(GX_GY_GZ, None),
        check_vma=False,
    )
```

time: 195 us -> 172 us (0.88)
  the two profiles are of different devices: /device:TPU:64 before, /device:TPU:40 now
where the time goes in v2:
time: 172 us; the launch traced here: 171 us
  waiting for transfers between devices  75.4 us (44%)
  blocking collectives  39.3 us (23%)
  starting transfers between devices  30.8 us (18%)
  Pallas kernels  25 us (15%)
    all_to_all x4, waiting for transfers between devices, exchange(): return lax.all_to_all(blocks, axes, split_axis=0, concat_axis=0, tiled=True)  75.4 us
    all_to_all x4, starting transfers between devices, exchange(): return lax.all_to_all(blocks, axes, split_axis=0, concat_axis=0, tiled=True)  30.8 us
    all_to_all x1, blocking collectives, exchange(): return lax.all_to_all(blocks, axes, split_axis=0, concat_axis=0, tiled=True)  21.3 us
    psum x2, blocking collectives, per_device(): sums = lax.psum(lax.psum(sums, 'gx'), 'gy_1')  18 us
    pallas_call x1, Pallas kernels, per_device(): call(own_two_kernel, 'own_rows_two', 60 * MAC, 5 << 20, out_shape=(shape(...  4.38 us
    pallas_call x1, Pallas kernels, per_device(): call(functools.partial(hidden_kernel, count), 'hidden_replicas', 64 * MAC...  4.31 us
    pallas_call x1, Pallas kernels, per_device(): call(replica_kernel, 'replicas', 64 * MAC, 4 << 20, out_shape=(wire, view...  4.24 us
    pallas_call x1, Pallas kernels, per_device(): call(own_kernel, 'own_rows', 60 * MAC, 5 << 20, out_shape=(pltpu.VMEM((OW...  3.84 us
  transfers between devices with their start and end apart: 4, of which 4 were waited for; matrix products, arithmetic and copies ran while one was open for 0% of the time, Pallas kernels for 6%

profile of v2, /device:TPU:40, one launch (start us, length us, event | category | flops | bytes accessed | tf_op | source)
XLA Modules:
  0.0 170.9 jit_solution(3553549234030765900)
XLA Ops:
  0.0 0.0 copy-start.5
  0.0 2.6 %outgoing.1 = (bf16[16,128,256]{2,1,0:T(8,128)(2,1)}, s32[16]{0:T(128)}) custom-call(s32[128]{0:T(128)} %root.3, s32[128]{0:T(128)} %block.1, bf16[6,128,256]{2,1,0:T(8,128)(2,1)} %bitcast.4), custom_call_target="tpu_custom_call" | custom-call | bytes 2097152 | tf_op jit(solution)/shard_map/outgoing/pallas_call | solution.py:300
  2.7 0.0 copy-start.8
  2.7 12.9 %all-to-all-start = ((bf16[16,128,256]{2,1,0:T(8,128)(2,1)}), bf16[16,128,256]{2,1,0:T(8,128)(2,1)S(1)}, u32[]{:S(2)}, u32[]{:S(2)}) async-start(bf16[16,128,256]{2,1,0:T(8,128)(2,1)} %get-tuple-element.28), calls=%async_computation | async-start | bytes 2097152 | tf_op jit(solution)/shard_map/all_to_all | solution.py:298
  15.6 0.0 copy-done.9
  15.6 0.1 copy.14.cols
  15.7 0.1 copy.15.present
  15.8 0.0 copy-done.5
  15.8 1.9 %tables.1 = (s32[136]{0:T(256)S(1)}, bf16[6,128,256]{2,1,0:T(8,128)(2,1)S(1)}) custom-call(s32[128]{0:T(128)S(1)} %copy-done.5, s32[14,8]{1,0:T(8,128)S(1)} %copy.14.cols, s32[14,8]{1,0:T(8,128)S(1)} %copy.15.present, s32[16]{0:T(128)S(1)} %copy-done.8, bf16[6,128,256]{2,1,0:T(8,128)(2,1)S(1)} %bitcast.5), custom_call_target="tpu_custom_call" | custom-call | bytes 8388608 | tf_op jit(solution)/shard_map/tables/pallas_call | solution.py:314
  17.7 22.1 %all-to-all-done.incoming = bf16[16,128,256]{2,1,0:T(8,128)(2,1)S(1)} async-done(((bf16[16,128,256]{2,1,0:T(8,128)(2,1)}), bf16[16,128,256]{2,1,0:T(8,128)(2,1)S(1)}, u32[]{:S(2)}, u32[]{:S(2)}) %all-to-all-start) | async-done | bytes 1048608 | tf_op jit(solution)/shard_map/all_to_all | solution.py:298
  39.8 4.2 %replicas.1 = (bf16[16,128,256]{2,1,0:T(8,128)(2,1)}, bf16[15,128,256]{2,1,0:T(8,128)(2,1)S(1)}) custom-call(s32[136]{0:T(256)S(1)} %get-tuple-element.26.table, bf16[6,128,256]{2,1,0:T(8,128)(2,1)S(1)} %get-tuple-element.27.rows, bf16[16,128,256]{2,1,0:T(8,128)(2,1)S(1)} %all-to-all-done.incoming, bf16[14,8,128,128]{3,2,1,0:T(8,128)(2,1)} %tiles.7), custom_call_target="tpu_custom_call" | custom-call | flops 536870912 | bytes 4194304 | tf_op jit(solution)/shard_map/replicas/pallas_call | solution.py:325
  44.0 0.0 copy-start.1
  44.1 0.0 copy-start.3
  44.1 7.3 %all-to-all-start.1 = ((bf16[16,128,256]{2,1,0:T(8,128)(2,1)}), bf16[16,128,256]{2,1,0:T(8,128)(2,1)S(1)}, u32[]{:S(2)}, u32[]{:S(2)}) async-start(bf16[16,128,256]{2,1,0:T(8,128)(2,1)} %get-tuple-element.29), calls=%async_computation.1 | async-start | bytes 2097152 | tf_op jit(solution)/shard_map/all_to_all | solution.py:298
  51.4 3.8 %own_rows.1 = (f32[4,128,256]{2,1,0:T(8,128)S(1)}, f32[2,128,256]{2,1,0:T(8,128)S(1)}, f32[2,128,256]{2,1,0:T(8,128)S(1)}, f32[2,256]{1,0:T(2,128)S(1)}) custom-call(s32[136]{0:T(256)S(1)} %get-tuple-element.26.table, bf16[15,128,256]{2,1,0:T(8,128)(2,1)S(1)} %get-tuple-element.30.view, bf16[14,8,128,128]{3,2,1,0:T(8,128)(2,1)} %tiles.7, ...), custom_call_target="tpu_custom_call" | custom-call | flops 503316480 | bytes 5242880 | tf_op jit(solution)/shard_map/own_rows/pallas_call | solution.py:334
  55.2 20.8 %all-to-all-done.1.incoming = bf16[16,128,256]{2,1,0:T(8,128)(2,1)S(1)} async-done(((bf16[16,128,256]{2,1,0:T(8,128)(2,1)}), bf16[16,128,256]{2,1,0:T(8,128)(2,1)S(1)}, u32[]{:S(2)}, u32[]{:S(2)}) %all-to-all-start.1) | async-done | bytes 1048608 | tf_op jit(solution)/shard_map/all_to_all | solution.py:298
  76.0 2.1 %split_rows.1 = (f32[2,128,256]{2,1,0:T(8,128)S(1)}, bf16[16,144,256]{2,1,0:T(8,128)(2,1)}, f32[2,256]{1,0:T(2,128)S(1)}) custom-call(s32[136]{0:T(256)S(1)} %get-tuple-element.26.table, bf16[16,128,256]{2,1,0:T(8,128)(2,1)S(1)} %all-to-all-done.1.incoming, f32[2,128,256]{2,1,0:T(8,128)S(1)} %get-tuple-element.31.part_split, ...), custom_call_target="tpu_custom_call" | custom-call | flops 33554432 | bytes 3145728 | tf_op jit(solution)/shard_map/split_rows/pallas_call | solution.py:342
  78.2 0.0 copy-start.6
  78.2 0.0 copy-start.7
  78.2 6.8 %all-to-all-start.2 = ((bf16[16,144,256]{2,1,0:T(8,128)(2,1)}), bf16[16,144,256]{2,1,0:T(8,128)(2,1)S(1)}, u32[]{:S(2)}, u32[]{:S(2)}) async-start(bf16[16,144,256]{2,1,0:T(8,128)(2,1)} %get-tuple-element.34), calls=%async_computation.2 | async-start | bytes 2359296 | tf_op jit(solution)/shard_map/all_to_all | solution.py:298
  85.0 15.5 %psum.14 = f32[2,256]{1,0:T(2,128)S(1)} all-reduce(f32[2,256]{1,0:T(2,128)S(1)} %get-tuple-element.35), channel_id=1, replica_groups=mesh['gx'=8,'gy_0'=2,'gy_1'=2,'gz_0'=4,'gz_1'=4] {'gx'}, use_global_device_ids=true, to_apply=%region_0.0 | all-reduce | flops 512 | bytes 4096 | tf_op jit(solution)/shard_map/psum | solution.py:358
  100.5 2.5 %psum.15 = f32[2,256]{1,0:T(2,128)S(1)} all-reduce(f32[2,256]{1,0:T(2,128)S(1)} %psum.14), channel_id=1, replica_groups=mesh['gx'=8,'gy_0'=2,'gy_1'=2,'gz_0'=4,'gz_1'=4] {'gy_1'}, use_global_device_ids=true, to_apply=%region_1.0 | all-reduce | flops 512 | bytes 4096 | tf_op jit(solution)/shard_map/psum | solution.py:358
  103.0 7.8 %all-to-all-done.2.incoming = bf16[16,144,256]{2,1,0:T(8,128)(2,1)S(1)} async-done(((bf16[16,144,256]{2,1,0:T(8,128)(2,1)}), bf16[16,144,256]{2,1,0:T(8,128)(2,1)S(1)}, u32[]{:S(2)}, u32[]{:S(2)}) %all-to-all-start.2) | async-done | bytes 1179680 | tf_op jit(solution)/shard_map/all_to_all | solution.py:298
  110.8 21.3 %all_to_all.25.sums = f32[32,2,256]{2,1,0:T(2,128)S(1)} all-to-all(f32[32,2,256]{2,1,0:T(2,128)S(1)} %broadcast_in_dim.3), channel_id=1, replica_groups=mesh['gx'=8,'gy_0'=2,'gy_1'=2,'gz_0'=4,'gz_1'=4] {'gy_0','gz_0','gz_1'}, dimensions={0} | all-to-all | bytes 131072 | tf_op jit(solution)/shard_map/all_to_all | solution.py:298
  132.2 0.0 copy-done.7
  132.2 4.3 %hidden_replicas.1 = (bf16[16,128,256]{2,1,0:T(8,128)(2,1)}, bf16[15,128,256]{2,1,0:T(8,128)(2,1)S(1)}) custom-call(s32[136]{0:T(256)S(1)} %get-tuple-element.26.table, f32[32,2,256]{2,1,0:T(2,128)S(1)} %all_to_all.25.sums, f32[1,256]{1,0:T(1,128)S(1)} %bitcast.6, f32[1,256]{1,0:T(1,128)S(1)} %bitcast.7, f32[4,128,256]{2,1,0:T(8,128)S(1)} %get-tuple-element.37.first_own, ...), custom_call_target="tpu_custom_call" | custom-call | flops 536870912 | bytes 5242880 | tf_op jit(solution)/shard_map/hidden_replicas/pallas_call | solution.py:362
  136.5 0.0 copy-start.2
  136.5 0.0 copy-start.4
  136.5 3.8 %all-to-all-start.4 = ((bf16[16,128,256]{2,1,0:T(8,128)(2,1)}), bf16[16,128,256]{2,1,0:T(8,128)(2,1)S(1)}, u32[]{:S(2)}, u32[]{:S(2)}) async-start(bf16[16,128,256]{2,1,0:T(8,128)(2,1)} %get-tuple-element.40), calls=%async_computation.4 | async-start | bytes 2097152 | tf_op jit(solution)/shard_map/all_to_all | solution.py:298
  140.4 4.4 %own_rows_two.1 = (bf16[6,128,256]{2,1,0:T(8,128)(2,1)}, f32[2,128,256]{2,1,0:T(8,128)S(1)}, f32[2,128,256]{2,1,0:T(8,128)S(1)}) custom-call(s32[136]{0:T(256)S(1)} %get-tuple-element.26.table, bf16[15,128,256]{2,1,0:T(8,128)(2,1)S(1)} %get-tuple-element.41.view, bf16[14,8,128,128]{3,2,1,0:T(8,128)(2,1)} %tiles.7, bf16[256,256]{1,0:T(8,128)(2,1)S(1)} %copy-done.4, ...), custom_call_target="tpu_custom_call" | custom-call | flops 503316480 | bytes 5242880 | tf_op jit(solution)/shard_map/own_rows_two/pallas_call | solution.py:371
  144.7 24.6 %all-to-all-done.4.incoming = bf16[16,128,256]{2,1,0:T(8,128)(2,1)S(1)} async-done(((bf16[16,128,256]{2,1,0:T(8,128)(2,1)}), bf16[16,128,256]{2,1,0:T(8,128)(2,1)S(1)}, u32[]{:S(2)}, u32[]{:S(2)}) %all-to-all-start.4) | async-done | bytes 1048608 | tf_op jit(solution)/shard_map/all_to_all | solution.py:298
  169.3 1.6 split_rows_two.1
  (12 shorter events, 0.0 us)
Async XLA Ops:
  0.0 15.6 %copy-start.9 = (s32[14,8]{0,1:T(8,128)S(1)}, s32[14,8]{0,1:T(8,128)}, u32[]{:S(2)}) copy-start(s32[14,8]{0,1:T(8,128)} %param.14) | copy-start | bytes 1348
  0.0 15.7 %copy-start.10 = (s32[14,8]{0,1:T(8,128)S(1)}, s32[14,8]{0,1:T(8,128)}, u32[]{:S(2)}) copy-start(s32[14,8]{0,1:T(8,128)} %param.15) | copy-start | bytes 1348
  0.0 15.7 %copy-start = (bf16[768,256]{1,0:T(8,128)(2,1)S(1)}, bf16[768,256]{1,0:T(8,128)(2,1)}, u32[]{:S(2)}) copy-start(bf16[768,256]{1,0:T(8,128)(2,1)} %param.12) | copy-start | bytes 1179652
  0.0 15.7 %copy-start.5 = (s32[128]{0:T(128)S(1)}, s32[128]{0:T(128)}, u32[]{:S(2)}) copy-start(s32[128]{0:T(128)} %root.3) | copy-start | bytes 1540
  2.7 13.1 %copy-start.8 = (s32[16]{0:T(128)S(1)}, s32[16]{0:T(128)}, u32[]{:S(2)}) copy-start(s32[16]{0:T(128)} %get-tuple-element.25.sel) | copy-start | bytes 196
  2.7 37.1 %all-to-all-start = ((bf16[16,128,256]{2,1,0:T(8,128)(2,1)}), bf16[16,128,256]{2,1,0:T(8,128)(2,1)S(1)}, u32[]{:S(2)}, u32[]{:S(2)}) async-start(bf16[16,128,256]{2,1,0:T(8,128)(2,1)} %get-tuple-element.28), calls=%async_computation | async-start | bytes 2097152 | tf_op jit(solution)/shard_map/all_to_all | solution.py:298
  44.0 7.3 %copy-start.1 = (bf16[256,256]{1,0:T(8,128)(2,1)S(1)}, bf16[256,256]{1,0:T(8,128)(2,1)}, u32[]{:S(2)}) copy-start(bf16[256,256]{1,0:T(8,128)(2,1)} %w_neigh.5) | copy-start | bytes 393220
  44.1 7.3 %copy-start.3 = (bf16[256,256]{1,0:T(8,128)(2,1)S(1)}, bf16[256,256]{1,0:T(8,128)(2,1)}, u32[]{:S(2)}) copy-start(bf16[256,256]{1,0:T(8,128)(2,1)} %w_self.2) | copy-start | bytes 393220
  44.1 31.9 %all-to-all-start.1 = ((bf16[16,128,256]{2,1,0:T(8,128)(2,1)}), bf16[16,128,256]{2,1,0:T(8,128)(2,1)S(1)}, u32[]{:S(2)}, u32[]{:S(2)}) async-start(bf16[16,128,256]{2,1,0:T(8,128)(2,1)} %get-tuple-element.29), calls=%async_computation.1 | async-start | bytes 2097152 | tf_op jit(solution)/shard_map/all_to_all | solution.py:298
  78.2 54.0 %copy-start.6 = (f32[256]{0:T(256)S(1)}, f32[256]{0:T(256)}, u32[]{:S(2)}) copy-start(f32[256]{0:T(256)} %param.20) | copy-start | bytes 3076
  78.2 54.0 %copy-start.7 = (f32[256]{0:T(256)S(1)}, f32[256]{0:T(256)}, u32[]{:S(2)}) copy-start(f32[256]{0:T(256)} %param.21) | copy-start | bytes 3076
  78.2 32.6 %all-to-all-start.2 = ((bf16[16,144,256]{2,1,0:T(8,128)(2,1)}), bf16[16,144,256]{2,1,0:T(8,128)(2,1)S(1)}, u32[]{:S(2)}, u32[]{:S(2)}) async-start(bf16[16,144,256]{2,1,0:T(8,128)(2,1)} %get-tuple-element.34), calls=%async_computation.2 | async-start | bytes 2359296 | tf_op jit(solution)/shard_map/all_to_all | solution.py:298
  136.5 3.8 %copy-start.2 = (bf16[256,256]{1,0:T(8,128)(2,1)S(1)}, bf16[256,256]{1,0:T(8,128)(2,1)}, u32[]{:S(2)}) copy-start(bf16[256,256]{1,0:T(8,128)(2,1)} %w_neigh.7) | copy-start | bytes 393220
  136.5 3.8 %copy-start.4 = (bf16[256,256]{1,0:T(8,128)(2,1)S(1)}, bf16[256,256]{1,0:T(8,128)(2,1)}, u32[]{:S(2)}) copy-start(bf16[256,256]{1,0:T(8,128)(2,1)} %w_self.3) | copy-start | bytes 393220
  136.5 32.8 %all-to-all-start.4 = ((bf16[16,128,256]{2,1,0:T(8,128)(2,1)}), bf16[16,128,256]{2,1,0:T(8,128)(2,1)S(1)}, u32[]{:S(2)}, u32[]{:S(2)}) async-start(bf16[16,128,256]{2,1,0:T(8,128)(2,1)} %get-tuple-element.40), calls=%async_computation.4 | async-start | bytes 2097152 | tf_op jit(solution)/shard_map/all_to_all | solution.py:298

commit v3 on v2

--- a/solution.py
+++ b/solution.py
@@ -22,7 +22,7 @@
 GZ = ("gz_0", "gz_1")
 GX_GY_GZ = ("gx", "gy_0", "gy_1", "gz_0", "gz_1")
 GX_GY = ("gx", "gy_0", "gy_1")
-REST = ("gy_0", "gz_0", "gz_1")
+COLUMN = ("gy_0", "gy_1", "gz_1")
 ROOTS_AT = 112
 SEL_AT = 120
 
@@ -58,15 +58,8 @@
     return lax.axis_index("gz_0") * 4 + lax.axis_index("gz_1")
 
 
-def send_selected(sel, blocks, out, sems):
-    copies = [
-        pltpu.make_async_copy(blocks.at[jnp.maximum(sel(q) - 1, 0)], out.at[q], sems.at[q])
-        for q in range(GROUP)
-    ]
-    for c in copies:
-        c.start()
-    for c in copies:
-        c.wait()
+def loop(n, step):
+    lax.fori_loop(0, n, lambda i, c: (step(i), c)[1], 0)
 
 
 def outgoing_kernel(root, block, rows, out, sel, split, root_s, block_s, sem, sems):
@@ -80,29 +73,36 @@
     for c in loads:
         c.wait()
     mine = my_place()
-    for q in range(GROUP):
+
+    def send(q, chosen):
+        return pltpu.make_async_copy(split.at[chosen], out.at[q], sems.at[q])
+
+    def select(q):
         held = jnp.int32(0)
         for j in range(HOST):
             held = jnp.where(root_s[q * HOST + j] == mine, block_s[q * HOST + j] + 1, held)
         sel[q] = held
-    send_selected(lambda q: sel[q], split, out, sems)
-
-
-def tables_kernel(root, cols, present, sel, rows, table, rows_v, sem):
-    load_rows = pltpu.make_async_copy(rows, rows_v, sem)
+        send(q, jnp.maximum(held - 1, 0)).start()
+
+    loop(GROUP, select)
+    loop(GROUP, lambda q: send(q, 0).wait())
+
+
+def tables_kernel(root, cols, present, sel, rows, table, view, sem):
+    load_rows = pltpu.make_async_copy(rows, view.at[pl.ds(0, ROOTED)], sem)
     load_rows.start()
     mine = my_place()
 
-    def slots(b, carry):
+    def slots(b):
         for k in range(K):
             table[b * K + k] = jnp.where(present[b, k] > 0, cols[b, k], SLOTS)
-        return carry
-
-    lax.fori_loop(0, SLOTS, slots, 0)
+
+    loop(SLOTS, slots)
     for h in range(HOST):
         table[ROOTS_AT + h] = root[mine * HOST + h]
     for q in range(GROUP):
         table[SEL_AT + q] = sel[q]
+    view[SLOTS] = jnp.zeros((TILE, F), bf16)
     load_rows.wait()
 
 
@@ -111,7 +111,7 @@
 
 
 def load_tiles(tiles, tbuf, tsem, first, count):
-    lax.fori_loop(0, count, lambda i, c: (tile_copy(tiles, tbuf, tsem, first, i).start(), c)[1], 0)
+    loop(count, lambda i: tile_copy(tiles, tbuf, tsem, first, i).start())
 
 
 def tile_row(table, tiles, tbuf, tsem, first, i, view):
@@ -130,34 +130,27 @@
     def send(h):
         return pltpu.make_async_copy(obuf.at[h], out.at[table[ROOTS_AT + h]], osem.at[h])
 
-    def step(h, carry):
+    def step(h):
         obuf[h] = tile_row(table, tiles, tbuf, tsem, ROOTED, h, view).astype(bf16)
 
         @pl.when(h > 0)
         def _():
             send(h - 1).start()
 
-        return carry
-
-    lax.fori_loop(0, HOST, step, 0)
+    loop(HOST, step)
     send(HOST - 1).start()
-    lax.fori_loop(0, HOST, lambda h, c: (send(h).wait(), c)[1], 0)
-
-
-def replica_kernel(table, rows, incoming, tiles, out, view, tbuf, obuf, tsem, osem):
+    loop(HOST, lambda h: send(h).wait())
+
+
+def replica_kernel(table, begun, incoming, tiles, out, view, tbuf, obuf, vsem, tsem, osem):
+    def hosted(h):
+        return pltpu.make_async_copy(
+            incoming.at[table[ROOTS_AT + h]], view.at[ROOTED + h], vsem.at[h]
+        )
+
+    loop(HOST, lambda h: hosted(h).start())
     load_tiles(tiles, tbuf, tsem, ROOTED, HOST)
-
-    def own(b, carry):
-        view[b] = rows[b]
-        return carry
-
-    def hosted(h, carry):
-        view[ROOTED + h] = incoming[table[ROOTS_AT + h]]
-        return carry
-
-    lax.fori_loop(0, ROOTED, own, 0)
-    lax.fori_loop(0, HOST, hosted, 0)
-    view[SLOTS] = jnp.zeros((TILE, F), bf16)
+    loop(HOST, lambda h: hosted(h).wait())
     replica_rows(table, tiles, out, view, tbuf, obuf, tsem, osem)
 
 
@@ -183,34 +176,48 @@
 
 
 def add_replicas(table, incoming, total):
-    for q in range(GROUP):
+    def add(q):
         s = table[SEL_AT + q]
 
         @pl.when(s > 0)
-        def _(q=q, s=s):
+        def _():
             total[s - 1] += incoming[q].astype(f32)
 
-
-def split_kernel(
-    table, incoming, part_split, self_split, own_sums, w_neigh, first_split, out, sums, total, pay, sems
-):
+    loop(GROUP, add)
+
+
+def split_kernel(table, incoming, part_split, self_split, own_sums, w_neigh, first_split, sums, total):
     total[...] = part_split[...]
     add_replicas(table, incoming, total)
-    for s in range(SPLIT):
-        first_split[s] = self_split[s] + dot(total[s].astype(bf16), w_neigh[...])
     s1, s2 = own_sums[0:1], own_sums[1:2]
     for s in range(SPLIT):
-        first = first_split[s]
+        first = self_split[s] + dot(total[s].astype(bf16), w_neigh[...])
+        first_split[s] = first
         s1 += jnp.sum(first, axis=0, keepdims=True)
         s2 += jnp.sum(first * first, axis=0, keepdims=True)
-    sums[0:1] = s1
-    sums[1:2] = s2
-    center = (s1 * (1.0 / (ROOTED * TILE))).astype(bf16)
+
+    def fill(q):
+        sums[q, 0:1] = s1
+        sums[q, 1:2] = s2
+
+    loop(GROUP, fill)
+
+
+def centered_kernel(table, first_split, sums, out, pay, sems):
+    center = (sums[0, 0:1] * (1.0 / (ROOTED * TILE))).astype(bf16)
     shift = center.astype(f32)
-    for s in range(SPLIT):
+
+    def fill(s):
         pay[s, pl.ds(0, TILE)] = (first_split[s] - shift).astype(bf16)
         pay[s, pl.ds(TILE, CENTER_ROWS)] = jnp.broadcast_to(center, (CENTER_ROWS, F))
-    send_selected(lambda q: table[SEL_AT + q], pay, out, sems)
+
+    def send(q):
+        chosen = jnp.maximum(table[SEL_AT + q] - 1, 0)
+        return pltpu.make_async_copy(pay.at[chosen], out.at[q], sems.at[q])
+
+    loop(SPLIT, fill)
+    loop(GROUP, lambda q: send(q).start())
+    loop(GROUP, lambda q: send(q).wait())
 
 
 def hidden_kernel(
@@ -218,9 +225,8 @@
     out, view, tbuf, obuf, tsem, osem,
 ):
     load_tiles(tiles, tbuf, tsem, ROOTED, HOST)
-    total = jnp.sum(sums[...], axis=0)
-    mean = total[0:1] * (1.0 / count)
-    var = total[1:2] * (1.0 / count) - mean * mean
+    mean = sums[0:1] * (1.0 / count)
+    var = sums[1:2] * (1.0 / count) - mean * mean
     inv = lax.rsqrt(var + 1e-5)
 
     def norm(first, less):
@@ -299,7 +305,7 @@
 
     outgoing, sel = call(
         outgoing_kernel, "outgoing", 0, 2 << 20, room=60 << 20,
-        out_shape=(wire, shape((GROUP,), jnp.int32)),
+        out_shape=(wire, pltpu.SMEM((GROUP,), jnp.int32)),
         in_specs=[HBM] * 3,
         out_specs=(HBM, SMEM),
         scratch_shapes=[
@@ -311,11 +317,11 @@
     )(host_root, host_block, rows)
     incoming = exchange(outgoing)
 
-    table, rows_v = call(
+    table, view = call(
         tables_kernel, "tables", 0, 8 << 20,
         out_shape=(
-            shape((SEL_AT + GROUP,), jnp.int32),
-            pltpu.VMEM((ROOTED, TILE, F), bf16),
+            pltpu.SMEM((SEL_AT + GROUP,), jnp.int32),
+            view_v,
         ),
         in_specs=[SMEM] * 4 + [HBM],
         out_specs=(SMEM, VMEM),
@@ -327,8 +333,9 @@
         out_shape=(wire, view_v),
         in_specs=[SMEM] + [VMEM] * 2 + [HBM],
         out_specs=(HBM, VMEM),
-        scratch_shapes=[tile_rows(HOST), row_buffer, DMA((HOST,)), DMA((HOST,))],
-    )(table, rows_v, incoming, tile_values)
+        input_output_aliases={1: 1},
+        scratch_shapes=[tile_rows(HOST), row_buffer] + [DMA((HOST,))] * 3,
+    )(table, view, incoming, tile_values)
     returned = exchange(outgoing)
 
     first_own, self_split, part_split, own_sums = call(
@@ -339,25 +346,24 @@
         scratch_shapes=[tile_rows(ROOTED), DMA((ROOTED,))],
     )(table, view, tile_values, self_one, neigh_one)
 
-    first_split, outgoing, sums = call(
+    first_split, sums = call(
         split_kernel, "split_rows", 4 * MAC, 3 << 20,
-        out_shape=(
-            split_f32,
-            pltpu.HBM((GROUP, TILE + CENTER_ROWS, F), bf16),
-            pltpu.VMEM((2, F), f32),
-        ),
+        out_shape=(split_f32, pltpu.VMEM((GROUP, 2, F), f32)),
         in_specs=[SMEM] + [VMEM] * 5,
-        out_specs=(VMEM, HBM, VMEM),
-        scratch_shapes=[
-            pltpu.VMEM((SPLIT, TILE, F), f32),
-            pltpu.VMEM((SPLIT, TILE + CENTER_ROWS, F), bf16),
-            DMA((GROUP,)),
-        ],
+        out_specs=(VMEM, VMEM),
+        scratch_shapes=[pltpu.VMEM((SPLIT, TILE, F), f32)],
     )(table, returned, part_split, self_split, own_sums, neigh_one)
+    column_sums = exchange(sums, COLUMN)
+    outgoing = call(
+        centered_kernel, "centered", 0, 2 << 20,
+        out_shape=pltpu.HBM((GROUP, TILE + CENTER_ROWS, F), bf16),
+        in_specs=[SMEM] + [VMEM] * 2,
+        out_specs=HBM,
+        scratch_shapes=[pltpu.VMEM((SPLIT, TILE + CENTER_ROWS, F), bf16), DMA((GROUP,))],
+    )(table, first_split, sums)
+    outgoing, column_sums = lax.optimization_barrier((outgoing, column_sums))
     incoming = exchange(outgoing)
-    sums = lax.psum(lax.psum(sums, "gx"), "gy_1")
-    incoming, sums = lax.optimization_barrier((incoming, sums))
-    sums = exchange(jnp.broadcast_to(sums, (2 * GROUP, 2, F)), REST)
+    sums = lax.psum(lax.psum(jnp.sum(column_sums, axis=0), "gx"), "gz_0")
 
     outgoing, view = call(
         functools.partial(hidden_kernel, count), "hidden_replicas", 64 * MAC, 5 << 20,

time: 172 us -> 168 us (0.977)
  the two profiles are of different devices: /device:TPU:40 before, /device:TPU:16 now
where the time goes in v3:
time: 168 us; the launch traced here: 167 us
  waiting for transfers between devices  81 us (48%)
  starting transfers between devices  35.7 us (21%)
  blocking collectives  26.5 us (16%)
  Pallas kernels  23.1 us (14%)
    all_to_all x5, waiting for transfers between devices, exchange(): return lax.all_to_all(blocks, axes, split_axis=0, concat_axis=0, tiled=True)  81 us
    all_to_all x5, starting transfers between devices, exchange(): return lax.all_to_all(blocks, axes, split_axis=0, concat_axis=0, tiled=True)  35.7 us
    psum x2, blocking collectives, per_device(): sums = lax.psum(lax.psum(jnp.sum(column_sums, axis=0), 'gx'), 'gz_0')  26.5 us
    pallas_call x1, Pallas kernels, per_device(): call(replica_kernel, 'replicas', 64 * MAC, 4 << 20, out_shape=(wire, view...  4.45 us
    pallas_call x1, Pallas kernels, per_device(): call(own_two_kernel, 'own_rows_two', 60 * MAC, 5 << 20, out_shape=(shape(...  3.83 us
    pallas_call x1, Pallas kernels, per_device(): call(functools.partial(hidden_kernel, count), 'hidden_replicas', 64 * MAC...  3.72 us
  transfers between devices with their start and end apart: 5, of which 5 were waited for; matrix products, arithmetic and copies ran while one was open for 0% of the time, Pallas kernels for 6%

profile of v3, /device:TPU:16, one launch (start us, length us, event | category | flops | bytes accessed | tf_op | source)
XLA Modules:
  0.0 166.8 jit_solution(17599933497512651135)
XLA Ops:
  0.0 2.1 %outgoing.1 = (bf16[16,128,256]{2,1,0:T(8,128)(2,1)}, s32[16]{0:T(128)S(4)}) custom-call(s32[128]{0:T(128)} %root.3, s32[128]{0:T(128)} %block.1, bf16[6,128,256]{2,1,0:T(8,128)(2,1)} %bitcast.4), custom_call_target="tpu_custom_call" | custom-call | bytes 2097152 | tf_op jit(solution)/shard_map/outgoing/pallas_call | solution.py:306
  2.1 12.9 %all-to-all-start = ((bf16[16,128,256]{2,1,0:T(8,128)(2,1)}), bf16[16,128,256]{2,1,0:T(8,128)(2,1)S(1)}, u32[]{:S(2)}, u32[]{:S(2)}) async-start(bf16[16,128,256]{2,1,0:T(8,128)(2,1)} %get-tuple-element.27), calls=%async_computation | async-start | bytes 2097152 | tf_op jit(solution)/shard_map/all_to_all | solution.py:304
  15.0 0.1 copy.15.cols
  15.1 0.0 copy-done.9
  15.1 0.1 copy.16.present
  15.2 0.0 copy-done.5
  15.2 1.3 tables.1
  16.5 22.7 %all-to-all-done.incoming = bf16[16,128,256]{2,1,0:T(8,128)(2,1)S(1)} async-done(((bf16[16,128,256]{2,1,0:T(8,128)(2,1)}), bf16[16,128,256]{2,1,0:T(8,128)(2,1)S(1)}, u32[]{:S(2)}, u32[]{:S(2)}) %all-to-all-start) | async-done | bytes 1048608 | tf_op jit(solution)/shard_map/all_to_all | solution.py:304
  39.3 4.5 %replicas.1 = (bf16[16,128,256]{2,1,0:T(8,128)(2,1)}, bf16[15,128,256]{2,1,0:T(8,128)(2,1)S(1)}) custom-call(s32[136]{0:T(256)S(4)} %get-tuple-element.25.table, bf16[15,128,256]{2,1,0:T(8,128)(2,1)S(1)} %get-tuple-element.26.begun, bf16[16,128,256]{2,1,0:T(8,128)(2,1)S(1)} %all-to-all-done.incoming, ...), custom_call_target="tpu_custom_call", output_to_operand_aliasing={{1}: (1, {})} | custom-call | flops 536870912 | bytes 4194304 | tf_op jit(solution)/shard_map/replicas/pallas_call | solution.py:331
  43.7 0.0 copy-start.1
  43.7 0.0 copy-start.3
  43.7 7.3 %all-to-all-start.1 = ((bf16[16,128,256]{2,1,0:T(8,128)(2,1)}), bf16[16,128,256]{2,1,0:T(8,128)(2,1)S(1)}, u32[]{:S(2)}, u32[]{:S(2)}) async-start(bf16[16,128,256]{2,1,0:T(8,128)(2,1)} %get-tuple-element.28), calls=%async_computation.1 | async-start | bytes 2097152 | tf_op jit(solution)/shard_map/all_to_all | solution.py:304
  51.1 3.3 %own_rows.1 = (f32[4,128,256]{2,1,0:T(8,128)S(1)}, f32[2,128,256]{2,1,0:T(8,128)S(1)}, f32[2,128,256]{2,1,0:T(8,128)S(1)}, f32[2,256]{1,0:T(2,128)S(1)}) custom-call(s32[136]{0:T(256)S(4)} %get-tuple-element.25.table, bf16[15,128,256]{2,1,0:T(8,128)(2,1)S(1)} %get-tuple-element.29.view, bf16[14,8,128,128]{3,2,1,0:T(8,128)(2,1)} %tiles.7, ...), custom_call_target="tpu_custom_call" | custom-call | flops 503316480 | bytes 5242880 | tf_op jit(solution)/shard_map/own_rows/pallas_call | solution.py:341
  54.4 21.3 %all-to-all-done.1.incoming = bf16[16,128,256]{2,1,0:T(8,128)(2,1)S(1)} async-done(((bf16[16,128,256]{2,1,0:T(8,128)(2,1)}), bf16[16,128,256]{2,1,0:T(8,128)(2,1)S(1)}, u32[]{:S(2)}, u32[]{:S(2)}) %all-to-all-start.1) | async-done | bytes 1048608 | tf_op jit(solution)/shard_map/all_to_all | solution.py:304
  75.7 1.2 split_rows.1
  77.0 7.6 %all-to-all-start.2 = ((f32[16,2,256]{2,1,0:T(2,128)}), f32[16,2,256]{2,1,0:T(2,128)S(1)}, u32[]{:S(2)}, u32[]{:S(2)}) async-start(f32[16,2,256]{2,1,0:T(2,128)} %get-tuple-element.34.sums), calls=%async_computation.2 | async-start | bytes 65536 | tf_op jit(solution)/shard_map/all_to_all | solution.py:304
  84.6 2.0 %centered.1 = bf16[16,144,256]{2,1,0:T(8,128)(2,1)} custom-call(s32[136]{0:T(256)S(4)} %get-tuple-element.25.table, f32[2,128,256]{2,1,0:T(8,128)S(1)} %get-tuple-element.33.first_split, f32[16,2,256]{2,1,0:T(2,128)} %get-tuple-element.34.sums), custom_call_target="tpu_custom_call" | custom-call | bytes 2097152 | tf_op jit(solution)/shard_map/centered/pallas_call | solution.py:357
  86.6 0.0 copy-start.6
  86.6 0.0 copy-start.7
  86.6 5.7 %all-to-all-done.2 = f32[16,2,256]{2,1,0:T(2,128)S(1)} async-done(((f32[16,2,256]{2,1,0:T(2,128)}), f32[16,2,256]{2,1,0:T(2,128)S(1)}, u32[]{:S(2)}, u32[]{:S(2)}) %all-to-all-start.2) | async-done | bytes 32800 | tf_op jit(solution)/shard_map/all_to_all | solution.py:304
  92.3 3.7 %all-to-all-start.3 = ((bf16[16,144,256]{2,1,0:T(8,128)(2,1)}), bf16[16,144,256]{2,1,0:T(8,128)(2,1)S(1)}, u32[]{:S(2)}, u32[]{:S(2)}) async-start(bf16[16,144,256]{2,1,0:T(8,128)(2,1)} %centered.1), calls=%async_computation.3 | async-start | bytes 2359296 | tf_op jit(solution)/shard_map/all_to_all | solution.py:304
  96.0 15.3 %psum.14 = f32[2,256]{1,0:T(2,128)S(1)} all-reduce(f32[2,256]{1,0:T(2,128)S(1)} %reduce_sum.9), channel_id=1, replica_groups=mesh['gx'=8,'gy_0'=2,'gy_1'=2,'gz_0'=4,'gz_1'=4] {'gx'}, use_global_device_ids=true, to_apply=%region_1.0 | all-reduce | flops 512 | bytes 4096 | tf_op jit(solution)/shard_map/psum | solution.py:366
  111.3 11.2 %psum.15.sums = f32[2,256]{1,0:T(2,128)S(1)} all-reduce(f32[2,256]{1,0:T(2,128)S(1)} %psum.14), channel_id=1, replica_groups=mesh['gx'=8,'gy_0'=2,'gy_1'=2,'gz_0'=4,'gz_1'=4] {'gz_0'}, use_global_device_ids=true, to_apply=%region_2.0 | all-reduce | flops 512 | bytes 4096 | tf_op jit(solution)/shard_map/psum | solution.py:366
  122.6 6.3 %all-to-all-done.3.incoming = bf16[16,144,256]{2,1,0:T(8,128)(2,1)S(1)} async-done(((bf16[16,144,256]{2,1,0:T(8,128)(2,1)}), bf16[16,144,256]{2,1,0:T(8,128)(2,1)S(1)}, u32[]{:S(2)}, u32[]{:S(2)}) %all-to-all-start.3) | async-done | bytes 1179680 | tf_op jit(solution)/shard_map/all_to_all | solution.py:304
  128.9 0.0 copy-done.7
  128.9 3.7 %hidden_replicas.1 = (bf16[16,128,256]{2,1,0:T(8,128)(2,1)}, bf16[15,128,256]{2,1,0:T(8,128)(2,1)S(1)}) custom-call(s32[136]{0:T(256)S(4)} %get-tuple-element.25.table, f32[2,256]{1,0:T(2,128)S(1)} %psum.15.sums, f32[1,256]{1,0:T(1,128)S(1)} %bitcast.6, f32[1,256]{1,0:T(1,128)S(1)} %bitcast.7, f32[4,128,256]{2,1,0:T(8,128)S(1)} %get-tuple-element.36.first_own, ...), custom_call_target="tpu_custom_call" | custom-call | flops 536870912 | bytes 5242880 | tf_op jit(solution)/shard_map/hidden_replicas/pallas_call | solution.py:368
  132.6 0.0 copy-start.2
  132.6 0.0 copy-start.4
  132.6 4.2 %all-to-all-start.4 = ((bf16[16,128,256]{2,1,0:T(8,128)(2,1)}), bf16[16,128,256]{2,1,0:T(8,128)(2,1)S(1)}, u32[]{:S(2)}, u32[]{:S(2)}) async-start(bf16[16,128,256]{2,1,0:T(8,128)(2,1)} %get-tuple-element.38), calls=%async_computation.4 | async-start | bytes 2097152 | tf_op jit(solution)/shard_map/all_to_all | solution.py:304
  136.8 3.8 %own_rows_two.1 = (bf16[6,128,256]{2,1,0:T(8,128)(2,1)}, f32[2,128,256]{2,1,0:T(8,128)S(1)}, f32[2,128,256]{2,1,0:T(8,128)S(1)}) custom-call(s32[136]{0:T(256)S(4)} %get-tuple-element.25.table, bf16[15,128,256]{2,1,0:T(8,128)(2,1)S(1)} %get-tuple-element.39.view, bf16[14,8,128,128]{3,2,1,0:T(8,128)(2,1)} %tiles.7, bf16[256,256]{1,0:T(8,128)(2,1)S(1)} %copy-done.4, ...), custom_call_target="tpu_custom_call" | custom-call | flops 503316480 | bytes 5242880 | tf_op jit(solution)/shard_map/own_rows_two/pallas_call | solution.py:377
  140.7 24.9 %all-to-all-done.4.incoming = bf16[16,128,256]{2,1,0:T(8,128)(2,1)S(1)} async-done(((bf16[16,128,256]{2,1,0:T(8,128)(2,1)}), bf16[16,128,256]{2,1,0:T(8,128)(2,1)S(1)}, u32[]{:S(2)}, u32[]{:S(2)}) %all-to-all-start.4) | async-done | bytes 1048608 | tf_op jit(solution)/shard_map/all_to_all | solution.py:304
  165.6 1.2 split_rows_two.1
  (12 shorter events, 0.1 us)
Async XLA Ops:
  0.0 15.0 %copy-start.8 = (s32[14,8]{0,1:T(8,128)S(1)}, s32[14,8]{0,1:T(8,128)}, u32[]{:S(2)}) copy-start(s32[14,8]{0,1:T(8,128)} %param.14) | copy-start | bytes 1348
  0.0 15.1 %copy-start.9 = (s32[14,8]{0,1:T(8,128)S(1)}, s32[14,8]{0,1:T(8,128)}, u32[]{:S(2)}) copy-start(s32[14,8]{0,1:T(8,128)} %param.15) | copy-start | bytes 1348
  0.0 15.2 %copy-start = (bf16[768,256]{1,0:T(8,128)(2,1)S(1)}, bf16[768,256]{1,0:T(8,128)(2,1)}, u32[]{:S(2)}) copy-start(bf16[768,256]{1,0:T(8,128)(2,1)} %param.12) | copy-start | bytes 1179652
  0.0 15.2 %copy-start.5 = (s32[128]{0:T(128)S(1)}, s32[128]{0:T(128)}, u32[]{:S(2)}) copy-start(s32[128]{0:T(128)} %root.3) | copy-start | bytes 1540
  2.1 37.1 %all-to-all-start = ((bf16[16,128,256]{2,1,0:T(8,128)(2,1)}), bf16[16,128,256]{2,1,0:T(8,128)(2,1)S(1)}, u32[]{:S(2)}, u32[]{:S(2)}) async-start(bf16[16,128,256]{2,1,0:T(8,128)(2,1)} %get-tuple-element.27), calls=%async_computation | async-start | bytes 2097152 | tf_op jit(solution)/shard_map/all_to_all | solution.py:304
  43.7 7.4 %copy-start.1 = (bf16[256,256]{1,0:T(8,128)(2,1)S(1)}, bf16[256,256]{1,0:T(8,128)(2,1)}, u32[]{:S(2)}) copy-start(bf16[256,256]{1,0:T(8,128)(2,1)} %w_neigh.5) | copy-start | bytes 393220
  43.7 7.4 %copy-start.3 = (bf16[256,256]{1,0:T(8,128)(2,1)S(1)}, bf16[256,256]{1,0:T(8,128)(2,1)}, u32[]{:S(2)}) copy-start(bf16[256,256]{1,0:T(8,128)(2,1)} %w_self.2) | copy-start | bytes 393220
  43.7 32.0 %all-to-all-start.1 = ((bf16[16,128,256]{2,1,0:T(8,128)(2,1)}), bf16[16,128,256]{2,1,0:T(8,128)(2,1)S(1)}, u32[]{:S(2)}, u32[]{:S(2)}) async-start(bf16[16,128,256]{2,1,0:T(8,128)(2,1)} %get-tuple-element.28), calls=%async_computation.1 | async-start | bytes 2097152 | tf_op jit(solution)/shard_map/all_to_all | solution.py:304
  77.0 15.3 %all-to-all-start.2 = ((f32[16,2,256]{2,1,0:T(2,128)}), f32[16,2,256]{2,1,0:T(2,128)S(1)}, u32[]{:S(2)}, u32[]{:S(2)}) async-start(f32[16,2,256]{2,1,0:T(2,128)} %get-tuple-element.34.sums), calls=%async_computation.2 | async-start | bytes 65536 | tf_op jit(solution)/shard_map/all_to_all | solution.py:304
  86.6 42.3 %copy-start.6 = (f32[256]{0:T(256)S(1)}, f32[256]{0:T(256)}, u32[]{:S(2)}) copy-start(f32[256]{0:T(256)} %param.20) | copy-start | bytes 3076
  86.6 42.3 %copy-start.7 = (f32[256]{0:T(256)S(1)}, f32[256]{0:T(256)}, u32[]{:S(2)}) copy-start(f32[256]{0:T(256)} %param.21) | copy-start | bytes 3076
  92.3 36.6 %all-to-all-start.3 = ((bf16[16,144,256]{2,1,0:T(8,128)(2,1)}), bf16[16,144,256]{2,1,0:T(8,128)(2,1)S(1)}, u32[]{:S(2)}, u32[]{:S(2)}) async-start(bf16[16,144,256]{2,1,0:T(8,128)(2,1)} %centered.1), calls=%async_computation.3 | async-start | bytes 2359296 | tf_op jit(solution)/shard_map/all_to_all | solution.py:304
  132.6 4.2 %copy-start.2 = (bf16[256,256]{1,0:T(8,128)(2,1)S(1)}, bf16[256,256]{1,0:T(8,128)(2,1)}, u32[]{:S(2)}) copy-start(bf16[256,256]{1,0:T(8,128)(2,1)} %w_neigh.7) | copy-start | bytes 393220
  132.6 4.2 %copy-start.4 = (bf16[256,256]{1,0:T(8,128)(2,1)S(1)}, bf16[256,256]{1,0:T(8,128)(2,1)}, u32[]{:S(2)}) copy-start(bf16[256,256]{1,0:T(8,128)(2,1)} %w_self.3) | copy-start | bytes 393220
  132.6 32.9 %all-to-all-start.4 = ((bf16[16,128,256]{2,1,0:T(8,128)(2,1)}), bf16[16,128,256]{2,1,0:T(8,128)(2,1)S(1)}, u32[]{:S(2)}, u32[]{:S(2)}) async-start(bf16[16,128,256]{2,1,0:T(8,128)(2,1)} %get-tuple-element.38), calls=%async_computation.4 | async-start | bytes 2097152 | tf_op jit(solution)/shard_map/all_to_all | solution.py:304

commit v4 on v3

--- a/solution.py
+++ b/solution.py
@@ -15,16 +15,24 @@
 SLOTS = 14
 K = 8
 TILE = 128
+CENTER_ROWS = 16
 F = 256
 GROUP = 16
-CENTER_ROWS = 16
 VMEM_BYTES = 50 << 20
 GZ = ("gz_0", "gz_1")
 GX_GY_GZ = ("gx", "gy_0", "gy_1", "gz_0", "gz_1")
 GX_GY = ("gx", "gy_0", "gy_1")
 COLUMN = ("gy_0", "gy_1", "gz_1")
+PLANE = ("gx", "gz_0")
+PLANE_SIZE = 32
+PART = TILE + CENTER_ROWS
 ROOTS_AT = 112
 SEL_AT = 120
+SOURCE_AT = 136
+WITHIN_AT = 144
+PASS_AT = 152
+ENTRIES = 164
+SIDE = 4
 
 f32 = jnp.float32
 bf16 = jnp.bfloat16
@@ -40,10 +48,9 @@
     return jax.ShapeDtypeStruct(dims, dtype)
 
 
-def call(body, name, flops, size, room=VMEM_BYTES, **kw):
+def call(body, flops, size, room=VMEM_BYTES, **kw):
     return pl.pallas_call(
         body,
-        name=name,
         compiler_params=pltpu.CompilerParams(vmem_limit_bytes=room),
         cost_estimate=pl.CostEstimate(flops=flops, bytes_accessed=size, transcendentals=0),
         **kw,
@@ -88,18 +95,34 @@
     loop(GROUP, lambda q: send(q, 0).wait())
 
 
-def tables_kernel(root, cols, present, sel, rows, table, view, sem):
+def tables_kernel(root, block, cols, present, sel, rows, table, view, sem):
     load_rows = pltpu.make_async_copy(rows, view.at[pl.ds(0, ROOTED)], sem)
     load_rows.start()
     mine = my_place()
+    my_x, my_z = lax.axis_index("gz_0"), lax.axis_index("gz_1")
 
     def slots(b):
         for k in range(K):
             table[b * K + k] = jnp.where(present[b, k] > 0, cols[b, k], SLOTS)
 
+    def passed_on(i):
+        target = ((my_x + 1 + i // SIDE) & (SIDE - 1)) * SIDE + my_z
+        source = my_x * SIDE + ((my_z - i) & (SIDE - 1))
+        chosen = jnp.int32(0)
+        for j in range(HOST):
+            at = target * HOST + j
+            chosen = jnp.where(root[at] == source, block[at], chosen)
+        table[PASS_AT + i] = chosen
+
     loop(SLOTS, slots)
+    loop((SIDE - 1) * SIDE, passed_on)
     for h in range(HOST):
-        table[ROOTS_AT + h] = root[mine * HOST + h]
+        q = root[mine * HOST + h]
+        table[ROOTS_AT + h] = q
+        along_x = (my_x - q // SIDE) & (SIDE - 1)
+        along_z = (my_z - q) & (SIDE - 1)
+        table[SOURCE_AT + h] = jnp.where(along_x == 0, along_z - 1, along_x + SIDE - 2)
+        table[WITHIN_AT + h] = jnp.where(along_x == 0, block[mine * HOST + h], along_z)
     for q in range(GROUP):
         table[SEL_AT + q] = sel[q]
     view[SLOTS] = jnp.zeros((TILE, F), bf16)
@@ -186,7 +209,7 @@
     loop(GROUP, add)
 
 
-def split_kernel(table, incoming, part_split, self_split, own_sums, w_neigh, first_split, sums, total):
+def split_kernel(table, incoming, part_split, self_split, own_sums, w_neigh, first_split, sums, parts, total):
     total[...] = part_split[...]
     add_replicas(table, incoming, total)
     s1, s2 = own_sums[0:1], own_sums[1:2]
@@ -201,55 +224,67 @@
         sums[q, 1:2] = s2
 
     loop(GROUP, fill)
-
-
-def centered_kernel(table, first_split, sums, out, pay, sems):
-    center = (sums[0, 0:1] * (1.0 / (ROOTED * TILE))).astype(bf16)
-    shift = center.astype(f32)
-
-    def fill(s):
-        pay[s, pl.ds(0, TILE)] = (first_split[s] - shift).astype(bf16)
-        pay[s, pl.ds(TILE, CENTER_ROWS)] = jnp.broadcast_to(center, (CENTER_ROWS, F))
-
-    def send(q):
-        chosen = jnp.maximum(table[SEL_AT + q] - 1, 0)
-        return pltpu.make_async_copy(pay.at[chosen], out.at[q], sems.at[q])
-
-    loop(SPLIT, fill)
-    loop(GROUP, lambda q: send(q).start())
-    loop(GROUP, lambda q: send(q).wait())
+    center = (s1 * (1.0 / (ROOTED * TILE))).astype(bf16)
+    less = center.astype(f32)
+    for s in range(SPLIT):
+        parts[s, pl.ds(0, TILE)] = (first_split[s] - less).astype(bf16)
+        parts[s, pl.ds(TILE, CENTER_ROWS)] = jnp.broadcast_to(center, (CENTER_ROWS, F))
+
+
+def again_kernel(column_sums, sums):
+    total = jnp.sum(column_sums[...], axis=0)
+
+    def fill(q):
+        sums[q] = total
+
+    loop(PLANE_SIZE, fill)
+
+
+def pass_kernel(table, mine, one, two, three, ahead_one, ahead_two, ahead_three):
+    for i, out in enumerate((ahead_one, ahead_two, ahead_three)):
+        for j, parts in enumerate((mine, one, two, three)):
+            out[j] = parts[table[PASS_AT + i * SIDE + j]]
 
 
 def hidden_kernel(
-    count, table, sums, scale, shift, first_own, first_split, incoming, tiles,
-    out, view, tbuf, obuf, tsem, osem,
+    count, table, sums, scale, shift, first_own, first_split, *refs
 ):
+    received, (tiles, out, view, raw, tbuf, obuf, rsem, tsem, osem) = refs[:6], refs[6:]
+
+    def take(h):
+        for i, parts in enumerate(received):
+
+            @pl.when(table[SOURCE_AT + h] == i)
+            def _():
+                pltpu.make_async_copy(
+                    parts.at[table[WITHIN_AT + h]], raw.at[h], rsem.at[h]
+                ).start()
+
+    loop(HOST, take)
     load_tiles(tiles, tbuf, tsem, ROOTED, HOST)
-    mean = sums[0:1] * (1.0 / count)
-    var = sums[1:2] * (1.0 / count) - mean * mean
+    total = jnp.sum(sums[...], axis=0)
+    mean = total[0:1] * (1.0 / count)
+    var = total[1:2] * (1.0 / count) - mean * mean
     inv = lax.rsqrt(var + 1e-5)
 
     def norm(first, less):
         return jax.nn.relu((first - less) * inv * scale[...] + shift[...]).astype(bf16)
 
-    def own(b, carry):
+    def own(b):
         view[b] = norm(first_own[b], mean)
-        return carry
-
-    def split(s, carry):
+
+    def split(s):
         view[OWN + s] = norm(first_split[s], mean)
-        return carry
-
-    def hosted(h, carry):
-        q = table[ROOTS_AT + h]
-        centered = incoming[q, pl.ds(0, TILE)].astype(f32)
-        center = incoming[q, pl.ds(TILE, CENTER_ROWS)].astype(f32)[0:1]
+
+    def hosted(h):
+        pltpu.make_async_copy(received[0].at[0], raw.at[h], rsem.at[h]).wait()
+        centered = raw[h, pl.ds(0, TILE)].astype(f32)
+        center = raw[h, pl.ds(TILE, CENTER_ROWS)].astype(f32)[0:1]
         view[ROOTED + h] = norm(centered, mean - center)
-        return carry
-
-    lax.fori_loop(0, OWN, own, 0)
-    lax.fori_loop(0, SPLIT, split, 0)
-    lax.fori_loop(0, HOST, hosted, 0)
+
+    loop(OWN, own)
+    loop(SPLIT, split)
+    loop(HOST, hosted)
     view[SLOTS] = jnp.zeros((TILE, F), bf16)
     replica_rows(table, tiles, out, view, tbuf, obuf, tsem, osem)
 
@@ -285,7 +320,7 @@
 MAC = 2 * TILE * TILE * F
 
 
-def per_device(
+def layers(
     features, tile_values, tile_columns, tile_present, host_root, host_block,
     self_one, neigh_one, scale_one, shift_one, self_two, neigh_two,
 ):
@@ -304,7 +339,7 @@
         return lax.all_to_all(blocks, axes, split_axis=0, concat_axis=0, tiled=True)
 
     outgoing, sel = call(
-        outgoing_kernel, "outgoing", 0, 2 << 20, room=60 << 20,
+        outgoing_kernel, 0, 2 << 20, room=60 << 20,
         out_shape=(wire, pltpu.SMEM((GROUP,), jnp.int32)),
         in_specs=[HBM] * 3,
         out_specs=(HBM, SMEM),
@@ -318,18 +353,18 @@
     incoming = exchange(outgoing)
 
     table, view = call(
-        tables_kernel, "tables", 0, 8 << 20,
+        tables_kernel, 0, 8 << 20,
         out_shape=(
-            pltpu.SMEM((SEL_AT + GROUP,), jnp.int32),
+            pltpu.SMEM((ENTRIES,), jnp.int32),
             view_v,
         ),
-        in_specs=[SMEM] * 4 + [HBM],
+        in_specs=[SMEM] * 5 + [HBM],
         out_specs=(SMEM, VMEM),
         scratch_shapes=[DMA],
-    )(host_root, tile_columns, tile_present, sel, rows)
+    )(host_root, host_block, tile_columns, tile_present, sel, rows)
 
     outgoing, view = call(
-        replica_kernel, "replicas", 64 * MAC, 4 << 20,
+        replica_kernel, 64 * MAC, 4 << 20,
         out_shape=(wire, view_v),
         in_specs=[SMEM] + [VMEM] * 2 + [HBM],
         out_specs=(HBM, VMEM),
@@ -339,43 +374,56 @@
     returned = exchange(outgoing)
 
     first_own, self_split, part_split, own_sums = call(
-        own_kernel, "own_rows", 60 * MAC, 5 << 20,
+        own_kernel, 60 * MAC, 5 << 20,
         out_shape=(pltpu.VMEM((OWN, TILE, F), f32), split_f32, split_f32, pltpu.VMEM((2, F), f32)),
         in_specs=[SMEM, VMEM, HBM, VMEM, VMEM],
         out_specs=(VMEM,) * 4,
         scratch_shapes=[tile_rows(ROOTED), DMA((ROOTED,))],
     )(table, view, tile_values, self_one, neigh_one)
 
-    first_split, sums = call(
-        split_kernel, "split_rows", 4 * MAC, 3 << 20,
-        out_shape=(split_f32, pltpu.VMEM((GROUP, 2, F), f32)),
+    parts_v = pltpu.VMEM((SPLIT, PART, F), bf16)
+    row_v = pltpu.VMEM((SIDE, PART, F), bf16)
+
+    first_split, sums, parts = call(
+        split_kernel, 4 * MAC, 3 << 20,
+        out_shape=(split_f32, pltpu.VMEM((GROUP, 2, F), f32), parts_v),
         in_specs=[SMEM] + [VMEM] * 5,
-        out_specs=(VMEM, VMEM),
+        out_specs=(VMEM,) * 3,
         scratch_shapes=[pltpu.VMEM((SPLIT, TILE, F), f32)],
     )(table, returned, part_split, self_split, own_sums, neigh_one)
-    column_sums = exchange(sums, COLUMN)
-    outgoing = call(
-        centered_kernel, "centered", 0, 2 << 20,
-        out_shape=pltpu.HBM((GROUP, TILE + CENTER_ROWS, F), bf16),
-        in_specs=[SMEM] + [VMEM] * 2,
-        out_specs=HBM,
-        scratch_shapes=[pltpu.VMEM((SPLIT, TILE + CENTER_ROWS, F), bf16), DMA((GROUP,))],
-    )(table, first_split, sums)
-    outgoing, column_sums = lax.optimization_barrier((outgoing, column_sums))
-    incoming = exchange(outgoing)
-    sums = lax.psum(lax.psum(jnp.sum(column_sums, axis=0), "gx"), "gz_0")
+    sums = exchange(sums, COLUMN)
+    column = []
+    for d in range(1, SIDE):
+        column.append(lax.ppermute(parts, "gz_1", [(i, (i + d) % SIDE) for i in range(SIDE)]))
+    sums = call(
+        again_kernel, 0, 1 << 17,
+        out_shape=pltpu.VMEM((PLANE_SIZE, 2, F), f32),
+        in_specs=[VMEM],
+        out_specs=VMEM,
+    )(sums)
+    sums = exchange(sums, PLANE)
+    ahead = call(
+        pass_kernel, 0, 2 << 20,
+        out_shape=(row_v,) * 3,
+        in_specs=[SMEM] + [VMEM] * 4,
+        out_specs=(VMEM,) * 3,
+    )(table, parts, *column)
+    row = []
+    for d in range(1, SIDE):
+        row.append(lax.ppermute(ahead[d - 1], "gz_0", [(i, (i + d) % SIDE) for i in range(SIDE)]))
 
     outgoing, view = call(
-        functools.partial(hidden_kernel, count), "hidden_replicas", 64 * MAC, 5 << 20,
+        functools.partial(hidden_kernel, count), 64 * MAC, 5 << 20,
         out_shape=(wire, view_v),
-        in_specs=[SMEM] + [VMEM] * 6 + [HBM],
+        in_specs=[SMEM] + [VMEM] * 11 + [HBM],
         out_specs=(HBM, VMEM),
-        scratch_shapes=[tile_rows(HOST), row_buffer, DMA((HOST,)), DMA((HOST,))],
-    )(table, sums, scale, shift, first_own, first_split, incoming, tile_values)
+        scratch_shapes=[pltpu.VMEM((HOST, PART, F), bf16), tile_rows(HOST), row_buffer]
+        + [DMA((HOST,))] * 3,
+    )(table, sums, scale, shift, first_own, first_split, *column, *row, tile_values)
     returned = exchange(outgoing)
 
     begun, self_split, part_split = call(
-        own_two_kernel, "own_rows_two", 60 * MAC, 5 << 20,
+        own_two_kernel, 60 * MAC, 5 << 20,
         out_shape=(shape((ROOTED, TILE, F), bf16), split_f32, split_f32),
         in_specs=[SMEM, VMEM, HBM, VMEM, VMEM],
         out_specs=(VMEM,) * 3,
@@ -383,7 +431,7 @@
     )(table, view, tile_values, self_two, neigh_two)
 
     embedding = call(
-        last_kernel, "split_rows_two", 4 * MAC, 3 << 20,
+        last_kernel, 4 * MAC, 3 << 20,
         out_shape=shape((ROOTED, TILE, F), bf16),
         in_specs=[SMEM] + [VMEM] * 4 + [ANY],
         out_specs=ANY,
@@ -398,7 +446,7 @@
         mesh.devices.reshape(mesh.shape["gx"], 2, 2, 4, 4), ("gx", "gy_0", "gy_1", "gz_0", "gz_1")
     )
     return jax.shard_map(
-        per_device,
+        layers,
         mesh=finer,
         in_specs=(
             P(GX_GY_GZ, None),

time: 168 us -> 179 us (1.065)
  the two profiles are of different devices: /device:TPU:16 before, /device:TPU:8 now
where the time goes in v4:
time: 179 us; the launch traced here: 178 us
  waiting for transfers between devices  75.3 us (42%)
  starting transfers between devices  46 us (26%)
  blocking collectives  29.8 us (17%)
  Pallas kernels  22.5 us (13%)
  local copies, waits for them, and re-layouts  3.88 us (2%)
    all_to_all x3, waiting for transfers between devices, exchange(): return lax.all_to_all(blocks, axes, split_axis=0, concat_axis=0, tiled=True)  65 us
    all_to_all x2, blocking collectives, exchange(): return lax.all_to_all(blocks, axes, split_axis=0, concat_axis=0, tiled=True)  29.8 us
    all_to_all x3, starting transfers between devices, exchange(): return lax.all_to_all(blocks, axes, split_axis=0, concat_axis=0, tiled=True)  23.7 us
    ppermute x3, starting transfers between devices, layers(): lax.ppermute(parts, 'gz_1', [(i, (i + d) % SIDE) for i in range(SIDE)])  13.3 us
    ppermute x3, waiting for transfers between devices, layers(): lax.ppermute(parts, 'gz_1', [(i, (i + d) % SIDE) for i in range(SIDE)])  10.4 us
    ppermute x3, starting transfers between devices, layers(): lax.ppermute(ahead[d - 1], 'gz_0', [(i, (i + d) % SIDE) for i in range(SI...  8.97 us
    pallas_call x1, Pallas kernels, layers(): call(functools.partial(hidden_kernel, count), 64 * MAC, 5 << 20, out_shap...  5.03 us
    pallas_call x1, Pallas kernels, layers(): call(replica_kernel, 64 * MAC, 4 << 20, out_shape=(wire, view_v), in_spec...  4.55 us
  transfers between devices with their start and end apart: 9, of which 5 were waited for; matrix products, arithmetic and copies ran while one was open for 1% of the time, Pallas kernels for 5%

profile of v4, /device:TPU:8, one launch (start us, length us, event | category | flops | bytes accessed | tf_op | source)
XLA Modules:
  0.0 177.8 jit_solution(17740146270272291779)
XLA Ops:
  0.0 2.1 %shard_map.118 = (bf16[16,128,256]{2,1,0:T(8,128)(2,1)}, s32[16]{0:T(128)S(4)}) custom-call(s32[128]{0:T(128)} %root.3, s32[128]{0:T(128)} %block.3, bf16[6,128,256]{2,1,0:T(8,128)(2,1)} %bitcast.4), custom_call_target="tpu_custom_call" | custom-call | bytes 2097152 | tf_op jit(solution)/shard_map/pallas_call | solution.py:341
  2.1 12.9 %all-to-all-start = ((bf16[16,128,256]{2,1,0:T(8,128)(2,1)}), bf16[16,128,256]{2,1,0:T(8,128)(2,1)S(1)}, u32[]{:S(2)}, u32[]{:S(2)}) async-start(bf16[16,128,256]{2,1,0:T(8,128)(2,1)} %get-tuple-element.29), calls=%async_computation | async-start | bytes 2097152 | tf_op jit(solution)/shard_map/all_to_all | solution.py:339
  15.0 0.8 copy.15.cols
  15.8 0.8 copy.16.present
  16.5 1.0 copy-done
  17.5 0.7 copy-done.5
  18.2 0.7 copy-done.6
  18.8 1.6 shard_map.119
  20.5 18.7 %all-to-all-done.incoming = bf16[16,128,256]{2,1,0:T(8,128)(2,1)S(1)} async-done(((bf16[16,128,256]{2,1,0:T(8,128)(2,1)}), bf16[16,128,256]{2,1,0:T(8,128)(2,1)S(1)}, u32[]{:S(2)}, u32[]{:S(2)}) %all-to-all-start) | async-done | bytes 1048608 | tf_op jit(solution)/shard_map/all_to_all | solution.py:339
  39.2 4.5 %shard_map.120 = (bf16[16,128,256]{2,1,0:T(8,128)(2,1)}, bf16[15,128,256]{2,1,0:T(8,128)(2,1)S(1)}) custom-call(s32[164]{0:T(256)S(4)} %get-tuple-element.27.table, bf16[15,128,256]{2,1,0:T(8,128)(2,1)S(1)} %get-tuple-element.28.begun, bf16[16,128,256]{2,1,0:T(8,128)(2,1)S(1)} %all-to-all-done.incoming, ...), custom_call_target="tpu_custom_call", output_to_operand_aliasing={{1}: (1, {})} | custom-call | flops 536870912 | bytes 4194304 | tf_op jit(solution)/shard_map/pallas_call | solution.py:366
  43.8 7.2 %all-to-all-start.1 = ((bf16[16,128,256]{2,1,0:T(8,128)(2,1)}), bf16[16,128,256]{2,1,0:T(8,128)(2,1)S(1)}, u32[]{:S(2)}, u32[]{:S(2)}) async-start(bf16[16,128,256]{2,1,0:T(8,128)(2,1)} %get-tuple-element.30), calls=%async_computation.1 | async-start | bytes 2097152 | tf_op jit(solution)/shard_map/all_to_all | solution.py:339
  51.0 3.3 %shard_map.121 = (f32[4,128,256]{2,1,0:T(8,128)S(1)}, f32[2,128,256]{2,1,0:T(8,128)S(1)}, f32[2,128,256]{2,1,0:T(8,128)S(1)}, f32[2,256]{1,0:T(2,128)S(1)}) custom-call(s32[164]{0:T(256)S(4)} %get-tuple-element.27.table, bf16[15,128,256]{2,1,0:T(8,128)(2,1)S(1)} %get-tuple-element.31.view, bf16[14,8,128,128]{3,2,1,0:T(8,128)(2,1)} %tiles.5, ...), custom_call_target="tpu_custom_call" | custom-call | flops 503316480 | bytes 5242880 | tf_op jit(solution)/shard_map/pallas_call | solution.py:376
  54.3 21.3 %all-to-all-done.1.incoming = bf16[16,128,256]{2,1,0:T(8,128)(2,1)S(1)} async-done(((bf16[16,128,256]{2,1,0:T(8,128)(2,1)}), bf16[16,128,256]{2,1,0:T(8,128)(2,1)S(1)}, u32[]{:S(2)}, u32[]{:S(2)}) %all-to-all-start.1) | async-done | bytes 1048608 | tf_op jit(solution)/shard_map/all_to_all | solution.py:339
  75.6 0.6 shard_map.122
  76.3 2.7 %collective-permute-start.2 = (bf16[2,144,256]{2,1,0:T(8,128)(2,1)S(1)}, bf16[2,144,256]{2,1,0:T(8,128)(2,1)S(1)}, u32[]{:S(2)}, u32[]{:S(2)}) collective-permute-start(bf16[2,144,256]{2,1,0:T(8,128)(2,1)S(1)} %get-tuple-element.38.mine), channel_id=1, source_target_pairs={{0,3},{1,0},{2,1},{3,2},{4,7},{5,4},{6,5},{7,6},{8,11},{9,8},{10,9... | collective-permute-start | bytes 442376 | tf_op jit(solution)/shard_map/ppermute | solution.py:397
  79.0 8.6 %collective-permute-start.1 = (bf16[2,144,256]{2,1,0:T(8,128)(2,1)S(1)}, bf16[2,144,256]{2,1,0:T(8,128)(2,1)S(1)}, u32[]{:S(2)}, u32[]{:S(2)}) collective-permute-start(bf16[2,144,256]{2,1,0:T(8,128)(2,1)S(1)} %get-tuple-element.38.mine), channel_id=1, source_target_pairs={{0,2},{1,3},{2,0},{3,1},{4,6},{5,7},{6,4},{7,5},{8,10},{9,11},{10,... | collective-permute-start | bytes 442376 | tf_op jit(solution)/shard_map/ppermute | solution.py:397
  87.6 1.9 %collective-permute-start = (bf16[2,144,256]{2,1,0:T(8,128)(2,1)S(1)}, bf16[2,144,256]{2,1,0:T(8,128)(2,1)S(1)}, u32[]{:S(2)}, u32[]{:S(2)}) collective-permute-start(bf16[2,144,256]{2,1,0:T(8,128)(2,1)S(1)} %get-tuple-element.38.mine), channel_id=1, source_target_pairs={{0,1},{1,2},{2,3},{3,0},{4,5},{5,6},{6,7},{7,4},{8,9},{9,10},{10,1... | collective-permute-start | bytes 442376 | tf_op jit(solution)/shard_map/ppermute | solution.py:397
  89.5 4.8 %collective-permute-done.1.two.refs_1_ = bf16[2,144,256]{2,1,0:T(8,128)(2,1)S(1)} collective-permute-done((bf16[2,144,256]{2,1,0:T(8,128)(2,1)S(1)}, bf16[2,144,256]{2,1,0:T(8,128)(2,1)S(1)}, u32[]{:S(2)}, u32[]{:S(2)}) %collective-permute-start.1) | collective-permute-done | bytes 147488 | tf_op jit(solution)/shard_map/ppermute | solution.py:397
  94.4 5.5 %collective-permute-done.one.refs_0_ = bf16[2,144,256]{2,1,0:T(8,128)(2,1)S(1)} collective-permute-done((bf16[2,144,256]{2,1,0:T(8,128)(2,1)S(1)}, bf16[2,144,256]{2,1,0:T(8,128)(2,1)S(1)}, u32[]{:S(2)}, u32[]{:S(2)}) %collective-permute-start) | collective-permute-done | bytes 147488 | tf_op jit(solution)/shard_map/ppermute | solution.py:397
  99.9 0.1 shard_map.124
  100.0 1.9 %collective-permute-start.3 = (bf16[4,144,256]{2,1,0:T(8,128)(2,1)S(1)}, bf16[4,144,256]{2,1,0:T(8,128)(2,1)S(1)}, u32[]{:S(2)}, u32[]{:S(2)}) collective-permute-start(bf16[4,144,256]{2,1,0:T(8,128)(2,1)S(1)} %get-tuple-element.39), channel_id=1, source_target_pairs={{0,4},{4,8},{8,12},{12,0},{1,5},{5,9},{9,13},{13,1},{2,6},{6,10},{... | collective-permute-start | bytes 884744 | tf_op jit(solution)/shard_map/ppermute | solution.py:413
  101.9 1.9 %collective-permute-start.4 = (bf16[4,144,256]{2,1,0:T(8,128)(2,1)S(1)}, bf16[4,144,256]{2,1,0:T(8,128)(2,1)S(1)}, u32[]{:S(2)}, u32[]{:S(2)}) collective-permute-start(bf16[4,144,256]{2,1,0:T(8,128)(2,1)S(1)} %get-tuple-element.40), channel_id=1, source_target_pairs={{0,8},{4,12},{8,0},{12,4},{1,9},{5,13},{9,1},{13,5},{2,10},{6,14},... | collective-permute-start | bytes 884744 | tf_op jit(solution)/shard_map/ppermute | solution.py:413
  103.8 5.1 %collective-permute-start.5 = (bf16[4,144,256]{2,1,0:T(8,128)(2,1)S(1)}, bf16[4,144,256]{2,1,0:T(8,128)(2,1)S(1)}, u32[]{:S(2)}, u32[]{:S(2)}) collective-permute-start(bf16[4,144,256]{2,1,0:T(8,128)(2,1)S(1)} %get-tuple-element.41), channel_id=1, source_target_pairs={{0,12},{4,0},{8,4},{12,8},{1,13},{5,1},{9,5},{13,9},{2,14},{6,2},{... | collective-permute-start | bytes 884744 | tf_op jit(solution)/shard_map/ppermute | solution.py:413
  109.0 12.1 %all_to_all.25.column_sums = f32[16,2,256]{2,1,0:T(2,128)S(1)} all-to-all(f32[16,2,256]{2,1,0:T(2,128)S(1)} %get-tuple-element.35), channel_id=1, replica_groups=mesh['gx'=8,'gy_0'=2,'gy_1'=2,'gz_0'=4,'gz_1'=4] {'gy_0','gy_1','gz_1'}, dimensions={0} | all-to-all | bytes 65536 | tf_op jit(solution)/shard_map/all_to_all | solution.py:339
  121.0 0.2 shard_map.123
  121.2 17.8 %all_to_all.26.sums = f32[32,2,256]{2,1,0:T(2,128)S(1)} all-to-all(f32[32,2,256]{2,1,0:T(2,128)S(1)} %shard_map.123), channel_id=1, replica_groups=mesh['gx'=8,'gy_0'=2,'gy_1'=2,'gz_0'=4,'gz_1'=4] {'gx','gz_0'}, dimensions={0} | all-to-all | bytes 131072 | tf_op jit(solution)/shard_map/all_to_all | solution.py:339
  139.0 0.0 copy-start.2
  139.0 5.0 %shard_map.125 = (bf16[16,128,256]{2,1,0:T(8,128)(2,1)}, bf16[15,128,256]{2,1,0:T(8,128)(2,1)S(1)}) custom-call(s32[164]{0:T(256)S(4)} %get-tuple-element.27.table, f32[32,2,256]{2,1,0:T(2,128)S(1)} %all_to_all.26.sums, f32[1,256]{1,0:T(1,128)S(1)} %bitcast.6, f32[1,256]{1,0:T(1,128)S(1)} %bitcast.7, f32[4,128,256]{2,1,0:T(8,128)S(1)} %get-tuple-element.36.first_own, ...), custom_call_target="tpu_custom_call" | custom-call | flops 536870912 | bytes 5242880 | tf_op jit(solution)/shard_map/pallas_call | solution.py:415
  144.1 3.7 %all-to-all-start.4 = ((bf16[16,128,256]{2,1,0:T(8,128)(2,1)}), bf16[16,128,256]{2,1,0:T(8,128)(2,1)S(1)}, u32[]{:S(2)}, u32[]{:S(2)}) async-start(bf16[16,128,256]{2,1,0:T(8,128)(2,1)} %get-tuple-element.42), calls=%async_computation.4 | async-start | bytes 2097152 | tf_op jit(solution)/shard_map/all_to_all | solution.py:339
  147.8 3.8 %shard_map.126 = (bf16[6,128,256]{2,1,0:T(8,128)(2,1)}, f32[2,128,256]{2,1,0:T(8,128)S(1)}, f32[2,128,256]{2,1,0:T(8,128)S(1)}) custom-call(s32[164]{0:T(256)S(4)} %get-tuple-element.27.table, bf16[15,128,256]{2,1,0:T(8,128)(2,1)S(1)} %get-tuple-element.43.view, bf16[14,8,128,128]{3,2,1,0:T(8,128)(2,1)} %tiles.5, bf16[256,256]{1,0:T(8,128)(2,1)S(1)} %copy-done.4, ...), custom_call_target="tpu_custom_call" | custom-call | flops 503316480 | bytes 5242880 | tf_op jit(solution)/shard_map/pallas_call | solution.py:425
  151.6 24.9 %all-to-all-done.4.incoming = bf16[16,128,256]{2,1,0:T(8,128)(2,1)S(1)} async-done(((bf16[16,128,256]{2,1,0:T(8,128)(2,1)}), bf16[16,128,256]{2,1,0:T(8,128)(2,1)S(1)}, u32[]{:S(2)}, u32[]{:S(2)}) %all-to-all-start.4) | async-done | bytes 1048608 | tf_op jit(solution)/shard_map/all_to_all | solution.py:339
  176.6 1.2 shard_map.127
  (18 shorter events, 0.0 us)
Async XLA Ops:
  2.1 37.1 %all-to-all-start = ((bf16[16,128,256]{2,1,0:T(8,128)(2,1)}), bf16[16,128,256]{2,1,0:T(8,128)(2,1)S(1)}, u32[]{:S(2)}, u32[]{:S(2)}) async-start(bf16[16,128,256]{2,1,0:T(8,128)(2,1)} %get-tuple-element.29), calls=%async_computation | async-start | bytes 2097152 | tf_op jit(solution)/shard_map/all_to_all | solution.py:339
  16.5 1.0 copy-start
  17.5 0.7 copy-start.5
  18.2 0.7 copy-start.6
  39.2 11.8 %copy-start.1 = (bf16[256,256]{1,0:T(8,128)(2,1)S(1)}, bf16[256,256]{1,0:T(8,128)(2,1)}, u32[]{:S(2)}) copy-start(bf16[256,256]{1,0:T(8,128)(2,1)} %w_neigh.5) | copy-start | bytes 393220
  39.2 11.8 %copy-start.3 = (bf16[256,256]{1,0:T(8,128)(2,1)S(1)}, bf16[256,256]{1,0:T(8,128)(2,1)}, u32[]{:S(2)}) copy-start(bf16[256,256]{1,0:T(8,128)(2,1)} %w_self.2) | copy-start | bytes 393220
  43.8 31.9 %all-to-all-start.1 = ((bf16[16,128,256]{2,1,0:T(8,128)(2,1)}), bf16[16,128,256]{2,1,0:T(8,128)(2,1)S(1)}, u32[]{:S(2)}, u32[]{:S(2)}) async-start(bf16[16,128,256]{2,1,0:T(8,128)(2,1)} %get-tuple-element.30), calls=%async_computation.1 | async-start | bytes 2097152 | tf_op jit(solution)/shard_map/all_to_all | solution.py:339
  51.0 88.0 %copy-start.7 = (f32[256]{0:T(256)S(1)}, f32[256]{0:T(256)}, u32[]{:S(2)}) copy-start(f32[256]{0:T(256)} %param.20) | copy-start | bytes 3076
  51.0 88.0 %copy-start.8 = (f32[256]{0:T(256)S(1)}, f32[256]{0:T(256)}, u32[]{:S(2)}) copy-start(f32[256]{0:T(256)} %param.21) | copy-start | bytes 3076
  76.3 13.3 %collective-permute-start.2 = (bf16[2,144,256]{2,1,0:T(8,128)(2,1)S(1)}, bf16[2,144,256]{2,1,0:T(8,128)(2,1)S(1)}, u32[]{:S(2)}, u32[]{:S(2)}) collective-permute-start(bf16[2,144,256]{2,1,0:T(8,128)(2,1)S(1)} %get-tuple-element.38.mine), channel_id=1, source_target_pairs={{0,3},{1,0},{2,1},{3,2},{4,7},{5,4},{6,5},{7,6},{8,11},{9,8},{10,9... | collective-permute-start | bytes 442376 | tf_op jit(solution)/shard_map/ppermute | solution.py:397
  79.0 15.4 %collective-permute-start.1 = (bf16[2,144,256]{2,1,0:T(8,128)(2,1)S(1)}, bf16[2,144,256]{2,1,0:T(8,128)(2,1)S(1)}, u32[]{:S(2)}, u32[]{:S(2)}) collective-permute-start(bf16[2,144,256]{2,1,0:T(8,128)(2,1)S(1)} %get-tuple-element.38.mine), channel_id=1, source_target_pairs={{0,2},{1,3},{2,0},{3,1},{4,6},{5,7},{6,4},{7,5},{8,10},{9,11},{10,... | collective-permute-start | bytes 442376 | tf_op jit(solution)/shard_map/ppermute | solution.py:397
  87.6 12.3 %collective-permute-start = (bf16[2,144,256]{2,1,0:T(8,128)(2,1)S(1)}, bf16[2,144,256]{2,1,0:T(8,128)(2,1)S(1)}, u32[]{:S(2)}, u32[]{:S(2)}) collective-permute-start(bf16[2,144,256]{2,1,0:T(8,128)(2,1)S(1)} %get-tuple-element.38.mine), channel_id=1, source_target_pairs={{0,1},{1,2},{2,3},{3,0},{4,5},{5,6},{6,7},{7,4},{8,9},{9,10},{10,1... | collective-permute-start | bytes 442376 | tf_op jit(solution)/shard_map/ppermute | solution.py:397
  100.0 39.0 %collective-permute-start.3 = (bf16[4,144,256]{2,1,0:T(8,128)(2,1)S(1)}, bf16[4,144,256]{2,1,0:T(8,128)(2,1)S(1)}, u32[]{:S(2)}, u32[]{:S(2)}) collective-permute-start(bf16[4,144,256]{2,1,0:T(8,128)(2,1)S(1)} %get-tuple-element.39), channel_id=1, source_target_pairs={{0,4},{4,8},{8,12},{12,0},{1,5},{5,9},{9,13},{13,1},{2,6},{6,10},{... | collective-permute-start | bytes 884744 | tf_op jit(solution)/shard_map/ppermute | solution.py:413
  101.9 37.1 %collective-permute-start.4 = (bf16[4,144,256]{2,1,0:T(8,128)(2,1)S(1)}, bf16[4,144,256]{2,1,0:T(8,128)(2,1)S(1)}, u32[]{:S(2)}, u32[]{:S(2)}) collective-permute-start(bf16[4,144,256]{2,1,0:T(8,128)(2,1)S(1)} %get-tuple-element.40), channel_id=1, source_target_pairs={{0,8},{4,12},{8,0},{12,4},{1,9},{5,13},{9,1},{13,5},{2,10},{6,14},... | collective-permute-start | bytes 884744 | tf_op jit(solution)/shard_map/ppermute | solution.py:413
  103.8 35.2 %collective-permute-start.5 = (bf16[4,144,256]{2,1,0:T(8,128)(2,1)S(1)}, bf16[4,144,256]{2,1,0:T(8,128)(2,1)S(1)}, u32[]{:S(2)}, u32[]{:S(2)}) collective-permute-start(bf16[4,144,256]{2,1,0:T(8,128)(2,1)S(1)} %get-tuple-element.41), channel_id=1, source_target_pairs={{0,12},{4,0},{8,4},{12,8},{1,13},{5,1},{9,5},{13,9},{2,14},{6,2},{... | collective-permute-start | bytes 884744 | tf_op jit(solution)/shard_map/ppermute | solution.py:413
  139.0 8.7 %copy-start.2 = (bf16[256,256]{1,0:T(8,128)(2,1)S(1)}, bf16[256,256]{1,0:T(8,128)(2,1)}, u32[]{:S(2)}) copy-start(bf16[256,256]{1,0:T(8,128)(2,1)} %w_neigh.7) | copy-start | bytes 393220
  139.0 8.7 %copy-start.4 = (bf16[256,256]{1,0:T(8,128)(2,1)S(1)}, bf16[256,256]{1,0:T(8,128)(2,1)}, u32[]{:S(2)}) copy-start(bf16[256,256]{1,0:T(8,128)(2,1)} %w_self.3) | copy-start | bytes 393220
  144.1 32.5 %all-to-all-start.4 = ((bf16[16,128,256]{2,1,0:T(8,128)(2,1)}), bf16[16,128,256]{2,1,0:T(8,128)(2,1)S(1)}, u32[]{:S(2)}, u32[]{:S(2)}) async-start(bf16[16,128,256]{2,1,0:T(8,128)(2,1)} %get-tuple-element.42), calls=%async_computation.4 | async-start | bytes 2097152 | tf_op jit(solution)/shard_map/all_to_all | solution.py:339

commit v5 on v3

--- a/solution.py
+++ b/solution.py
@@ -22,9 +22,13 @@
 GZ = ("gz_0", "gz_1")
 GX_GY_GZ = ("gx", "gy_0", "gy_1", "gz_0", "gz_1")
 GX_GY = ("gx", "gy_0", "gy_1")
-COLUMN = ("gy_0", "gy_1", "gz_1")
+PLANE = ("gx", "gz_0")
+PLANE_SIZE = 32
 ROOTS_AT = 112
 SEL_AT = 120
+PASS_AT = 136
+ENTRIES = 152
+SIDE = 4
 
 f32 = jnp.float32
 bf16 = jnp.bfloat16
@@ -40,10 +44,9 @@
     return jax.ShapeDtypeStruct(dims, dtype)
 
 
-def call(body, name, flops, size, room=VMEM_BYTES, **kw):
+def call(body, flops, size, room=VMEM_BYTES, **kw):
     return pl.pallas_call(
         body,
-        name=name,
         compiler_params=pltpu.CompilerParams(vmem_limit_bytes=room),
         cost_estimate=pl.CostEstimate(flops=flops, bytes_accessed=size, transcendentals=0),
         **kw,
@@ -88,16 +91,26 @@
     loop(GROUP, lambda q: send(q, 0).wait())
 
 
-def tables_kernel(root, cols, present, sel, rows, table, view, sem):
+def tables_kernel(root, block, cols, present, sel, rows, table, view, sem):
     load_rows = pltpu.make_async_copy(rows, view.at[pl.ds(0, ROOTED)], sem)
     load_rows.start()
     mine = my_place()
+    my_x, my_z = lax.axis_index("gz_0"), lax.axis_index("gz_1")
+
+    def passed_on(i):
+        target, source = (i // SIDE) * SIDE + my_z, my_x * SIDE + (i & (SIDE - 1))
+        chosen = jnp.int32(0)
+        for j in range(HOST):
+            at = target * HOST + j
+            chosen = jnp.where(root[at] == source, block[at], chosen)
+        table[PASS_AT + i] = chosen
 
     def slots(b):
         for k in range(K):
             table[b * K + k] = jnp.where(present[b, k] > 0, cols[b, k], SLOTS)
 
     loop(SLOTS, slots)
+    loop(GROUP, passed_on)
     for h in range(HOST):
         table[ROOTS_AT + h] = root[mine * HOST + h]
     for q in range(GROUP):
@@ -186,7 +199,7 @@
     loop(GROUP, add)
 
 
-def split_kernel(table, incoming, part_split, self_split, own_sums, w_neigh, first_split, sums, total):
+def split_kernel(table, incoming, part_split, self_split, own_sums, w_neigh, first_split, sums, parts, total):
     total[...] = part_split[...]
     add_replicas(table, incoming, total)
     s1, s2 = own_sums[0:1], own_sums[1:2]
@@ -200,24 +213,21 @@
         sums[q, 0:1] = s1
         sums[q, 1:2] = s2
 
-    loop(GROUP, fill)
-
-
-def centered_kernel(table, first_split, sums, out, pay, sems):
-    center = (sums[0, 0:1] * (1.0 / (ROOTED * TILE))).astype(bf16)
-    shift = center.astype(f32)
-
-    def fill(s):
-        pay[s, pl.ds(0, TILE)] = (first_split[s] - shift).astype(bf16)
-        pay[s, pl.ds(TILE, CENTER_ROWS)] = jnp.broadcast_to(center, (CENTER_ROWS, F))
-
-    def send(q):
-        chosen = jnp.maximum(table[SEL_AT + q] - 1, 0)
-        return pltpu.make_async_copy(pay.at[chosen], out.at[q], sems.at[q])
-
-    loop(SPLIT, fill)
-    loop(GROUP, lambda q: send(q).start())
-    loop(GROUP, lambda q: send(q).wait())
+    loop(PLANE_SIZE, fill)
+    center = (s1 * (1.0 / (ROOTED * TILE))).astype(bf16)
+    less = center.astype(f32)
+    for s in range(SPLIT):
+        parts[s, pl.ds(0, TILE)] = (first_split[s] - less).astype(bf16)
+        parts[s, pl.ds(TILE, CENTER_ROWS)] = jnp.broadcast_to(center, (CENTER_ROWS, F))
+
+
+def pass_kernel(table, column, out, sems):
+    def send(i):
+        chosen = (i & (SIDE - 1)) * SPLIT + table[PASS_AT + i]
+        return pltpu.make_async_copy(column.at[chosen], out.at[i], sems.at[i])
+
+    loop(GROUP, lambda i: send(i).start())
+    loop(GROUP, lambda i: send(i).wait())
 
 
 def hidden_kernel(
@@ -285,7 +295,7 @@
 MAC = 2 * TILE * TILE * F
 
 
-def per_device(
+def layers(
     features, tile_values, tile_columns, tile_present, host_root, host_block,
     self_one, neigh_one, scale_one, shift_one, self_two, neigh_two,
 ):
@@ -304,7 +314,7 @@
         return lax.all_to_all(blocks, axes, split_axis=0, concat_axis=0, tiled=True)
 
     outgoing, sel = call(
-        outgoing_kernel, "outgoing", 0, 2 << 20, room=60 << 20,
+        outgoing_kernel, 0, 2 << 20, room=60 << 20,
         out_shape=(wire, pltpu.SMEM((GROUP,), jnp.int32)),
         in_specs=[HBM] * 3,
         out_specs=(HBM, SMEM),
@@ -318,18 +328,18 @@
     incoming = exchange(outgoing)
 
     table, view = call(
-        tables_kernel, "tables", 0, 8 << 20,
+        tables_kernel, 0, 8 << 20,
         out_shape=(
-            pltpu.SMEM((SEL_AT + GROUP,), jnp.int32),
+            pltpu.SMEM((ENTRIES,), jnp.int32),
             view_v,
         ),
-        in_specs=[SMEM] * 4 + [HBM],
+        in_specs=[SMEM] * 5 + [HBM],
         out_specs=(SMEM, VMEM),
         scratch_shapes=[DMA],
-    )(host_root, tile_columns, tile_present, sel, rows)
+    )(host_root, host_block, tile_columns, tile_present, sel, rows)
 
     outgoing, view = call(
-        replica_kernel, "replicas", 64 * MAC, 4 << 20,
+        replica_kernel, 64 * MAC, 4 << 20,
         out_shape=(wire, view_v),
         in_specs=[SMEM] + [VMEM] * 2 + [HBM],
         out_specs=(HBM, VMEM),
@@ -339,34 +349,39 @@
     returned = exchange(outgoing)
 
     first_own, self_split, part_split, own_sums = call(
-        own_kernel, "own_rows", 60 * MAC, 5 << 20,
+        own_kernel, 60 * MAC, 5 << 20,
         out_shape=(pltpu.VMEM((OWN, TILE, F), f32), split_f32, split_f32, pltpu.VMEM((2, F), f32)),
         in_specs=[SMEM, VMEM, HBM, VMEM, VMEM],
         out_specs=(VMEM,) * 4,
         scratch_shapes=[tile_rows(ROOTED), DMA((ROOTED,))],
     )(table, view, tile_values, self_one, neigh_one)
 
-    first_split, sums = call(
-        split_kernel, "split_rows", 4 * MAC, 3 << 20,
-        out_shape=(split_f32, pltpu.VMEM((GROUP, 2, F), f32)),
+    first_split, sums, parts = call(
+        split_kernel, 4 * MAC, 3 << 20,
+        out_shape=(
+            split_f32,
+            pltpu.VMEM((PLANE_SIZE, 2, F), f32),
+            pltpu.VMEM((SPLIT, TILE + CENTER_ROWS, F), bf16),
+        ),
         in_specs=[SMEM] + [VMEM] * 5,
-        out_specs=(VMEM, VMEM),
+        out_specs=(VMEM,) * 3,
         scratch_shapes=[pltpu.VMEM((SPLIT, TILE, F), f32)],
     )(table, returned, part_split, self_split, own_sums, neigh_one)
-    column_sums = exchange(sums, COLUMN)
+    plane_sums = exchange(sums, PLANE)
+    column = lax.all_gather(parts, "gz_1", axis=0, tiled=True)
+    column, plane_sums = lax.optimization_barrier((column, plane_sums))
     outgoing = call(
-        centered_kernel, "centered", 0, 2 << 20,
+        pass_kernel, 0, 2 << 20,
         out_shape=pltpu.HBM((GROUP, TILE + CENTER_ROWS, F), bf16),
-        in_specs=[SMEM] + [VMEM] * 2,
+        in_specs=[SMEM, VMEM],
         out_specs=HBM,
-        scratch_shapes=[pltpu.VMEM((SPLIT, TILE + CENTER_ROWS, F), bf16), DMA((GROUP,))],
-    )(table, first_split, sums)
-    outgoing, column_sums = lax.optimization_barrier((outgoing, column_sums))
-    incoming = exchange(outgoing)
-    sums = lax.psum(lax.psum(jnp.sum(column_sums, axis=0), "gx"), "gz_0")
+        scratch_shapes=[DMA((GROUP,))],
+    )(table, column)
+    incoming = exchange(outgoing, "gz_0")
+    sums = lax.psum(lax.psum(jnp.sum(plane_sums, axis=0), ("gy_0", "gy_1")), "gz_1")
 
     outgoing, view = call(
-        functools.partial(hidden_kernel, count), "hidden_replicas", 64 * MAC, 5 << 20,
+        functools.partial(hidden_kernel, count), 64 * MAC, 5 << 20,
         out_shape=(wire, view_v),
         in_specs=[SMEM] + [VMEM] * 6 + [HBM],
         out_specs=(HBM, VMEM),
@@ -375,7 +390,7 @@
     returned = exchange(outgoing)
 
     begun, self_split, part_split = call(
-        own_two_kernel, "own_rows_two", 60 * MAC, 5 << 20,
+        own_two_kernel, 60 * MAC, 5 << 20,
         out_shape=(shape((ROOTED, TILE, F), bf16), split_f32, split_f32),
         in_specs=[SMEM, VMEM, HBM, VMEM, VMEM],
         out_specs=(VMEM,) * 3,
@@ -383,7 +398,7 @@
     )(table, view, tile_values, self_two, neigh_two)
 
     embedding = call(
-        last_kernel, "split_rows_two", 4 * MAC, 3 << 20,
+        last_kernel, 4 * MAC, 3 << 20,
         out_shape=shape((ROOTED, TILE, F), bf16),
         in_specs=[SMEM] + [VMEM] * 4 + [ANY],
         out_specs=ANY,
@@ -398,7 +413,7 @@
         mesh.devices.reshape(mesh.shape["gx"], 2, 2, 4, 4), ("gx", "gy_0", "gy_1", "gz_0", "gz_1")
     )
     return jax.shard_map(
-        per_device,
+        layers,
         mesh=finer,
         in_specs=(
             P(GX_GY_GZ, None),

time: 168 us -> 167 us (level)
  the two profiles are of different devices: /device:TPU:16 before, /device:TPU:64 now
where the time goes in v5:
time: 167 us
  waiting for transfers between devices  75.7 us (45%)
  starting transfers between devices  35.5 us (21%)
  blocking collectives  32.2 us (19%)
  Pallas kernels  22.8 us (14%)
    all_to_all x5, waiting for transfers between devices, exchange(): return lax.all_to_all(blocks, axes, split_axis=0, concat_axis=0, tiled=True)  75.7 us
    all_to_all x5, starting transfers between devices, exchange(): return lax.all_to_all(blocks, axes, split_axis=0, concat_axis=0, tiled=True)  35.5 us
    all_gather x1, blocking collectives, layers(): column = lax.all_gather(parts, 'gz_1', axis=0, tiled=True)  15.2 us
    psum x1, blocking collectives, layers(): lax.psum(lax.psum(jnp.sum(plane_sums, axis=0), ('gy_0', 'gy_1')), 'gz_1')  11.3 us
    psum x1, blocking collectives, layers(): lax.psum(jnp.sum(plane_sums, axis=0), ('gy_0', 'gy_1'))  5.67 us
    pallas_call x1, Pallas kernels, layers(): call(replica_kernel, 64 * MAC, 4 << 20, out_shape=(wire, view_v), in_spec...  4.44 us
    pallas_call x1, Pallas kernels, layers(): call(own_two_kernel, 60 * MAC, 5 << 20, out_shape=(shape((ROOTED, TILE, F...  3.83 us
    pallas_call x1, Pallas kernels, layers(): call(functools.partial(hidden_kernel, count), 64 * MAC, 5 << 20, out_shap...  3.72 us
  transfers between devices with their start and end apart: 5, of which 3 were waited for; matrix products, arithmetic and copies ran while one was open for 0% of the time, Pallas kernels for 5%

profile of v5, /device:TPU:64, one launch (start us, length us, event | category | flops | bytes accessed | tf_op | source)
XLA Modules:
  0.0 166.6 jit_solution(3605850675237669220)
XLA Ops:
  0.0 0.0 copy-start.5
  0.0 0.0 copy-start.6
  0.0 2.1 %shard_map.118 = (bf16[16,128,256]{2,1,0:T(8,128)(2,1)}, s32[16]{0:T(128)S(4)}) custom-call(s32[128]{0:T(128)} %root.3, s32[128]{0:T(128)} %block.3, bf16[6,128,256]{2,1,0:T(8,128)(2,1)} %bitcast.4), custom_call_target="tpu_custom_call" | custom-call | bytes 2097152 | tf_op jit(solution)/shard_map/pallas_call | solution.py:316
  2.1 12.0 %all-to-all-start = ((bf16[16,128,256]{2,1,0:T(8,128)(2,1)}), bf16[16,128,256]{2,1,0:T(8,128)(2,1)S(1)}, u32[]{:S(2)}, u32[]{:S(2)}) async-start(bf16[16,128,256]{2,1,0:T(8,128)(2,1)} %get-tuple-element.28), calls=%async_computation | async-start | bytes 2097152 | tf_op jit(solution)/shard_map/all_to_all | solution.py:314
  14.1 0.1 copy.17.cols
  14.2 0.1 copy.18.present
  14.3 1.7 shard_map.119
  16.0 28.0 %all-to-all-done.incoming = bf16[16,128,256]{2,1,0:T(8,128)(2,1)S(1)} async-done(((bf16[16,128,256]{2,1,0:T(8,128)(2,1)}), bf16[16,128,256]{2,1,0:T(8,128)(2,1)S(1)}, u32[]{:S(2)}, u32[]{:S(2)}) %all-to-all-start) | async-done | bytes 1048608 | tf_op jit(solution)/shard_map/all_to_all | solution.py:314
  44.0 4.4 %shard_map.120 = (bf16[16,128,256]{2,1,0:T(8,128)(2,1)}, bf16[15,128,256]{2,1,0:T(8,128)(2,1)S(1)}) custom-call(s32[152]{0:T(256)S(4)} %get-tuple-element.26.table, bf16[15,128,256]{2,1,0:T(8,128)(2,1)S(1)} %get-tuple-element.27.begun, bf16[16,128,256]{2,1,0:T(8,128)(2,1)S(1)} %all-to-all-done.incoming, ...), custom_call_target="tpu_custom_call", output_to_operand_aliasing={{1}: (1, {})} | custom-call | flops 536870912 | bytes 4194304 | tf_op jit(solution)/shard_map/pallas_call | solution.py:341
  48.4 0.0 copy-start.1
  48.4 0.0 copy-start.3
  48.4 3.9 %all-to-all-start.1 = ((bf16[16,128,256]{2,1,0:T(8,128)(2,1)}), bf16[16,128,256]{2,1,0:T(8,128)(2,1)S(1)}, u32[]{:S(2)}, u32[]{:S(2)}) async-start(bf16[16,128,256]{2,1,0:T(8,128)(2,1)} %get-tuple-element.29), calls=%async_computation.1 | async-start | bytes 2097152 | tf_op jit(solution)/shard_map/all_to_all | solution.py:314
  52.4 3.3 %shard_map.121 = (f32[4,128,256]{2,1,0:T(8,128)S(1)}, f32[2,128,256]{2,1,0:T(8,128)S(1)}, f32[2,128,256]{2,1,0:T(8,128)S(1)}, f32[2,256]{1,0:T(2,128)S(1)}) custom-call(s32[152]{0:T(256)S(4)} %get-tuple-element.26.table, bf16[15,128,256]{2,1,0:T(8,128)(2,1)S(1)} %get-tuple-element.30.view, bf16[14,8,128,128]{3,2,1,0:T(8,128)(2,1)} %tiles.7, ...), custom_call_target="tpu_custom_call" | custom-call | flops 503316480 | bytes 5242880 | tf_op jit(solution)/shard_map/pallas_call | solution.py:351
  55.7 23.9 %all-to-all-done.1.incoming = bf16[16,128,256]{2,1,0:T(8,128)(2,1)S(1)} async-done(((bf16[16,128,256]{2,1,0:T(8,128)(2,1)}), bf16[16,128,256]{2,1,0:T(8,128)(2,1)S(1)}, u32[]{:S(2)}, u32[]{:S(2)}) %all-to-all-start.1) | async-done | bytes 1048608 | tf_op jit(solution)/shard_map/all_to_all | solution.py:314
  79.6 1.3 shard_map.122
  80.9 7.8 %all-to-all-start.2 = ((f32[32,2,256]{2,1,0:T(2,128)}), f32[32,2,256]{2,1,0:T(2,128)S(1)}, u32[]{:S(2)}, u32[]{:S(2)}) async-start(f32[32,2,256]{2,1,0:T(2,128)} %get-tuple-element.35), calls=%async_computation.2 | async-start | bytes 131072 | tf_op jit(solution)/shard_map/all_to_all | solution.py:314
  88.7 15.2 %all_gather.3.column = bf16[8,144,256]{2,1,0:T(8,128)(2,1)S(1)} all-gather(bf16[2,144,256]{2,1,0:T(8,128)(2,1)S(1)} %get-tuple-element.34), channel_id=1, replica_groups=mesh['gx'=8,'gy_0'=2,'gy_1'=2,'gz_0'=4,'gz_1'=4] {'gz_1'}, dimensions={0}, use_global_device_ids=true | all-gather | bytes 737280 | tf_op jit(solution)/shard_map/all_gather | solution.py:371
  104.0 0.0 all-to-all-done.2
  104.0 1.2 shard_map.123
  105.2 0.0 copy-start.7
  105.2 0.0 copy-start.8
  105.2 4.6 %all-to-all-start.3 = ((bf16[16,144,256]{2,1,0:T(8,128)(2,1)}), bf16[16,144,256]{2,1,0:T(8,128)(2,1)S(1)}, u32[]{:S(2)}, u32[]{:S(2)}) async-start(bf16[16,144,256]{2,1,0:T(8,128)(2,1)} %shard_map.123), calls=%async_computation.3 | async-start | bytes 2359296 | tf_op jit(solution)/shard_map/all_to_all | solution.py:314
  109.8 5.7 %psum.14 = f32[2,256]{1,0:T(2,128)S(1)} all-reduce(f32[2,256]{1,0:T(2,128)S(1)} %reduce_sum.9), channel_id=1, replica_groups=mesh['gx'=8,'gy_0'=2,'gy_1'=2,'gz_0'=4,'gz_1'=4] {'gy_0','gy_1'}, use_global_device_ids=true, to_apply=%region_1.0 | all-reduce | flops 512 | bytes 4096 | tf_op jit(solution)/shard_map/psum | solution.py:381
  115.5 11.3 %psum.15.sums = f32[2,256]{1,0:T(2,128)S(1)} all-reduce(f32[2,256]{1,0:T(2,128)S(1)} %psum.14), channel_id=1, replica_groups=mesh['gx'=8,'gy_0'=2,'gy_1'=2,'gz_0'=4,'gz_1'=4] {'gz_1'}, use_global_device_ids=true, to_apply=%region_2.0 | all-reduce | flops 512 | bytes 4096 | tf_op jit(solution)/shard_map/psum | solution.py:381
  126.8 0.0 all-to-all-done.3.incoming
  126.8 3.7 %shard_map.124 = (bf16[16,128,256]{2,1,0:T(8,128)(2,1)}, bf16[15,128,256]{2,1,0:T(8,128)(2,1)S(1)}) custom-call(s32[152]{0:T(256)S(4)} %get-tuple-element.26.table, f32[2,256]{1,0:T(2,128)S(1)} %psum.15.sums, f32[1,256]{1,0:T(1,128)S(1)} %bitcast.6, f32[1,256]{1,0:T(1,128)S(1)} %bitcast.7, f32[4,128,256]{2,1,0:T(8,128)S(1)} %get-tuple-element.37.first_own, ...), custom_call_target="tpu_custom_call" | custom-call | flops 536870912 | bytes 5242880 | tf_op jit(solution)/shard_map/pallas_call | solution.py:383
  130.5 0.0 copy-start.2
  130.5 0.0 copy-start.4
  130.5 7.3 %all-to-all-start.4 = ((bf16[16,128,256]{2,1,0:T(8,128)(2,1)}), bf16[16,128,256]{2,1,0:T(8,128)(2,1)S(1)}, u32[]{:S(2)}, u32[]{:S(2)}) async-start(bf16[16,128,256]{2,1,0:T(8,128)(2,1)} %get-tuple-element.40), calls=%async_computation.4 | async-start | bytes 2097152 | tf_op jit(solution)/shard_map/all_to_all | solution.py:314
  137.8 3.8 %shard_map.125 = (bf16[6,128,256]{2,1,0:T(8,128)(2,1)}, f32[2,128,256]{2,1,0:T(8,128)S(1)}, f32[2,128,256]{2,1,0:T(8,128)S(1)}) custom-call(s32[152]{0:T(256)S(4)} %get-tuple-element.26.table, bf16[15,128,256]{2,1,0:T(8,128)(2,1)S(1)} %get-tuple-element.41.view, bf16[14,8,128,128]{3,2,1,0:T(8,128)(2,1)} %tiles.7, bf16[256,256]{1,0:T(8,128)(2,1)S(1)} %copy-done.4, ...), custom_call_target="tpu_custom_call" | custom-call | flops 503316480 | bytes 5242880 | tf_op jit(solution)/shard_map/pallas_call | solution.py:392
  141.6 23.8 %all-to-all-done.4.incoming = bf16[16,128,256]{2,1,0:T(8,128)(2,1)S(1)} async-done(((bf16[16,128,256]{2,1,0:T(8,128)(2,1)}), bf16[16,128,256]{2,1,0:T(8,128)(2,1)S(1)}, u32[]{:S(2)}, u32[]{:S(2)}) %all-to-all-start.4) | async-done | bytes 1048608 | tf_op jit(solution)/shard_map/all_to_all | solution.py:314
  165.5 1.2 shard_map.126
  (15 shorter events, 0.1 us)
Async XLA Ops:
  0.0 14.1 %copy-start.9 = (s32[14,8]{0,1:T(8,128)S(1)}, s32[14,8]{0,1:T(8,128)}, u32[]{:S(2)}) copy-start(s32[14,8]{0,1:T(8,128)} %param.14) | copy-start | bytes 1348
  0.0 14.2 %copy-start.10 = (s32[14,8]{0,1:T(8,128)S(1)}, s32[14,8]{0,1:T(8,128)}, u32[]{:S(2)}) copy-start(s32[14,8]{0,1:T(8,128)} %param.15) | copy-start | bytes 1348
  0.0 14.3 %copy-start = (bf16[768,256]{1,0:T(8,128)(2,1)S(1)}, bf16[768,256]{1,0:T(8,128)(2,1)}, u32[]{:S(2)}) copy-start(bf16[768,256]{1,0:T(8,128)(2,1)} %param.12) | copy-start | bytes 1179652
  0.0 14.3 %copy-start.5 = (s32[128]{0:T(128)S(1)}, s32[128]{0:T(128)}, u32[]{:S(2)}) copy-start(s32[128]{0:T(128)} %root.3) | copy-start | bytes 1540
  0.0 14.3 %copy-start.6 = (s32[128]{0:T(128)S(1)}, s32[128]{0:T(128)}, u32[]{:S(2)}) copy-start(s32[128]{0:T(128)} %block.3) | copy-start | bytes 1540
  2.1 41.8 %all-to-all-start = ((bf16[16,128,256]{2,1,0:T(8,128)(2,1)}), bf16[16,128,256]{2,1,0:T(8,128)(2,1)S(1)}, u32[]{:S(2)}, u32[]{:S(2)}) async-start(bf16[16,128,256]{2,1,0:T(8,128)(2,1)} %get-tuple-element.28), calls=%async_computation | async-start | bytes 2097152 | tf_op jit(solution)/shard_map/all_to_all | solution.py:314
  48.4 3.9 %copy-start.1 = (bf16[256,256]{1,0:T(8,128)(2,1)S(1)}, bf16[256,256]{1,0:T(8,128)(2,1)}, u32[]{:S(2)}) copy-start(bf16[256,256]{1,0:T(8,128)(2,1)} %w_neigh.5) | copy-start | bytes 393220
  48.4 3.9 %copy-start.3 = (bf16[256,256]{1,0:T(8,128)(2,1)S(1)}, bf16[256,256]{1,0:T(8,128)(2,1)}, u32[]{:S(2)}) copy-start(bf16[256,256]{1,0:T(8,128)(2,1)} %w_self.2) | copy-start | bytes 393220
  48.4 31.1 %all-to-all-start.1 = ((bf16[16,128,256]{2,1,0:T(8,128)(2,1)}), bf16[16,128,256]{2,1,0:T(8,128)(2,1)S(1)}, u32[]{:S(2)}, u32[]{:S(2)}) async-start(bf16[16,128,256]{2,1,0:T(8,128)(2,1)} %get-tuple-element.29), calls=%async_computation.1 | async-start | bytes 2097152 | tf_op jit(solution)/shard_map/all_to_all | solution.py:314
  80.9 23.0 %all-to-all-start.2 = ((f32[32,2,256]{2,1,0:T(2,128)}), f32[32,2,256]{2,1,0:T(2,128)S(1)}, u32[]{:S(2)}, u32[]{:S(2)}) async-start(f32[32,2,256]{2,1,0:T(2,128)} %get-tuple-element.35), calls=%async_computation.2 | async-start | bytes 131072 | tf_op jit(solution)/shard_map/all_to_all | solution.py:314
  105.2 21.6 %copy-start.7 = (f32[256]{0:T(256)S(1)}, f32[256]{0:T(256)}, u32[]{:S(2)}) copy-start(f32[256]{0:T(256)} %param.20) | copy-start | bytes 3076
  105.2 21.6 %copy-start.8 = (f32[256]{0:T(256)S(1)}, f32[256]{0:T(256)}, u32[]{:S(2)}) copy-start(f32[256]{0:T(256)} %param.21) | copy-start | bytes 3076
  105.2 21.6 %all-to-all-start.3 = ((bf16[16,144,256]{2,1,0:T(8,128)(2,1)}), bf16[16,144,256]{2,1,0:T(8,128)(2,1)S(1)}, u32[]{:S(2)}, u32[]{:S(2)}) async-start(bf16[16,144,256]{2,1,0:T(8,128)(2,1)} %shard_map.123), calls=%async_computation.3 | async-start | bytes 2359296 | tf_op jit(solution)/shard_map/all_to_all | solution.py:314
  130.5 7.3 %copy-start.2 = (bf16[256,256]{1,0:T(8,128)(2,1)S(1)}, bf16[256,256]{1,0:T(8,128)(2,1)}, u32[]{:S(2)}) copy-start(bf16[256,256]{1,0:T(8,128)(2,1)} %w_neigh.7) | copy-start | bytes 393220
  130.5 7.3 %copy-start.4 = (bf16[256,256]{1,0:T(8,128)(2,1)S(1)}, bf16[256,256]{1,0:T(8,128)(2,1)}, u32[]{:S(2)}) copy-start(bf16[256,256]{1,0:T(8,128)(2,1)} %w_self.3) | copy-start | bytes 393220
  130.5 34.9 %all-to-all-start.4 = ((bf16[16,128,256]{2,1,0:T(8,128)(2,1)}), bf16[16,128,256]{2,1,0:T(8,128)(2,1)S(1)}, u32[]{:S(2)}, u32[]{:S(2)}) async-start(bf16[16,128,256]{2,1,0:T(8,128)(2,1)} %get-tuple-element.40), calls=%async_computation.4 | async-start | bytes 2097152 | tf_op jit(solution)/shard_map/all_to_all | solution.py:314

commit v6 on v5

--- a/solution.py
+++ b/solution.py
@@ -28,6 +28,7 @@
 SEL_AT = 120
 PASS_AT = 136
 ENTRIES = 152
+READY = 4
 SIDE = 4
 
 f32 = jnp.float32
@@ -78,7 +79,7 @@
     mine = my_place()
 
     def send(q, chosen):
-        return pltpu.make_async_copy(split.at[chosen], out.at[q], sems.at[q])
+        return pltpu.make_async_copy(split.at[chosen], out.at[q], sems)
 
     def select(q):
         held = jnp.int32(0)
@@ -88,12 +89,14 @@
         send(q, jnp.maximum(held - 1, 0)).start()
 
     loop(GROUP, select)
-    loop(GROUP, lambda q: send(q, 0).wait())
-
-
-def tables_kernel(root, block, cols, present, sel, rows, table, view, sem):
-    load_rows = pltpu.make_async_copy(rows, view.at[pl.ds(0, ROOTED)], sem)
+    pltpu.make_async_copy(out, out, sems).wait()
+
+
+def tables_kernel(root, block, cols, present, sel, rows, tiles, table, view, ready, sem):
+    load_rows = pltpu.make_async_copy(rows, view.at[pl.ds(0, ROOTED)], sem.at[0])
+    load_tiles = pltpu.make_async_copy(tiles.at[pl.ds(ROOTED, READY)], ready, sem.at[1])
     load_rows.start()
+    load_tiles.start()
     mine = my_place()
     my_x, my_z = lax.axis_index("gz_0"), lax.axis_index("gz_1")
 
@@ -117,6 +120,7 @@
         table[SEL_AT + q] = sel[q]
     view[SLOTS] = jnp.zeros((TILE, F), bf16)
     load_rows.wait()
+    load_tiles.wait()
 
 
 def tile_copy(tiles, tbuf, tsem, first, i):
@@ -127,44 +131,58 @@
     loop(count, lambda i: tile_copy(tiles, tbuf, tsem, first, i).start())
 
 
-def tile_row(table, tiles, tbuf, tsem, first, i, view):
-    tile_copy(tiles, tbuf, tsem, first, i).wait()
-    b = first + i
+def tile_sum(table, row_tiles, b, view):
     acc = None
     for k in range(0, K, 2):
-        left = jnp.concatenate([tbuf[i, k], tbuf[i, k + 1]], axis=1)
+        left = jnp.concatenate([row_tiles[k], row_tiles[k + 1]], axis=1)
         right = jnp.concatenate([view[table[b * K + k]], view[table[b * K + k + 1]]], axis=0)
         term = dot(left, right)
         acc = term if acc is None else acc + term
     return acc
 
 
-def replica_rows(table, tiles, out, view, tbuf, obuf, tsem, osem):
+def tile_row(table, tiles, tbuf, tsem, i, view):
+    tile_copy(tiles, tbuf, tsem, 0, i).wait()
+    return tile_sum(table, tbuf.at[i], i, view)
+
+
+def group_copies(tiles, tbuf, tsem, groups):
+    return {
+        first: pltpu.make_async_copy(
+            tiles.at[pl.ds(ROOTED + first, count)], tbuf.at[pl.ds(first, count)], tsem.at[n]
+        )
+        for n, (first, count) in enumerate(groups)
+    }
+
+
+def replica_rows(table, row_tiles, waits, out, view, obuf, osem):
     def send(h):
-        return pltpu.make_async_copy(obuf.at[h], out.at[table[ROOTS_AT + h]], osem.at[h])
-
-    def step(h):
-        obuf[h] = tile_row(table, tiles, tbuf, tsem, ROOTED, h, view).astype(bf16)
-
-        @pl.when(h > 0)
-        def _():
-            send(h - 1).start()
-
-    loop(HOST, step)
-    send(HOST - 1).start()
-    loop(HOST, lambda h: send(h).wait())
-
-
-def replica_kernel(table, begun, incoming, tiles, out, view, tbuf, obuf, vsem, tsem, osem):
-    def hosted(h):
-        return pltpu.make_async_copy(
-            incoming.at[table[ROOTS_AT + h]], view.at[ROOTED + h], vsem.at[h]
-        )
-
-    loop(HOST, lambda h: hosted(h).start())
-    load_tiles(tiles, tbuf, tsem, ROOTED, HOST)
-    loop(HOST, lambda h: hosted(h).wait())
-    replica_rows(table, tiles, out, view, tbuf, obuf, tsem, osem)
+        pltpu.make_async_copy(obuf.at[h], out.at[table[ROOTS_AT + h]], osem).start()
+
+    for h in range(HOST):
+        if h in waits:
+            waits[h].wait()
+        obuf[h] = tile_sum(table, row_tiles(h), ROOTED + h, view).astype(bf16)
+        if h:
+            send(h - 1)
+    send(HOST - 1)
+    pltpu.make_async_copy(obuf, out.at[pl.ds(0, HOST)], osem).wait()
+
+
+def replica_kernel(table, begun, incoming, ready, tiles, out, view, tbuf, obuf, vsem, tsem, osem):
+    for h in range(HOST):
+        pltpu.make_async_copy(
+            incoming.at[table[ROOTS_AT + h]], view.at[ROOTED + h], vsem
+        ).start()
+    later = group_copies(tiles, tbuf, tsem, ((READY, 2), (READY + 2, 2)))
+    for c in later.values():
+        c.start()
+    pltpu.make_async_copy(
+        incoming.at[pl.ds(0, HOST)], view.at[pl.ds(ROOTED, HOST)], vsem
+    ).wait()
+    replica_rows(
+        table, lambda h: ready.at[h] if h < READY else tbuf.at[h], later, out, view, obuf, osem
+    )
 
 
 def own_kernel(table, view, tiles, w_self, w_neigh, first_own, self_split, part_split, sums, tbuf, tsem):
@@ -172,7 +190,7 @@
     sums[...] = jnp.zeros((2, F), f32)
 
     def own(b, carry):
-        neighbours = tile_row(table, tiles, tbuf, tsem, 0, b, view).astype(bf16)
+        neighbours = tile_row(table, tiles, tbuf, tsem, b, view).astype(bf16)
         first = dot(view[b], w_self[...]) + dot(neighbours, w_neigh[...])
         first_own[b] = first
         sums[0:1] += jnp.sum(first, axis=0, keepdims=True)
@@ -180,7 +198,7 @@
         return carry
 
     def split(s, carry):
-        part_split[s] = tile_row(table, tiles, tbuf, tsem, 0, OWN + s, view)
+        part_split[s] = tile_row(table, tiles, tbuf, tsem, OWN + s, view)
         self_split[s] = dot(view[OWN + s], w_self[...])
         return carry
 
@@ -224,17 +242,19 @@
 def pass_kernel(table, column, out, sems):
     def send(i):
         chosen = (i & (SIDE - 1)) * SPLIT + table[PASS_AT + i]
-        return pltpu.make_async_copy(column.at[chosen], out.at[i], sems.at[i])
+        return pltpu.make_async_copy(column.at[chosen], out.at[i], sems)
 
     loop(GROUP, lambda i: send(i).start())
-    loop(GROUP, lambda i: send(i).wait())
+    pltpu.make_async_copy(out, out, sems).wait()
 
 
 def hidden_kernel(
     count, table, sums, scale, shift, first_own, first_split, incoming, tiles,
     out, view, tbuf, obuf, tsem, osem,
 ):
-    load_tiles(tiles, tbuf, tsem, ROOTED, HOST)
+    copies = group_copies(tiles, tbuf, tsem, ((0, 4), (4, 4)))
+    for c in copies.values():
+        c.start()
     mean = sums[0:1] * (1.0 / count)
     var = sums[1:2] * (1.0 / count) - mean * mean
     inv = lax.rsqrt(var + 1e-5)
@@ -261,20 +281,20 @@
     lax.fori_loop(0, SPLIT, split, 0)
     lax.fori_loop(0, HOST, hosted, 0)
     view[SLOTS] = jnp.zeros((TILE, F), bf16)
-    replica_rows(table, tiles, out, view, tbuf, obuf, tsem, osem)
+    replica_rows(table, lambda h: tbuf.at[h], copies, out, view, obuf, osem)
 
 
 def own_two_kernel(table, view, tiles, w_self, w_neigh, out, self_split, part_split, tbuf, tsem):
     load_tiles(tiles, tbuf, tsem, 0, ROOTED)
 
     def own(b, carry):
-        neighbours = tile_row(table, tiles, tbuf, tsem, 0, b, view).astype(bf16)
+        neighbours = tile_row(table, tiles, tbuf, tsem, b, view).astype(bf16)
         second = dot(view[b], w_self[...]) + dot(neighbours, w_neigh[...])
         out[b] = second.astype(bf16)
         return carry
 
     def split(s, carry):
-        part_split[s] = tile_row(table, tiles, tbuf, tsem, 0, OWN + s, view)
+        part_split[s] = tile_row(table, tiles, tbuf, tsem, OWN + s, view)
         self_split[s] = dot(view[OWN + s], w_self[...])
         return carry
 
@@ -322,30 +342,31 @@
             pltpu.VMEM((SPLIT, TILE, F), bf16),
             pltpu.SMEM((GROUP * HOST,), jnp.int32),
             pltpu.SMEM((GROUP * HOST,), jnp.int32),
-            DMA((3,)), DMA((GROUP,)),
+            DMA((3,)), DMA,
         ],
     )(host_root, host_block, rows)
     incoming = exchange(outgoing)
 
-    table, view = call(
+    table, view, ready = call(
         tables_kernel, 0, 8 << 20,
         out_shape=(
             pltpu.SMEM((ENTRIES,), jnp.int32),
             view_v,
+            tile_rows(READY),
         ),
-        in_specs=[SMEM] * 5 + [HBM],
-        out_specs=(SMEM, VMEM),
-        scratch_shapes=[DMA],
-    )(host_root, host_block, tile_columns, tile_present, sel, rows)
+        in_specs=[SMEM] * 5 + [HBM] * 2,
+        out_specs=(SMEM, VMEM, VMEM),
+        scratch_shapes=[DMA((2,))],
+    )(host_root, host_block, tile_columns, tile_present, sel, rows, tile_values)
 
     outgoing, view = call(
         replica_kernel, 64 * MAC, 4 << 20,
         out_shape=(wire, view_v),
-        in_specs=[SMEM] + [VMEM] * 2 + [HBM],
+        in_specs=[SMEM] + [VMEM] * 3 + [HBM],
         out_specs=(HBM, VMEM),
         input_output_aliases={1: 1},
-        scratch_shapes=[tile_rows(HOST), row_buffer] + [DMA((HOST,))] * 3,
-    )(table, view, incoming, tile_values)
+        scratch_shapes=[tile_rows(HOST), row_buffer, DMA, DMA((2,)), DMA],
+    )(table, view, incoming, ready, tile_values)
     returned = exchange(outgoing)
 
     first_own, self_split, part_split, own_sums = call(
@@ -375,7 +396,7 @@
         out_shape=pltpu.HBM((GROUP, TILE + CENTER_ROWS, F), bf16),
         in_specs=[SMEM, VMEM],
         out_specs=HBM,
-        scratch_shapes=[DMA((GROUP,))],
+        scratch_shapes=[DMA],
     )(table, column)
     incoming = exchange(outgoing, "gz_0")
     sums = lax.psum(lax.psum(jnp.sum(plane_sums, axis=0), ("gy_0", "gy_1")), "gz_1")
@@ -385,7 +406,7 @@
         out_shape=(wire, view_v),
         in_specs=[SMEM] + [VMEM] * 6 + [HBM],
         out_specs=(HBM, VMEM),
-        scratch_shapes=[tile_rows(HOST), row_buffer, DMA((HOST,)), DMA((HOST,))],
+        scratch_shapes=[tile_rows(HOST), row_buffer, DMA((2,)), DMA],
     )(table, sums, scale, shift, first_own, first_split, incoming, tile_values)
     returned = exchange(outgoing)
 

time: 167 us -> 165 us (0.988)
  Pallas kernels: 22.8 us -> 20.8 us
  transfers between devices with their start and end apart: 5 -> 5, of which waited for: 3 -> 3; matrix products, arithmetic and copies ran while one was open for 0% -> 0% of each run, Pallas kernels for 5% -> 6%
where the time goes in v6:
time: 165 us; the launch traced here: 164 us
  waiting for transfers between devices  74.9 us (45%)
  starting transfers between devices  35.5 us (22%)
  blocking collectives  32.2 us (20%)
  Pallas kernels  20.8 us (13%)
    all_to_all x5, waiting for transfers between devices, exchange(): return lax.all_to_all(blocks, axes, split_axis=0, concat_axis=0, tiled=True)  74.9 us
    all_to_all x5, starting transfers between devices, exchange(): return lax.all_to_all(blocks, axes, split_axis=0, concat_axis=0, tiled=True)  35.5 us
    all_gather x1, blocking collectives, layers(): column = lax.all_gather(parts, 'gz_1', axis=0, tiled=True)  15.2 us
    psum x1, blocking collectives, layers(): lax.psum(lax.psum(jnp.sum(plane_sums, axis=0), ('gy_0', 'gy_1')), 'gz_1')  11.3 us
    psum x1, blocking collectives, layers(): lax.psum(jnp.sum(plane_sums, axis=0), ('gy_0', 'gy_1'))  5.67 us
    pallas_call x1, Pallas kernels, layers(): call(own_two_kernel, 60 * MAC, 5 << 20, out_shape=(shape((ROOTED, TILE, F...  3.82 us
  transfers between devices with their start and end apart: 5, of which 3 were waited for; matrix products, arithmetic and copies ran while one was open for 0% of the time, Pallas kernels for 6%

profile of v6, /device:TPU:64, one launch (start us, length us, event | category | flops | bytes accessed | tf_op | source)
XLA Modules:
  0.0 163.8 jit_solution(7300730372754813783)
XLA Ops:
  0.0 0.0 copy-start.5
  0.0 0.0 copy-start.6
  0.0 2.0 %shard_map.118 = (bf16[16,128,256]{2,1,0:T(8,128)(2,1)}, s32[16]{0:T(128)S(4)}) custom-call(s32[128]{0:T(128)} %root.3, s32[128]{0:T(128)} %block.3, bf16[6,128,256]{2,1,0:T(8,128)(2,1)} %bitcast.4), custom_call_target="tpu_custom_call" | custom-call | bytes 2097152 | tf_op jit(solution)/shard_map/pallas_call | solution.py:336
  2.0 12.0 %all-to-all-start = ((bf16[16,128,256]{2,1,0:T(8,128)(2,1)}), bf16[16,128,256]{2,1,0:T(8,128)(2,1)S(1)}, u32[]{:S(2)}, u32[]{:S(2)}) async-start(bf16[16,128,256]{2,1,0:T(8,128)(2,1)} %get-tuple-element.29), calls=%async_computation | async-start | bytes 2097152 | tf_op jit(solution)/shard_map/all_to_all | solution.py:334
  14.0 0.1 copy.17.cols
  14.1 0.1 copy.18.present
  14.2 2.2 %shard_map.119 = (s32[152]{0:T(256)S(4)}, bf16[15,128,256]{2,1,0:T(8,128)(2,1)S(1)}, bf16[4,8,128,128]{3,2,1,0:T(8,128)(2,1)S(1)}) custom-call(s32[128]{0:T(128)S(1)} %copy-done.5, s32[128]{0:T(128)S(1)} %copy-done.6, s32[14,8]{1,0:T(8,128)S(1)} %copy.17.cols, s32[14,8]{1,0:T(8,128)S(1)} %copy.18.present, s32[16]{0:T(128)S(4)} %get-tuple-element.26.sel, ...), custom_call_target="tpu_custom_call" | custom-call | bytes 8388608 | tf_op jit(solution)/shard_map/pallas_call | solution.py:350
  16.4 27.4 %all-to-all-done.incoming = bf16[16,128,256]{2,1,0:T(8,128)(2,1)S(1)} async-done(((bf16[16,128,256]{2,1,0:T(8,128)(2,1)}), bf16[16,128,256]{2,1,0:T(8,128)(2,1)S(1)}, u32[]{:S(2)}, u32[]{:S(2)}) %all-to-all-start) | async-done | bytes 1048608 | tf_op jit(solution)/shard_map/all_to_all | solution.py:334
  43.8 3.0 %shard_map.120 = (bf16[16,128,256]{2,1,0:T(8,128)(2,1)}, bf16[15,128,256]{2,1,0:T(8,128)(2,1)S(1)}) custom-call(s32[152]{0:T(256)S(4)} %get-tuple-element.27.table, bf16[15,128,256]{2,1,0:T(8,128)(2,1)S(1)} %get-tuple-element.28.begun, bf16[16,128,256]{2,1,0:T(8,128)(2,1)S(1)} %all-to-all-done.incoming, ...), custom_call_target="tpu_custom_call", output_to_operand_aliasing={{1}: (1, {})} | custom-call | flops 536870912 | bytes 4194304 | tf_op jit(solution)/shard_map/pallas_call | solution.py:362
  46.9 0.0 copy-start.1
  46.9 0.0 copy-start.3
  46.9 3.9 %all-to-all-start.1 = ((bf16[16,128,256]{2,1,0:T(8,128)(2,1)}), bf16[16,128,256]{2,1,0:T(8,128)(2,1)S(1)}, u32[]{:S(2)}, u32[]{:S(2)}) async-start(bf16[16,128,256]{2,1,0:T(8,128)(2,1)} %get-tuple-element.31), calls=%async_computation.1 | async-start | bytes 2097152 | tf_op jit(solution)/shard_map/all_to_all | solution.py:334
  50.8 3.3 %shard_map.121 = (f32[4,128,256]{2,1,0:T(8,128)S(1)}, f32[2,128,256]{2,1,0:T(8,128)S(1)}, f32[2,128,256]{2,1,0:T(8,128)S(1)}, f32[2,256]{1,0:T(2,128)S(1)}) custom-call(s32[152]{0:T(256)S(4)} %get-tuple-element.27.table, bf16[15,128,256]{2,1,0:T(8,128)(2,1)S(1)} %get-tuple-element.32.view, bf16[14,8,128,128]{3,2,1,0:T(8,128)(2,1)} %tiles.9, ...), custom_call_target="tpu_custom_call" | custom-call | flops 503316480 | bytes 5242880 | tf_op jit(solution)/shard_map/pallas_call | solution.py:372
  54.1 23.9 %all-to-all-done.1.incoming = bf16[16,128,256]{2,1,0:T(8,128)(2,1)S(1)} async-done(((bf16[16,128,256]{2,1,0:T(8,128)(2,1)}), bf16[16,128,256]{2,1,0:T(8,128)(2,1)S(1)}, u32[]{:S(2)}, u32[]{:S(2)}) %all-to-all-start.1) | async-done | bytes 1048608 | tf_op jit(solution)/shard_map/all_to_all | solution.py:334
  78.0 1.3 shard_map.122
  79.4 7.8 %all-to-all-start.2 = ((f32[32,2,256]{2,1,0:T(2,128)}), f32[32,2,256]{2,1,0:T(2,128)S(1)}, u32[]{:S(2)}, u32[]{:S(2)}) async-start(f32[32,2,256]{2,1,0:T(2,128)} %get-tuple-element.37), calls=%async_computation.2 | async-start | bytes 131072 | tf_op jit(solution)/shard_map/all_to_all | solution.py:334
  87.2 15.2 %all_gather.3.column = bf16[8,144,256]{2,1,0:T(8,128)(2,1)S(1)} all-gather(bf16[2,144,256]{2,1,0:T(8,128)(2,1)S(1)} %get-tuple-element.36), channel_id=1, replica_groups=mesh['gx'=8,'gy_0'=2,'gy_1'=2,'gz_0'=4,'gz_1'=4] {'gz_1'}, dimensions={0}, use_global_device_ids=true | all-gather | bytes 737280 | tf_op jit(solution)/shard_map/all_gather | solution.py:392
  102.4 0.0 all-to-all-done.2
  102.4 1.1 shard_map.123
  103.5 0.0 copy-start.7
  103.5 0.0 copy-start.8
  103.5 4.6 %all-to-all-start.3 = ((bf16[16,144,256]{2,1,0:T(8,128)(2,1)}), bf16[16,144,256]{2,1,0:T(8,128)(2,1)S(1)}, u32[]{:S(2)}, u32[]{:S(2)}) async-start(bf16[16,144,256]{2,1,0:T(8,128)(2,1)} %shard_map.123), calls=%async_computation.3 | async-start | bytes 2359296 | tf_op jit(solution)/shard_map/all_to_all | solution.py:334
  108.1 5.7 %psum.14 = f32[2,256]{1,0:T(2,128)S(1)} all-reduce(f32[2,256]{1,0:T(2,128)S(1)} %reduce_sum.9), channel_id=1, replica_groups=mesh['gx'=8,'gy_0'=2,'gy_1'=2,'gz_0'=4,'gz_1'=4] {'gy_0','gy_1'}, use_global_device_ids=true, to_apply=%region_1.0 | all-reduce | flops 512 | bytes 4096 | tf_op jit(solution)/shard_map/psum | solution.py:402
  113.8 11.3 %psum.15.sums = f32[2,256]{1,0:T(2,128)S(1)} all-reduce(f32[2,256]{1,0:T(2,128)S(1)} %psum.14), channel_id=1, replica_groups=mesh['gx'=8,'gy_0'=2,'gy_1'=2,'gz_0'=4,'gz_1'=4] {'gz_1'}, use_global_device_ids=true, to_apply=%region_2.0 | all-reduce | flops 512 | bytes 4096 | tf_op jit(solution)/shard_map/psum | solution.py:402
  125.1 0.0 all-to-all-done.3.incoming
  125.1 2.9 %shard_map.124 = (bf16[16,128,256]{2,1,0:T(8,128)(2,1)}, bf16[15,128,256]{2,1,0:T(8,128)(2,1)S(1)}) custom-call(s32[152]{0:T(256)S(4)} %get-tuple-element.27.table, f32[2,256]{1,0:T(2,128)S(1)} %psum.15.sums, f32[1,256]{1,0:T(1,128)S(1)} %bitcast.6, f32[1,256]{1,0:T(1,128)S(1)} %bitcast.7, f32[4,128,256]{2,1,0:T(8,128)S(1)} %get-tuple-element.39.first_own, ...), custom_call_target="tpu_custom_call" | custom-call | flops 536870912 | bytes 5242880 | tf_op jit(solution)/shard_map/pallas_call | solution.py:404
  128.0 0.0 copy-start.2
  128.0 0.0 copy-start.4
  128.0 7.2 %all-to-all-start.4 = ((bf16[16,128,256]{2,1,0:T(8,128)(2,1)}), bf16[16,128,256]{2,1,0:T(8,128)(2,1)S(1)}, u32[]{:S(2)}, u32[]{:S(2)}) async-start(bf16[16,128,256]{2,1,0:T(8,128)(2,1)} %get-tuple-element.42), calls=%async_computation.4 | async-start | bytes 2097152 | tf_op jit(solution)/shard_map/all_to_all | solution.py:334
  135.3 3.8 %shard_map.125 = (bf16[6,128,256]{2,1,0:T(8,128)(2,1)}, f32[2,128,256]{2,1,0:T(8,128)S(1)}, f32[2,128,256]{2,1,0:T(8,128)S(1)}) custom-call(s32[152]{0:T(256)S(4)} %get-tuple-element.27.table, bf16[15,128,256]{2,1,0:T(8,128)(2,1)S(1)} %get-tuple-element.43.view, bf16[14,8,128,128]{3,2,1,0:T(8,128)(2,1)} %tiles.9, bf16[256,256]{1,0:T(8,128)(2,1)S(1)} %copy-done.4, ...), custom_call_target="tpu_custom_call" | custom-call | flops 503316480 | bytes 5242880 | tf_op jit(solution)/shard_map/pallas_call | solution.py:413
  139.1 23.5 %all-to-all-done.4.incoming = bf16[16,128,256]{2,1,0:T(8,128)(2,1)S(1)} async-done(((bf16[16,128,256]{2,1,0:T(8,128)(2,1)}), bf16[16,128,256]{2,1,0:T(8,128)(2,1)S(1)}, u32[]{:S(2)}, u32[]{:S(2)}) %all-to-all-start.4) | async-done | bytes 1048608 | tf_op jit(solution)/shard_map/all_to_all | solution.py:334
  162.6 1.2 shard_map.126
  (15 shorter events, 0.1 us)
Async XLA Ops:
  0.0 14.0 %copy-start.9 = (s32[14,8]{0,1:T(8,128)S(1)}, s32[14,8]{0,1:T(8,128)}, u32[]{:S(2)}) copy-start(s32[14,8]{0,1:T(8,128)} %param.14) | copy-start | bytes 1348
  0.0 14.1 %copy-start.10 = (s32[14,8]{0,1:T(8,128)S(1)}, s32[14,8]{0,1:T(8,128)}, u32[]{:S(2)}) copy-start(s32[14,8]{0,1:T(8,128)} %param.15) | copy-start | bytes 1348
  0.0 14.2 %copy-start = (bf16[768,256]{1,0:T(8,128)(2,1)S(1)}, bf16[768,256]{1,0:T(8,128)(2,1)}, u32[]{:S(2)}) copy-start(bf16[768,256]{1,0:T(8,128)(2,1)} %param.12) | copy-start | bytes 1179652
  0.0 14.2 %copy-start.5 = (s32[128]{0:T(128)S(1)}, s32[128]{0:T(128)}, u32[]{:S(2)}) copy-start(s32[128]{0:T(128)} %root.3) | copy-start | bytes 1540
  0.0 14.2 %copy-start.6 = (s32[128]{0:T(128)S(1)}, s32[128]{0:T(128)}, u32[]{:S(2)}) copy-start(s32[128]{0:T(128)} %block.3) | copy-start | bytes 1540
  2.0 41.8 %all-to-all-start = ((bf16[16,128,256]{2,1,0:T(8,128)(2,1)}), bf16[16,128,256]{2,1,0:T(8,128)(2,1)S(1)}, u32[]{:S(2)}, u32[]{:S(2)}) async-start(bf16[16,128,256]{2,1,0:T(8,128)(2,1)} %get-tuple-element.29), calls=%async_computation | async-start | bytes 2097152 | tf_op jit(solution)/shard_map/all_to_all | solution.py:334
  46.9 3.9 %copy-start.1 = (bf16[256,256]{1,0:T(8,128)(2,1)S(1)}, bf16[256,256]{1,0:T(8,128)(2,1)}, u32[]{:S(2)}) copy-start(bf16[256,256]{1,0:T(8,128)(2,1)} %w_neigh.5) | copy-start | bytes 393220
  46.9 3.9 %copy-start.3 = (bf16[256,256]{1,0:T(8,128)(2,1)S(1)}, bf16[256,256]{1,0:T(8,128)(2,1)}, u32[]{:S(2)}) copy-start(bf16[256,256]{1,0:T(8,128)(2,1)} %w_self.2) | copy-start | bytes 393220
  46.9 31.1 %all-to-all-start.1 = ((bf16[16,128,256]{2,1,0:T(8,128)(2,1)}), bf16[16,128,256]{2,1,0:T(8,128)(2,1)S(1)}, u32[]{:S(2)}, u32[]{:S(2)}) async-start(bf16[16,128,256]{2,1,0:T(8,128)(2,1)} %get-tuple-element.31), calls=%async_computation.1 | async-start | bytes 2097152 | tf_op jit(solution)/shard_map/all_to_all | solution.py:334
  79.4 23.1 %all-to-all-start.2 = ((f32[32,2,256]{2,1,0:T(2,128)}), f32[32,2,256]{2,1,0:T(2,128)S(1)}, u32[]{:S(2)}, u32[]{:S(2)}) async-start(f32[32,2,256]{2,1,0:T(2,128)} %get-tuple-element.37), calls=%async_computation.2 | async-start | bytes 131072 | tf_op jit(solution)/shard_map/all_to_all | solution.py:334
  103.5 21.6 %copy-start.7 = (f32[256]{0:T(256)S(1)}, f32[256]{0:T(256)}, u32[]{:S(2)}) copy-start(f32[256]{0:T(256)} %param.20) | copy-start | bytes 3076
  103.5 21.6 %copy-start.8 = (f32[256]{0:T(256)S(1)}, f32[256]{0:T(256)}, u32[]{:S(2)}) copy-start(f32[256]{0:T(256)} %param.21) | copy-start | bytes 3076
  103.5 21.6 %all-to-all-start.3 = ((bf16[16,144,256]{2,1,0:T(8,128)(2,1)}), bf16[16,144,256]{2,1,0:T(8,128)(2,1)S(1)}, u32[]{:S(2)}, u32[]{:S(2)}) async-start(bf16[16,144,256]{2,1,0:T(8,128)(2,1)} %shard_map.123), calls=%async_computation.3 | async-start | bytes 2359296 | tf_op jit(solution)/shard_map/all_to_all | solution.py:334
  128.0 7.3 %copy-start.2 = (bf16[256,256]{1,0:T(8,128)(2,1)S(1)}, bf16[256,256]{1,0:T(8,128)(2,1)}, u32[]{:S(2)}) copy-start(bf16[256,256]{1,0:T(8,128)(2,1)} %w_neigh.7) | copy-start | bytes 393220
  128.0 7.3 %copy-start.4 = (bf16[256,256]{1,0:T(8,128)(2,1)S(1)}, bf16[256,256]{1,0:T(8,128)(2,1)}, u32[]{:S(2)}) copy-start(bf16[256,256]{1,0:T(8,128)(2,1)} %w_self.3) | copy-start | bytes 393220
  128.0 34.6 %all-to-all-start.4 = ((bf16[16,128,256]{2,1,0:T(8,128)(2,1)}), bf16[16,128,256]{2,1,0:T(8,128)(2,1)S(1)}, u32[]{:S(2)}, u32[]{:S(2)}) async-start(bf16[16,128,256]{2,1,0:T(8,128)(2,1)} %get-tuple-element.42), calls=%async_computation.4 | async-start | bytes 2097152 | tf_op jit(solution)/shard_map/all_to_all | solution.py:334

commit v7 on v6

--- a/solution.py
+++ b/solution.py
@@ -26,8 +26,7 @@
 PLANE_SIZE = 32
 ROOTS_AT = 112
 SEL_AT = 120
-PASS_AT = 136
-ENTRIES = 152
+ENTRIES = 136
 READY = 4
 SIDE = 4
 
@@ -66,58 +65,51 @@
     lax.fori_loop(0, n, lambda i, c: (step(i), c)[1], 0)
 
 
-def outgoing_kernel(root, block, rows, out, sel, split, root_s, block_s, sem, sems):
+def begin_kernel(root, block, rows, picks, parts, root_s, block_s, sem):
     loads = [
         pltpu.make_async_copy(root, root_s, sem.at[0]),
         pltpu.make_async_copy(block, block_s, sem.at[1]),
-        pltpu.make_async_copy(rows.at[pl.ds(OWN, SPLIT)], split, sem.at[2]),
+        pltpu.make_async_copy(rows.at[pl.ds(OWN, SPLIT)], parts, sem.at[2]),
     ]
     for c in loads:
         c.start()
-    for c in loads:
+    for c in loads[:2]:
         c.wait()
-    mine = my_place()
-
-    def send(q, chosen):
-        return pltpu.make_async_copy(split.at[chosen], out.at[q], sems)
-
-    def select(q):
-        held = jnp.int32(0)
+    my_x, my_z = lax.axis_index("gz_0"), lax.axis_index("gz_1")
+
+    def pick(i):
+        target, source = (i // SIDE) * SIDE + my_z, my_x * SIDE + (i & (SIDE - 1))
+        chosen = jnp.int32(0)
         for j in range(HOST):
-            held = jnp.where(root_s[q * HOST + j] == mine, block_s[q * HOST + j] + 1, held)
-        sel[q] = held
-        send(q, jnp.maximum(held - 1, 0)).start()
-
-    loop(GROUP, select)
-    pltpu.make_async_copy(out, out, sems).wait()
-
-
-def tables_kernel(root, block, cols, present, sel, rows, tiles, table, view, ready, sem):
+            at = target * HOST + j
+            chosen = jnp.where(root_s[at] == source, block_s[at], chosen)
+        picks[i] = chosen
+
+    loop(GROUP, pick)
+    loads[2].wait()
+
+
+def tables_kernel(root, block, cols, present, rows, tiles, table, view, ready, sem):
     load_rows = pltpu.make_async_copy(rows, view.at[pl.ds(0, ROOTED)], sem.at[0])
     load_tiles = pltpu.make_async_copy(tiles.at[pl.ds(ROOTED, READY)], ready, sem.at[1])
     load_rows.start()
     load_tiles.start()
     mine = my_place()
-    my_x, my_z = lax.axis_index("gz_0"), lax.axis_index("gz_1")
-
-    def passed_on(i):
-        target, source = (i // SIDE) * SIDE + my_z, my_x * SIDE + (i & (SIDE - 1))
-        chosen = jnp.int32(0)
+
+    def select(q):
+        held = jnp.int32(0)
         for j in range(HOST):
-            at = target * HOST + j
-            chosen = jnp.where(root[at] == source, block[at], chosen)
-        table[PASS_AT + i] = chosen
+            held = jnp.where(root[q * HOST + j] == mine, block[q * HOST + j] + 1, held)
+        table[SEL_AT + q] = held
 
     def slots(b):
         for k in range(K):
             table[b * K + k] = jnp.where(present[b, k] > 0, cols[b, k], SLOTS)
 
     loop(SLOTS, slots)
-    loop(GROUP, passed_on)
+    loop(GROUP, select)
     for h in range(HOST):
         table[ROOTS_AT + h] = root[mine * HOST + h]
-    for q in range(GROUP):
-        table[SEL_AT + q] = sel[q]
     view[SLOTS] = jnp.zeros((TILE, F), bf16)
     load_rows.wait()
     load_tiles.wait()
@@ -239,13 +231,13 @@
         parts[s, pl.ds(TILE, CENTER_ROWS)] = jnp.broadcast_to(center, (CENTER_ROWS, F))
 
 
-def pass_kernel(table, column, out, sems):
+def pass_kernel(picks, column, out, sem):
     def send(i):
-        chosen = (i & (SIDE - 1)) * SPLIT + table[PASS_AT + i]
-        return pltpu.make_async_copy(column.at[chosen], out.at[i], sems)
+        chosen = (i & (SIDE - 1)) * SPLIT + picks[i]
+        return pltpu.make_async_copy(column.at[chosen], out.at[i], sem)
 
     loop(GROUP, lambda i: send(i).start())
-    pltpu.make_async_copy(out, out, sems).wait()
+    pltpu.make_async_copy(out, out, sem).wait()
 
 
 def hidden_kernel(
@@ -333,19 +325,25 @@
     def exchange(blocks, axes=GZ):
         return lax.all_to_all(blocks, axes, split_axis=0, concat_axis=0, tiled=True)
 
-    outgoing, sel = call(
-        outgoing_kernel, 0, 2 << 20, room=60 << 20,
-        out_shape=(wire, pltpu.SMEM((GROUP,), jnp.int32)),
+    def spread(parts):
+        column = lax.all_gather(parts, "gz_1", axis=0, tiled=True)
+        outgoing = call(
+            pass_kernel, 0, 2 << 20,
+            out_shape=pltpu.HBM((GROUP,) + parts.shape[1:], bf16),
+            in_specs=[SMEM, VMEM],
+            out_specs=HBM,
+            scratch_shapes=[DMA],
+        )(picks, column)
+        return exchange(outgoing, "gz_0")
+
+    picks, parts = call(
+        begin_kernel, 0, 1 << 18, room=60 << 20,
+        out_shape=(pltpu.SMEM((GROUP,), jnp.int32), pltpu.VMEM((SPLIT, TILE, F), bf16)),
         in_specs=[HBM] * 3,
-        out_specs=(HBM, SMEM),
-        scratch_shapes=[
-            pltpu.VMEM((SPLIT, TILE, F), bf16),
-            pltpu.SMEM((GROUP * HOST,), jnp.int32),
-            pltpu.SMEM((GROUP * HOST,), jnp.int32),
-            DMA((3,)), DMA,
-        ],
+        out_specs=(SMEM, VMEM),
+        scratch_shapes=[pltpu.SMEM((GROUP * HOST,), jnp.int32)] * 2 + [DMA((3,))],
     )(host_root, host_block, rows)
-    incoming = exchange(outgoing)
+    incoming = spread(parts)
 
     table, view, ready = call(
         tables_kernel, 0, 8 << 20,
@@ -354,10 +352,10 @@
             view_v,
             tile_rows(READY),
         ),
-        in_specs=[SMEM] * 5 + [HBM] * 2,
+        in_specs=[SMEM] * 4 + [HBM] * 2,
         out_specs=(SMEM, VMEM, VMEM),
         scratch_shapes=[DMA((2,))],
-    )(host_root, host_block, tile_columns, tile_present, sel, rows, tile_values)
+    )(host_root, host_block, tile_columns, tile_present, rows, tile_values)
 
     outgoing, view = call(
         replica_kernel, 64 * MAC, 4 << 20,
@@ -389,16 +387,7 @@
         scratch_shapes=[pltpu.VMEM((SPLIT, TILE, F), f32)],
     )(table, returned, part_split, self_split, own_sums, neigh_one)
     plane_sums = exchange(sums, PLANE)
-    column = lax.all_gather(parts, "gz_1", axis=0, tiled=True)
-    column, plane_sums = lax.optimization_barrier((column, plane_sums))
-    outgoing = call(
-        pass_kernel, 0, 2 << 20,
-        out_shape=pltpu.HBM((GROUP, TILE + CENTER_ROWS, F), bf16),
-        in_specs=[SMEM, VMEM],
-        out_specs=HBM,
-        scratch_shapes=[DMA],
-    )(table, column)
-    incoming = exchange(outgoing, "gz_0")
+    incoming = spread(parts)
     sums = lax.psum(lax.psum(jnp.sum(plane_sums, axis=0), ("gy_0", "gy_1")), "gz_1")
 
     outgoing, view = call(

time: 165 us -> 163 us (0.988)
  the two profiles are of different devices: /device:TPU:64 before, /device:TPU:88 now
where the time goes in v7:
time: 163 us; the launch traced here: 162 us
  waiting for transfers between devices  59.3 us (36%)
  blocking collectives  52.3 us (32%)
  starting transfers between devices  29.4 us (18%)
  Pallas kernels  20.9 us (13%)
    all_to_all x5, waiting for transfers between devices, exchange(): return lax.all_to_all(blocks, axes, split_axis=0, concat_axis=0, tiled=True)  59.3 us
    all_gather x2, blocking collectives, spread(): column = lax.all_gather(parts, 'gz_1', axis=0, tiled=True)  36.1 us
    all_to_all x5, starting transfers between devices, exchange(): return lax.all_to_all(blocks, axes, split_axis=0, concat_axis=0, tiled=True)  29.4 us
    psum x1, blocking collectives, layers(): lax.psum(lax.psum(jnp.sum(plane_sums, axis=0), ('gy_0', 'gy_1')), 'gz_1')  10.3 us
    psum x1, blocking collectives, layers(): lax.psum(jnp.sum(plane_sums, axis=0), ('gy_0', 'gy_1'))  5.96 us
    pallas_call x1, Pallas kernels, layers(): call(own_two_kernel, 60 * MAC, 5 << 20, out_shape=(shape((ROOTED, TILE, F...  3.82 us
    pallas_call x1, Pallas kernels, layers(): call(own_kernel, 60 * MAC, 5 << 20, out_shape=(pltpu.VMEM((OWN, TILE, F),...  3.29 us
  transfers between devices with their start and end apart: 5, of which 3 were waited for; matrix products, arithmetic and copies ran while one was open for 0% of the time, Pallas kernels for 6%

profile of v7, /device:TPU:88, one launch (start us, length us, event | category | flops | bytes accessed | tf_op | source)
XLA Modules:
  0.0 162.4 jit_solution(6899597731236823591)
XLA Ops:
  0.0 1.1 shard_map.119
  1.1 21.0 %all_gather.6.column = bf16[8,128,256]{2,1,0:T(8,128)(2,1)S(1)} all-gather(bf16[2,128,256]{2,1,0:T(8,128)(2,1)S(1)} %get-tuple-element.27), channel_id=1, replica_groups=mesh['gx'=8,'gy_0'=2,'gy_1'=2,'gz_0'=4,'gz_1'=4] {'gz_1'}, dimensions={0}, use_global_device_ids=true | all-gather | bytes 655360 | tf_op jit(solution)/shard_map/all_gather | solution.py:329
  22.1 1.0 shard_map.120
  23.1 0.0 copy-start.9
  23.1 0.0 copy-start.10
  23.1 0.0 copy-start
  23.1 0.0 copy-start.5
  23.1 4.4 %all-to-all-start = ((bf16[16,128,256]{2,1,0:T(8,128)(2,1)}), bf16[16,128,256]{2,1,0:T(8,128)(2,1)S(1)}, u32[]{:S(2)}, u32[]{:S(2)}) async-start(bf16[16,128,256]{2,1,0:T(8,128)(2,1)} %shard_map.120), calls=%async_computation | async-start | bytes 2097152 | tf_op jit(solution)/shard_map/all_to_all | solution.py:326
  27.6 0.1 copy.17.cols
  27.7 0.1 copy.18.present
  27.8 2.2 %shard_map.118 = (s32[136]{0:T(256)S(4)}, bf16[15,128,256]{2,1,0:T(8,128)(2,1)S(1)}, bf16[4,8,128,128]{3,2,1,0:T(8,128)(2,1)S(1)}) custom-call(s32[128]{0:T(128)S(1)} %copy-done.5, s32[128]{0:T(128)S(1)} %copy-done.6, s32[14,8]{1,0:T(8,128)S(1)} %copy.17.cols, s32[14,8]{1,0:T(8,128)S(1)} %copy.18.present, bf16[6,128,256]{2,1,0:T(8,128)(2,1)S(1)} %bitcast.5, ...), custom_call_target="tpu_custom_call" | custom-call | bytes 8388608 | tf_op jit(solution)/shard_map/pallas_call | solution.py:348
  30.0 12.4 %all-to-all-done.incoming = bf16[16,128,256]{2,1,0:T(8,128)(2,1)S(1)} async-done(((bf16[16,128,256]{2,1,0:T(8,128)(2,1)}), bf16[16,128,256]{2,1,0:T(8,128)(2,1)S(1)}, u32[]{:S(2)}, u32[]{:S(2)}) %all-to-all-start) | async-done | bytes 1048608 | tf_op jit(solution)/shard_map/all_to_all | solution.py:326
  42.4 3.0 %shard_map.121 = (bf16[16,128,256]{2,1,0:T(8,128)(2,1)}, bf16[15,128,256]{2,1,0:T(8,128)(2,1)S(1)}) custom-call(s32[136]{0:T(256)S(4)} %get-tuple-element.24.table, bf16[15,128,256]{2,1,0:T(8,128)(2,1)S(1)} %get-tuple-element.25.begun, bf16[16,128,256]{2,1,0:T(8,128)(2,1)S(1)} %all-to-all-done.incoming, ...), custom_call_target="tpu_custom_call", output_to_operand_aliasing={{1}: (1, {})} | custom-call | flops 536870912 | bytes 4194304 | tf_op jit(solution)/shard_map/pallas_call | solution.py:360
  45.4 0.0 copy-start.1
  45.5 4.7 %all-to-all-start.1 = ((bf16[16,128,256]{2,1,0:T(8,128)(2,1)}), bf16[16,128,256]{2,1,0:T(8,128)(2,1)S(1)}, u32[]{:S(2)}, u32[]{:S(2)}) async-start(bf16[16,128,256]{2,1,0:T(8,128)(2,1)} %get-tuple-element.29), calls=%async_computation.1 | async-start | bytes 2097152 | tf_op jit(solution)/shard_map/all_to_all | solution.py:326
  50.2 3.3 %shard_map.122 = (f32[4,128,256]{2,1,0:T(8,128)S(1)}, f32[2,128,256]{2,1,0:T(8,128)S(1)}, f32[2,128,256]{2,1,0:T(8,128)S(1)}, f32[2,256]{1,0:T(2,128)S(1)}) custom-call(s32[136]{0:T(256)S(4)} %get-tuple-element.24.table, bf16[15,128,256]{2,1,0:T(8,128)(2,1)S(1)} %get-tuple-element.30.view, bf16[14,8,128,128]{3,2,1,0:T(8,128)(2,1)} %tiles.9, ...), custom_call_target="tpu_custom_call" | custom-call | flops 503316480 | bytes 5242880 | tf_op jit(solution)/shard_map/pallas_call | solution.py:370
  53.5 23.4 %all-to-all-done.1.incoming = bf16[16,128,256]{2,1,0:T(8,128)(2,1)S(1)} async-done(((bf16[16,128,256]{2,1,0:T(8,128)(2,1)}), bf16[16,128,256]{2,1,0:T(8,128)(2,1)S(1)}, u32[]{:S(2)}, u32[]{:S(2)}) %all-to-all-start.1) | async-done | bytes 1048608 | tf_op jit(solution)/shard_map/all_to_all | solution.py:326
  76.9 1.3 shard_map.123
  78.2 7.9 %all-to-all-start.2 = ((f32[32,2,256]{2,1,0:T(2,128)}), f32[32,2,256]{2,1,0:T(2,128)S(1)}, u32[]{:S(2)}, u32[]{:S(2)}) async-start(f32[32,2,256]{2,1,0:T(2,128)} %get-tuple-element.34), calls=%async_computation.2 | async-start | bytes 131072 | tf_op jit(solution)/shard_map/all_to_all | solution.py:326
  86.2 15.1 %all_gather.7.column = bf16[8,144,256]{2,1,0:T(8,128)(2,1)S(1)} all-gather(bf16[2,144,256]{2,1,0:T(8,128)(2,1)S(1)} %get-tuple-element.37), channel_id=1, replica_groups=mesh['gx'=8,'gy_0'=2,'gy_1'=2,'gz_0'=4,'gz_1'=4] {'gz_1'}, dimensions={0}, use_global_device_ids=true | all-gather | bytes 737280 | tf_op jit(solution)/shard_map/all_gather | solution.py:329
  101.2 1.1 shard_map.124
  102.3 0.0 copy-start.7
  102.3 0.0 copy-start.8
  102.3 4.2 %all-to-all-start.3 = ((bf16[16,144,256]{2,1,0:T(8,128)(2,1)}), bf16[16,144,256]{2,1,0:T(8,128)(2,1)S(1)}, u32[]{:S(2)}, u32[]{:S(2)}) async-start(bf16[16,144,256]{2,1,0:T(8,128)(2,1)} %shard_map.124), calls=%async_computation.3 | async-start | bytes 2359296 | tf_op jit(solution)/shard_map/all_to_all | solution.py:326
  106.6 6.0 %psum.14 = f32[2,256]{1,0:T(2,128)S(1)} all-reduce(f32[2,256]{1,0:T(2,128)S(1)} %reduce_sum.9), channel_id=1, replica_groups=mesh['gx'=8,'gy_0'=2,'gy_1'=2,'gz_0'=4,'gz_1'=4] {'gy_0','gy_1'}, use_global_device_ids=true, to_apply=%region_1.0 | all-reduce | flops 512 | bytes 4096 | tf_op jit(solution)/shard_map/psum | solution.py:391
  112.6 10.3 %psum.15.sums = f32[2,256]{1,0:T(2,128)S(1)} all-reduce(f32[2,256]{1,0:T(2,128)S(1)} %psum.14), channel_id=1, replica_groups=mesh['gx'=8,'gy_0'=2,'gy_1'=2,'gz_0'=4,'gz_1'=4] {'gz_1'}, use_global_device_ids=true, to_apply=%region_2.0 | all-reduce | flops 512 | bytes 4096 | tf_op jit(solution)/shard_map/psum | solution.py:391
  122.9 2.9 %shard_map.125 = (bf16[16,128,256]{2,1,0:T(8,128)(2,1)}, bf16[15,128,256]{2,1,0:T(8,128)(2,1)S(1)}) custom-call(s32[136]{0:T(256)S(4)} %get-tuple-element.24.table, f32[2,256]{1,0:T(2,128)S(1)} %psum.15.sums, f32[1,256]{1,0:T(1,128)S(1)} %bitcast.6, f32[1,256]{1,0:T(1,128)S(1)} %bitcast.7, f32[4,128,256]{2,1,0:T(8,128)S(1)} %get-tuple-element.35.first_own, ...), custom_call_target="tpu_custom_call" | custom-call | flops 536870912 | bytes 5242880 | tf_op jit(solution)/shard_map/pallas_call | solution.py:393
  125.8 0.0 copy-start.2
  125.8 8.1 %all-to-all-start.4 = ((bf16[16,128,256]{2,1,0:T(8,128)(2,1)}), bf16[16,128,256]{2,1,0:T(8,128)(2,1)S(1)}, u32[]{:S(2)}, u32[]{:S(2)}) async-start(bf16[16,128,256]{2,1,0:T(8,128)(2,1)} %get-tuple-element.38), calls=%async_computation.4 | async-start | bytes 2097152 | tf_op jit(solution)/shard_map/all_to_all | solution.py:326
  133.9 3.8 %shard_map.126 = (bf16[6,128,256]{2,1,0:T(8,128)(2,1)}, f32[2,128,256]{2,1,0:T(8,128)S(1)}, f32[2,128,256]{2,1,0:T(8,128)S(1)}) custom-call(s32[136]{0:T(256)S(4)} %get-tuple-element.24.table, bf16[15,128,256]{2,1,0:T(8,128)(2,1)S(1)} %get-tuple-element.39.view, bf16[14,8,128,128]{3,2,1,0:T(8,128)(2,1)} %tiles.9, bf16[256,256]{1,0:T(8,128)(2,1)S(1)} %copy-done.4, ...), custom_call_target="tpu_custom_call" | custom-call | flops 503316480 | bytes 5242880 | tf_op jit(solution)/shard_map/pallas_call | solution.py:402
  137.7 23.5 %all-to-all-done.4.incoming = bf16[16,128,256]{2,1,0:T(8,128)(2,1)S(1)} async-done(((bf16[16,128,256]{2,1,0:T(8,128)(2,1)}), bf16[16,128,256]{2,1,0:T(8,128)(2,1)S(1)}, u32[]{:S(2)}, u32[]{:S(2)}) %all-to-all-start.4) | async-done | bytes 1048608 | tf_op jit(solution)/shard_map/all_to_all | solution.py:326
  161.2 1.2 shard_map.127
  (17 shorter events, 0.1 us)
Async XLA Ops:
  23.1 4.5 %copy-start.9 = (s32[14,8]{0,1:T(8,128)S(1)}, s32[14,8]{0,1:T(8,128)}, u32[]{:S(2)}) copy-start(s32[14,8]{0,1:T(8,128)} %param.14) | copy-start | bytes 1348
  23.1 4.6 %copy-start.10 = (s32[14,8]{0,1:T(8,128)S(1)}, s32[14,8]{0,1:T(8,128)}, u32[]{:S(2)}) copy-start(s32[14,8]{0,1:T(8,128)} %param.15) | copy-start | bytes 1348
  23.1 4.6 %copy-start = (bf16[768,256]{1,0:T(8,128)(2,1)S(1)}, bf16[768,256]{1,0:T(8,128)(2,1)}, u32[]{:S(2)}) copy-start(bf16[768,256]{1,0:T(8,128)(2,1)} %param.12) | copy-start | bytes 1179652
  23.1 4.6 %copy-start.5 = (s32[128]{0:T(128)S(1)}, s32[128]{0:T(128)}, u32[]{:S(2)}) copy-start(s32[128]{0:T(128)} %root.3) | copy-start | bytes 1540
  23.1 4.6 %copy-start.6 = (s32[128]{0:T(128)S(1)}, s32[128]{0:T(128)}, u32[]{:S(2)}) copy-start(s32[128]{0:T(128)} %block.3) | copy-start | bytes 1540
  23.1 19.2 %all-to-all-start = ((bf16[16,128,256]{2,1,0:T(8,128)(2,1)}), bf16[16,128,256]{2,1,0:T(8,128)(2,1)S(1)}, u32[]{:S(2)}, u32[]{:S(2)}) async-start(bf16[16,128,256]{2,1,0:T(8,128)(2,1)} %shard_map.120), calls=%async_computation | async-start | bytes 2097152 | tf_op jit(solution)/shard_map/all_to_all | solution.py:326
  45.4 4.8 %copy-start.1 = (bf16[256,256]{1,0:T(8,128)(2,1)S(1)}, bf16[256,256]{1,0:T(8,128)(2,1)}, u32[]{:S(2)}) copy-start(bf16[256,256]{1,0:T(8,128)(2,1)} %w_neigh.5) | copy-start | bytes 393220
  45.4 4.8 %copy-start.3 = (bf16[256,256]{1,0:T(8,128)(2,1)S(1)}, bf16[256,256]{1,0:T(8,128)(2,1)}, u32[]{:S(2)}) copy-start(bf16[256,256]{1,0:T(8,128)(2,1)} %w_self.2) | copy-start | bytes 393220
  45.5 31.4 %all-to-all-start.1 = ((bf16[16,128,256]{2,1,0:T(8,128)(2,1)}), bf16[16,128,256]{2,1,0:T(8,128)(2,1)S(1)}, u32[]{:S(2)}, u32[]{:S(2)}) async-start(bf16[16,128,256]{2,1,0:T(8,128)(2,1)} %get-tuple-element.29), calls=%async_computation.1 | async-start | bytes 2097152 | tf_op jit(solution)/shard_map/all_to_all | solution.py:326
  78.2 24.1 %all-to-all-start.2 = ((f32[32,2,256]{2,1,0:T(2,128)}), f32[32,2,256]{2,1,0:T(2,128)S(1)}, u32[]{:S(2)}, u32[]{:S(2)}) async-start(f32[32,2,256]{2,1,0:T(2,128)} %get-tuple-element.34), calls=%async_computation.2 | async-start | bytes 131072 | tf_op jit(solution)/shard_map/all_to_all | solution.py:326
  102.3 20.6 %copy-start.7 = (f32[256]{0:T(256)S(1)}, f32[256]{0:T(256)}, u32[]{:S(2)}) copy-start(f32[256]{0:T(256)} %param.20) | copy-start | bytes 3076
  102.3 20.6 %copy-start.8 = (f32[256]{0:T(256)S(1)}, f32[256]{0:T(256)}, u32[]{:S(2)}) copy-start(f32[256]{0:T(256)} %param.21) | copy-start | bytes 3076
  102.3 20.5 %all-to-all-start.3 = ((bf16[16,144,256]{2,1,0:T(8,128)(2,1)}), bf16[16,144,256]{2,1,0:T(8,128)(2,1)S(1)}, u32[]{:S(2)}, u32[]{:S(2)}) async-start(bf16[16,144,256]{2,1,0:T(8,128)(2,1)} %shard_map.124), calls=%async_computation.3 | async-start | bytes 2359296 | tf_op jit(solution)/shard_map/all_to_all | solution.py:326
  125.8 8.1 %copy-start.2 = (bf16[256,256]{1,0:T(8,128)(2,1)S(1)}, bf16[256,256]{1,0:T(8,128)(2,1)}, u32[]{:S(2)}) copy-start(bf16[256,256]{1,0:T(8,128)(2,1)} %w_neigh.7) | copy-start | bytes 393220
  125.8 8.1 %copy-start.4 = (bf16[256,256]{1,0:T(8,128)(2,1)S(1)}, bf16[256,256]{1,0:T(8,128)(2,1)}, u32[]{:S(2)}) copy-start(bf16[256,256]{1,0:T(8,128)(2,1)} %w_self.3) | copy-start | bytes 393220
  125.8 35.5 %all-to-all-start.4 = ((bf16[16,128,256]{2,1,0:T(8,128)(2,1)}), bf16[16,128,256]{2,1,0:T(8,128)(2,1)S(1)}, u32[]{:S(2)}, u32[]{:S(2)}) async-start(bf16[16,128,256]{2,1,0:T(8,128)(2,1)} %get-tuple-element.38), calls=%async_computation.4 | async-start | bytes 2097152 | tf_op jit(solution)/shard_map/all_to_all | solution.py:326

commit v8 on v7

--- a/solution.py
+++ b/solution.py
@@ -19,14 +19,15 @@
 GROUP = 16
 CENTER_ROWS = 16
 VMEM_BYTES = 50 << 20
-GZ = ("gz_0", "gz_1")
+GZ = ("gz_1", "gz_0")
 GX_GY_GZ = ("gx", "gy_0", "gy_1", "gz_0", "gz_1")
 GX_GY = ("gx", "gy_0", "gy_1")
 PLANE = ("gx", "gz_0")
 PLANE_SIZE = 32
 ROOTS_AT = 112
 SEL_AT = 120
-ENTRIES = 136
+TARGETS_AT = 136
+ENTRIES = 144
 READY = 4
 SIDE = 4
 
@@ -59,6 +60,10 @@
 
 def my_place():
     return lax.axis_index("gz_0") * 4 + lax.axis_index("gz_1")
+
+
+def swapped(q):
+    return (q & (SIDE - 1)) * SIDE + q // SIDE
 
 
 def loop(n, step):
@@ -100,7 +105,7 @@
         held = jnp.int32(0)
         for j in range(HOST):
             held = jnp.where(root[q * HOST + j] == mine, block[q * HOST + j] + 1, held)
-        table[SEL_AT + q] = held
+        table[SEL_AT + swapped(q)] = held
 
     def slots(b):
         for k in range(K):
@@ -109,7 +114,9 @@
     loop(SLOTS, slots)
     loop(GROUP, select)
     for h in range(HOST):
-        table[ROOTS_AT + h] = root[mine * HOST + h]
+        q = root[mine * HOST + h]
+        table[ROOTS_AT + h] = q
+        table[TARGETS_AT + h] = swapped(q)
     view[SLOTS] = jnp.zeros((TILE, F), bf16)
     load_rows.wait()
     load_tiles.wait()
@@ -149,7 +156,7 @@
 
 def replica_rows(table, row_tiles, waits, out, view, obuf, osem):
     def send(h):
-        pltpu.make_async_copy(obuf.at[h], out.at[table[ROOTS_AT + h]], osem).start()
+        pltpu.make_async_copy(obuf.at[h], out.at[table[TARGETS_AT + h]], osem).start()
 
     for h in range(HOST):
         if h in waits:

time: 163 us -> 166 us (1.018)
  the two profiles are of different devices: /device:TPU:88 before, /device:TPU:8 now
where the time goes in v8:
time: 166 us; the launch traced here: 165 us
  blocking collectives  59.6 us (36%)
  waiting for transfers between devices  53.2 us (32%)
  starting transfers between devices  31 us (19%)
  Pallas kernels  20.9 us (13%)
    all_to_all x5, waiting for transfers between devices, exchange(): return lax.all_to_all(blocks, axes, split_axis=0, concat_axis=0, tiled=True)  53.2 us
    all_gather x2, blocking collectives, spread(): column = lax.all_gather(parts, 'gz_1', axis=0, tiled=True)  40.9 us
    all_to_all x5, starting transfers between devices, exchange(): return lax.all_to_all(blocks, axes, split_axis=0, concat_axis=0, tiled=True)  31 us
    psum x1, blocking collectives, layers(): lax.psum(lax.psum(jnp.sum(plane_sums, axis=0), ('gy_0', 'gy_1')), 'gz_1')  11.8 us
    psum x1, blocking collectives, layers(): lax.psum(jnp.sum(plane_sums, axis=0), ('gy_0', 'gy_1'))  6.88 us
    pallas_call x1, Pallas kernels, layers(): call(own_two_kernel, 60 * MAC, 5 << 20, out_shape=(shape((ROOTED, TILE, F...  3.82 us
  transfers between devices with their start and end apart: 5, of which 3 were waited for; matrix products, arithmetic and copies ran while one was open for 0% of the time, Pallas kernels for 6%

profile of v8, /device:TPU:8, one launch (start us, length us, event | category | flops | bytes accessed | tf_op | source)
XLA Modules:
  0.0 165.2 jit_solution(1194742971604179524)
XLA Ops:
  0.0 1.1 shard_map.119
  1.1 21.7 %all_gather.6.column = bf16[8,128,256]{2,1,0:T(8,128)(2,1)S(1)} all-gather(bf16[2,128,256]{2,1,0:T(8,128)(2,1)S(1)} %get-tuple-element.27), channel_id=1, replica_groups=mesh['gx'=8,'gy_0'=2,'gy_1'=2,'gz_0'=4,'gz_1'=4] {'gz_1'}, dimensions={0}, use_global_device_ids=true | all-gather | bytes 655360 | tf_op jit(solution)/shard_map/all_gather | solution.py:336
  22.8 1.0 shard_map.120
  23.8 0.0 copy-start.9
  23.8 0.0 copy-start.10
  23.8 0.0 copy-start
  23.8 0.0 copy-start.5
  23.8 0.0 copy-start.6
  23.8 4.4 %all-to-all-start = ((bf16[16,128,256]{2,1,0:T(8,128)(2,1)}), bf16[16,128,256]{2,1,0:T(8,128)(2,1)S(1)}, u32[]{:S(2)}, u32[]{:S(2)}) async-start(bf16[16,128,256]{2,1,0:T(8,128)(2,1)} %shard_map.120), calls=%async_computation | async-start | bytes 2097152 | tf_op jit(solution)/shard_map/all_to_all | solution.py:333
  28.3 0.1 copy.17.cols
  28.4 0.1 copy.18.present
  28.5 2.2 %shard_map.118 = (s32[144]{0:T(256)S(4)}, bf16[15,128,256]{2,1,0:T(8,128)(2,1)S(1)}, bf16[4,8,128,128]{3,2,1,0:T(8,128)(2,1)S(1)}) custom-call(s32[128]{0:T(128)S(1)} %copy-done.5, s32[128]{0:T(128)S(1)} %copy-done.6, s32[14,8]{1,0:T(8,128)S(1)} %copy.17.cols, s32[14,8]{1,0:T(8,128)S(1)} %copy.18.present, bf16[6,128,256]{2,1,0:T(8,128)(2,1)S(1)} %bitcast.5, ...), custom_call_target="tpu_custom_call" | custom-call | bytes 8388608 | tf_op jit(solution)/shard_map/pallas_call | solution.py:355
  30.7 11.5 %all-to-all-done.incoming = bf16[16,128,256]{2,1,0:T(8,128)(2,1)S(1)} async-done(((bf16[16,128,256]{2,1,0:T(8,128)(2,1)}), bf16[16,128,256]{2,1,0:T(8,128)(2,1)S(1)}, u32[]{:S(2)}, u32[]{:S(2)}) %all-to-all-start) | async-done | bytes 1048608 | tf_op jit(solution)/shard_map/all_to_all | solution.py:333
  42.2 3.1 %shard_map.121 = (bf16[16,128,256]{2,1,0:T(8,128)(2,1)}, bf16[15,128,256]{2,1,0:T(8,128)(2,1)S(1)}) custom-call(s32[144]{0:T(256)S(4)} %get-tuple-element.24.table, bf16[15,128,256]{2,1,0:T(8,128)(2,1)S(1)} %get-tuple-element.25.begun, bf16[16,128,256]{2,1,0:T(8,128)(2,1)S(1)} %all-to-all-done.incoming, ...), custom_call_target="tpu_custom_call", output_to_operand_aliasing={{1}: (1, {})} | custom-call | flops 536870912 | bytes 4194304 | tf_op jit(solution)/shard_map/pallas_call | solution.py:367
  45.2 0.0 copy-start.1
  45.2 0.0 copy-start.3
  45.3 4.7 %all-to-all-start.1 = ((bf16[16,128,256]{2,1,0:T(8,128)(2,1)}), bf16[16,128,256]{2,1,0:T(8,128)(2,1)S(1)}, u32[]{:S(2)}, u32[]{:S(2)}) async-start(bf16[16,128,256]{2,1,0:T(8,128)(2,1)} %get-tuple-element.29), calls=%async_computation.1 | async-start | bytes 2097152 | tf_op jit(solution)/shard_map/all_to_all | solution.py:333
  50.0 3.3 %shard_map.122 = (f32[4,128,256]{2,1,0:T(8,128)S(1)}, f32[2,128,256]{2,1,0:T(8,128)S(1)}, f32[2,128,256]{2,1,0:T(8,128)S(1)}, f32[2,256]{1,0:T(2,128)S(1)}) custom-call(s32[144]{0:T(256)S(4)} %get-tuple-element.24.table, bf16[15,128,256]{2,1,0:T(8,128)(2,1)S(1)} %get-tuple-element.30.view, bf16[14,8,128,128]{3,2,1,0:T(8,128)(2,1)} %tiles.9, ...), custom_call_target="tpu_custom_call" | custom-call | flops 503316480 | bytes 5242880 | tf_op jit(solution)/shard_map/pallas_call | solution.py:377
  53.3 18.3 %all-to-all-done.1.incoming = bf16[16,128,256]{2,1,0:T(8,128)(2,1)S(1)} async-done(((bf16[16,128,256]{2,1,0:T(8,128)(2,1)}), bf16[16,128,256]{2,1,0:T(8,128)(2,1)S(1)}, u32[]{:S(2)}, u32[]{:S(2)}) %all-to-all-start.1) | async-done | bytes 1048608 | tf_op jit(solution)/shard_map/all_to_all | solution.py:333
  71.6 1.3 shard_map.123
  72.9 9.5 %all-to-all-start.2 = ((f32[32,2,256]{2,1,0:T(2,128)}), f32[32,2,256]{2,1,0:T(2,128)S(1)}, u32[]{:S(2)}, u32[]{:S(2)}) async-start(f32[32,2,256]{2,1,0:T(2,128)} %get-tuple-element.34), calls=%async_computation.2 | async-start | bytes 131072 | tf_op jit(solution)/shard_map/all_to_all | solution.py:333
  82.5 19.2 %all_gather.7.column = bf16[8,144,256]{2,1,0:T(8,128)(2,1)S(1)} all-gather(bf16[2,144,256]{2,1,0:T(8,128)(2,1)S(1)} %get-tuple-element.37), channel_id=1, replica_groups=mesh['gx'=8,'gy_0'=2,'gy_1'=2,'gz_0'=4,'gz_1'=4] {'gz_1'}, dimensions={0}, use_global_device_ids=true | all-gather | bytes 737280 | tf_op jit(solution)/shard_map/all_gather | solution.py:336
  101.7 1.1 shard_map.124
  102.8 0.0 copy-start.7
  102.8 4.3 %all-to-all-start.3 = ((bf16[16,144,256]{2,1,0:T(8,128)(2,1)}), bf16[16,144,256]{2,1,0:T(8,128)(2,1)S(1)}, u32[]{:S(2)}, u32[]{:S(2)}) async-start(bf16[16,144,256]{2,1,0:T(8,128)(2,1)} %shard_map.124), calls=%async_computation.3 | async-start | bytes 2359296 | tf_op jit(solution)/shard_map/all_to_all | solution.py:333
  107.1 6.9 %psum.14 = f32[2,256]{1,0:T(2,128)S(1)} all-reduce(f32[2,256]{1,0:T(2,128)S(1)} %reduce_sum.9), channel_id=1, replica_groups=mesh['gx'=8,'gy_0'=2,'gy_1'=2,'gz_0'=4,'gz_1'=4] {'gy_0','gy_1'}, use_global_device_ids=true, to_apply=%region_1.0 | all-reduce | flops 512 | bytes 4096 | tf_op jit(solution)/shard_map/psum | solution.py:398
  114.0 11.8 %psum.15.sums = f32[2,256]{1,0:T(2,128)S(1)} all-reduce(f32[2,256]{1,0:T(2,128)S(1)} %psum.14), channel_id=1, replica_groups=mesh['gx'=8,'gy_0'=2,'gy_1'=2,'gz_0'=4,'gz_1'=4] {'gz_1'}, use_global_device_ids=true, to_apply=%region_2.0 | all-reduce | flops 512 | bytes 4096 | tf_op jit(solution)/shard_map/psum | solution.py:398
  125.8 2.9 %shard_map.125 = (bf16[16,128,256]{2,1,0:T(8,128)(2,1)}, bf16[15,128,256]{2,1,0:T(8,128)(2,1)S(1)}) custom-call(s32[144]{0:T(256)S(4)} %get-tuple-element.24.table, f32[2,256]{1,0:T(2,128)S(1)} %psum.15.sums, f32[1,256]{1,0:T(1,128)S(1)} %bitcast.6, f32[1,256]{1,0:T(1,128)S(1)} %bitcast.7, f32[4,128,256]{2,1,0:T(8,128)S(1)} %get-tuple-element.35.first_own, ...), custom_call_target="tpu_custom_call" | custom-call | flops 536870912 | bytes 5242880 | tf_op jit(solution)/shard_map/pallas_call | solution.py:400
  128.7 8.0 %all-to-all-start.4 = ((bf16[16,128,256]{2,1,0:T(8,128)(2,1)}), bf16[16,128,256]{2,1,0:T(8,128)(2,1)S(1)}, u32[]{:S(2)}, u32[]{:S(2)}) async-start(bf16[16,128,256]{2,1,0:T(8,128)(2,1)} %get-tuple-element.38), calls=%async_computation.4 | async-start | bytes 2097152 | tf_op jit(solution)/shard_map/all_to_all | solution.py:333
  136.8 3.8 %shard_map.126 = (bf16[6,128,256]{2,1,0:T(8,128)(2,1)}, f32[2,128,256]{2,1,0:T(8,128)S(1)}, f32[2,128,256]{2,1,0:T(8,128)S(1)}) custom-call(s32[144]{0:T(256)S(4)} %get-tuple-element.24.table, bf16[15,128,256]{2,1,0:T(8,128)(2,1)S(1)} %get-tuple-element.39.view, bf16[14,8,128,128]{3,2,1,0:T(8,128)(2,1)} %tiles.9, bf16[256,256]{1,0:T(8,128)(2,1)S(1)} %copy-done.4, ...), custom_call_target="tpu_custom_call" | custom-call | flops 503316480 | bytes 5242880 | tf_op jit(solution)/shard_map/pallas_call | solution.py:409
  140.6 23.4 %all-to-all-done.4.incoming = bf16[16,128,256]{2,1,0:T(8,128)(2,1)S(1)} async-done(((bf16[16,128,256]{2,1,0:T(8,128)(2,1)}), bf16[16,128,256]{2,1,0:T(8,128)(2,1)S(1)}, u32[]{:S(2)}, u32[]{:S(2)}) %all-to-all-start.4) | async-done | bytes 1048608 | tf_op jit(solution)/shard_map/all_to_all | solution.py:333
  164.0 1.2 shard_map.127
  (17 shorter events, 0.1 us)
Async XLA Ops:
  23.8 4.5 %copy-start.9 = (s32[14,8]{0,1:T(8,128)S(1)}, s32[14,8]{0,1:T(8,128)}, u32[]{:S(2)}) copy-start(s32[14,8]{0,1:T(8,128)} %param.14) | copy-start | bytes 1348
  23.8 4.6 %copy-start.10 = (s32[14,8]{0,1:T(8,128)S(1)}, s32[14,8]{0,1:T(8,128)}, u32[]{:S(2)}) copy-start(s32[14,8]{0,1:T(8,128)} %param.15) | copy-start | bytes 1348
  23.8 4.6 %copy-start = (bf16[768,256]{1,0:T(8,128)(2,1)S(1)}, bf16[768,256]{1,0:T(8,128)(2,1)}, u32[]{:S(2)}) copy-start(bf16[768,256]{1,0:T(8,128)(2,1)} %param.12) | copy-start | bytes 1179652
  23.8 4.6 %copy-start.5 = (s32[128]{0:T(128)S(1)}, s32[128]{0:T(128)}, u32[]{:S(2)}) copy-start(s32[128]{0:T(128)} %root.3) | copy-start | bytes 1540
  23.8 4.6 %copy-start.6 = (s32[128]{0:T(128)S(1)}, s32[128]{0:T(128)}, u32[]{:S(2)}) copy-start(s32[128]{0:T(128)} %block.3) | copy-start | bytes 1540
  23.8 18.3 %all-to-all-start = ((bf16[16,128,256]{2,1,0:T(8,128)(2,1)}), bf16[16,128,256]{2,1,0:T(8,128)(2,1)S(1)}, u32[]{:S(2)}, u32[]{:S(2)}) async-start(bf16[16,128,256]{2,1,0:T(8,128)(2,1)} %shard_map.120), calls=%async_computation | async-start | bytes 2097152 | tf_op jit(solution)/shard_map/all_to_all | solution.py:333
  45.2 4.7 %copy-start.1 = (bf16[256,256]{1,0:T(8,128)(2,1)S(1)}, bf16[256,256]{1,0:T(8,128)(2,1)}, u32[]{:S(2)}) copy-start(bf16[256,256]{1,0:T(8,128)(2,1)} %w_neigh.5) | copy-start | bytes 393220
  45.2 4.7 %copy-start.3 = (bf16[256,256]{1,0:T(8,128)(2,1)S(1)}, bf16[256,256]{1,0:T(8,128)(2,1)}, u32[]{:S(2)}) copy-start(bf16[256,256]{1,0:T(8,128)(2,1)} %w_self.2) | copy-start | bytes 393220
  45.3 26.3 %all-to-all-start.1 = ((bf16[16,128,256]{2,1,0:T(8,128)(2,1)}), bf16[16,128,256]{2,1,0:T(8,128)(2,1)S(1)}, u32[]{:S(2)}, u32[]{:S(2)}) async-start(bf16[16,128,256]{2,1,0:T(8,128)(2,1)} %get-tuple-element.29), calls=%async_computation.1 | async-start | bytes 2097152 | tf_op jit(solution)/shard_map/all_to_all | solution.py:333
  72.9 29.9 %all-to-all-start.2 = ((f32[32,2,256]{2,1,0:T(2,128)}), f32[32,2,256]{2,1,0:T(2,128)S(1)}, u32[]{:S(2)}, u32[]{:S(2)}) async-start(f32[32,2,256]{2,1,0:T(2,128)} %get-tuple-element.34), calls=%async_computation.2 | async-start | bytes 131072 | tf_op jit(solution)/shard_map/all_to_all | solution.py:333
  102.8 23.1 %copy-start.7 = (f32[256]{0:T(256)S(1)}, f32[256]{0:T(256)}, u32[]{:S(2)}) copy-start(f32[256]{0:T(256)} %param.20) | copy-start | bytes 3076
  102.8 23.1 %copy-start.8 = (f32[256]{0:T(256)S(1)}, f32[256]{0:T(256)}, u32[]{:S(2)}) copy-start(f32[256]{0:T(256)} %param.21) | copy-start | bytes 3076
  102.8 23.0 %all-to-all-start.3 = ((bf16[16,144,256]{2,1,0:T(8,128)(2,1)}), bf16[16,144,256]{2,1,0:T(8,128)(2,1)S(1)}, u32[]{:S(2)}, u32[]{:S(2)}) async-start(bf16[16,144,256]{2,1,0:T(8,128)(2,1)} %shard_map.124), calls=%async_computation.3 | async-start | bytes 2359296 | tf_op jit(solution)/shard_map/all_to_all | solution.py:333
  128.7 8.1 %copy-start.2 = (bf16[256,256]{1,0:T(8,128)(2,1)S(1)}, bf16[256,256]{1,0:T(8,128)(2,1)}, u32[]{:S(2)}) copy-start(bf16[256,256]{1,0:T(8,128)(2,1)} %w_neigh.7) | copy-start | bytes 393220
  128.7 8.1 %copy-start.4 = (bf16[256,256]{1,0:T(8,128)(2,1)S(1)}, bf16[256,256]{1,0:T(8,128)(2,1)}, u32[]{:S(2)}) copy-start(bf16[256,256]{1,0:T(8,128)(2,1)} %w_self.3) | copy-start | bytes 393220
  128.7 35.3 %all-to-all-start.4 = ((bf16[16,128,256]{2,1,0:T(8,128)(2,1)}), bf16[16,128,256]{2,1,0:T(8,128)(2,1)S(1)}, u32[]{:S(2)}, u32[]{:S(2)}) async-start(bf16[16,128,256]{2,1,0:T(8,128)(2,1)} %get-tuple-element.38), calls=%async_computation.4 | async-start | bytes 2097152 | tf_op jit(solution)/shard_map/all_to_all | solution.py:333

commit v9 on v7

--- a/solution.py
+++ b/solution.py
@@ -231,12 +231,22 @@
         parts[s, pl.ds(TILE, CENTER_ROWS)] = jnp.broadcast_to(center, (CENTER_ROWS, F))
 
 
-def pass_kernel(picks, column, out, sem):
+def send_picked(picks, column, out, sem):
     def send(i):
         chosen = (i & (SIDE - 1)) * SPLIT + picks[i]
-        return pltpu.make_async_copy(column.at[chosen], out.at[i], sem)
-
-    loop(GROUP, lambda i: send(i).start())
+        pltpu.make_async_copy(column.at[chosen], out.at[i], sem).start()
+
+    loop(GROUP, send)
+
+
+def pass_kernel(picks, column, out, sem):
+    send_picked(picks, column, out, sem)
+    pltpu.make_async_copy(out, out, sem).wait()
+
+
+def pass_and_sum_kernel(picks, column, plane_sums, out, sums, sem):
+    send_picked(picks, column, out, sem)
+    sums[...] = jnp.sum(plane_sums[...], axis=0)
     pltpu.make_async_copy(out, out, sem).wait()
 
 
@@ -325,16 +335,8 @@
     def exchange(blocks, axes=GZ):
         return lax.all_to_all(blocks, axes, split_axis=0, concat_axis=0, tiled=True)
 
-    def spread(parts):
-        column = lax.all_gather(parts, "gz_1", axis=0, tiled=True)
-        outgoing = call(
-            pass_kernel, 0, 2 << 20,
-            out_shape=pltpu.HBM((GROUP,) + parts.shape[1:], bf16),
-            in_specs=[SMEM, VMEM],
-            out_specs=HBM,
-            scratch_shapes=[DMA],
-        )(picks, column)
-        return exchange(outgoing, "gz_0")
+    def gather(parts):
+        return lax.all_gather(parts, "gz_1", axis=0, tiled=True)
 
     picks, parts = call(
         begin_kernel, 0, 1 << 18, room=60 << 20,
@@ -343,7 +345,14 @@
         out_specs=(SMEM, VMEM),
         scratch_shapes=[pltpu.SMEM((GROUP * HOST,), jnp.int32)] * 2 + [DMA((3,))],
     )(host_root, host_block, rows)
-    incoming = spread(parts)
+    outgoing = call(
+        pass_kernel, 0, 2 << 20,
+        out_shape=wire,
+        in_specs=[SMEM, VMEM],
+        out_specs=HBM,
+        scratch_shapes=[DMA],
+    )(picks, gather(parts))
+    incoming = exchange(outgoing, "gz_0")
 
     table, view, ready = call(
         tables_kernel, 0, 8 << 20,
@@ -387,8 +396,19 @@
         scratch_shapes=[pltpu.VMEM((SPLIT, TILE, F), f32)],
     )(table, returned, part_split, self_split, own_sums, neigh_one)
     plane_sums = exchange(sums, PLANE)
-    incoming = spread(parts)
-    sums = lax.psum(lax.psum(jnp.sum(plane_sums, axis=0), ("gy_0", "gy_1")), "gz_1")
+    column = gather(parts)
+    outgoing, sums = call(
+        pass_and_sum_kernel, 0, 2 << 20,
+        out_shape=(
+            pltpu.HBM((GROUP, TILE + CENTER_ROWS, F), bf16),
+            pltpu.VMEM((2, F), f32),
+        ),
+        in_specs=[SMEM, VMEM, VMEM],
+        out_specs=(HBM, VMEM),
+        scratch_shapes=[DMA],
+    )(picks, column, plane_sums)
+    incoming = exchange(outgoing, "gz_0")
+    sums = lax.psum(lax.psum(sums, ("gy_0", "gy_1")), "gz_1")
 
     outgoing, view = call(
         functools.partial(hidden_kernel, count), 64 * MAC, 5 << 20,

time: 163 us -> 163 us (level)
  the two profiles are of different devices: /device:TPU:88 before, /device:TPU:64 now
where the time goes in v9:
time: 163 us; the launch traced here: 162 us
  waiting for transfers between devices  59.3 us (36%)
  blocking collectives  52.3 us (32%)
  starting transfers between devices  29.4 us (18%)
  Pallas kernels  20.9 us (13%)
    all_to_all x5, waiting for transfers between devices, exchange(): return lax.all_to_all(blocks, axes, split_axis=0, concat_axis=0, tiled=True)  59.3 us
    all_gather x2, blocking collectives, gather(): return lax.all_gather(parts, 'gz_1', axis=0, tiled=True)  36.1 us
    all_to_all x5, starting transfers between devices, exchange(): return lax.all_to_all(blocks, axes, split_axis=0, concat_axis=0, tiled=True)  29.4 us
    psum x2, blocking collectives, layers(): sums = lax.psum(lax.psum(sums, ('gy_0', 'gy_1')), 'gz_1')  16.2 us
    pallas_call x1, Pallas kernels, layers(): call(own_two_kernel, 60 * MAC, 5 << 20, out_shape=(shape((ROOTED, TILE, F...  3.82 us
    pallas_call x1, Pallas kernels, layers(): call(own_kernel, 60 * MAC, 5 << 20, out_shape=(pltpu.VMEM((OWN, TILE, F),...  3.29 us
  transfers between devices with their start and end apart: 5, of which 3 were waited for; matrix products, arithmetic and copies ran while one was open for 0% of the time, Pallas kernels for 6%

profile of v9, /device:TPU:64, one launch (start us, length us, event | category | flops | bytes accessed | tf_op | source)
XLA Modules:
  0.0 162.3 jit_solution(5972829660692134936)
XLA Ops:
  0.0 1.1 shard_map.119
  1.1 21.0 %all_gather.6.column = bf16[8,128,256]{2,1,0:T(8,128)(2,1)S(1)} all-gather(bf16[2,128,256]{2,1,0:T(8,128)(2,1)S(1)} %get-tuple-element.29), channel_id=1, replica_groups=mesh['gx'=8,'gy_0'=2,'gy_1'=2,'gz_0'=4,'gz_1'=4] {'gz_1'}, dimensions={0}, use_global_device_ids=true | all-gather | bytes 655360 | tf_op jit(solution)/shard_map/all_gather | solution.py:339
  22.1 1.0 shard_map.120
  23.1 0.0 copy-start.9
  23.1 0.0 copy-start.10
  23.1 0.0 copy-start
  23.1 0.0 copy-start.5
  23.1 0.0 copy-start.6
  23.2 4.4 %all-to-all-start = ((bf16[16,128,256]{2,1,0:T(8,128)(2,1)}), bf16[16,128,256]{2,1,0:T(8,128)(2,1)S(1)}, u32[]{:S(2)}, u32[]{:S(2)}) async-start(bf16[16,128,256]{2,1,0:T(8,128)(2,1)} %shard_map.120), calls=%async_computation | async-start | bytes 2097152 | tf_op jit(solution)/shard_map/all_to_all | solution.py:336
  27.6 0.1 copy.17.cols
  27.7 0.1 copy.18.present
  27.8 2.2 %shard_map.118 = (s32[136]{0:T(256)S(4)}, bf16[15,128,256]{2,1,0:T(8,128)(2,1)S(1)}, bf16[4,8,128,128]{3,2,1,0:T(8,128)(2,1)S(1)}) custom-call(s32[128]{0:T(128)S(1)} %copy-done.5, s32[128]{0:T(128)S(1)} %copy-done.6, s32[14,8]{1,0:T(8,128)S(1)} %copy.17.cols, s32[14,8]{1,0:T(8,128)S(1)} %copy.18.present, bf16[6,128,256]{2,1,0:T(8,128)(2,1)S(1)} %bitcast.5, ...), custom_call_target="tpu_custom_call" | custom-call | bytes 8388608 | tf_op jit(solution)/shard_map/pallas_call | solution.py:357
  30.0 12.4 %all-to-all-done.incoming = bf16[16,128,256]{2,1,0:T(8,128)(2,1)S(1)} async-done(((bf16[16,128,256]{2,1,0:T(8,128)(2,1)}), bf16[16,128,256]{2,1,0:T(8,128)(2,1)S(1)}, u32[]{:S(2)}, u32[]{:S(2)}) %all-to-all-start) | async-done | bytes 1048608 | tf_op jit(solution)/shard_map/all_to_all | solution.py:336
  42.4 3.1 %shard_map.121 = (bf16[16,128,256]{2,1,0:T(8,128)(2,1)}, bf16[15,128,256]{2,1,0:T(8,128)(2,1)S(1)}) custom-call(s32[136]{0:T(256)S(4)} %get-tuple-element.26.table, bf16[15,128,256]{2,1,0:T(8,128)(2,1)S(1)} %get-tuple-element.28.begun, bf16[16,128,256]{2,1,0:T(8,128)(2,1)S(1)} %all-to-all-done.incoming, ...), custom_call_target="tpu_custom_call", output_to_operand_aliasing={{1}: (1, {})} | custom-call | flops 536870912 | bytes 4194304 | tf_op jit(solution)/shard_map/pallas_call | solution.py:369
  45.4 0.0 copy-start.1
  45.5 0.0 copy-start.3
  45.5 4.7 %all-to-all-start.1 = ((bf16[16,128,256]{2,1,0:T(8,128)(2,1)}), bf16[16,128,256]{2,1,0:T(8,128)(2,1)S(1)}, u32[]{:S(2)}, u32[]{:S(2)}) async-start(bf16[16,128,256]{2,1,0:T(8,128)(2,1)} %get-tuple-element.31), calls=%async_computation.1 | async-start | bytes 2097152 | tf_op jit(solution)/shard_map/all_to_all | solution.py:336
  50.2 3.3 %shard_map.122 = (f32[4,128,256]{2,1,0:T(8,128)S(1)}, f32[2,128,256]{2,1,0:T(8,128)S(1)}, f32[2,128,256]{2,1,0:T(8,128)S(1)}, f32[2,256]{1,0:T(2,128)S(1)}) custom-call(s32[136]{0:T(256)S(4)} %get-tuple-element.26.table, bf16[15,128,256]{2,1,0:T(8,128)(2,1)S(1)} %get-tuple-element.32.view, bf16[14,8,128,128]{3,2,1,0:T(8,128)(2,1)} %tiles.9, ...), custom_call_target="tpu_custom_call" | custom-call | flops 503316480 | bytes 5242880 | tf_op jit(solution)/shard_map/pallas_call | solution.py:379
  53.5 23.4 %all-to-all-done.1.incoming = bf16[16,128,256]{2,1,0:T(8,128)(2,1)S(1)} async-done(((bf16[16,128,256]{2,1,0:T(8,128)(2,1)}), bf16[16,128,256]{2,1,0:T(8,128)(2,1)S(1)}, u32[]{:S(2)}, u32[]{:S(2)}) %all-to-all-start.1) | async-done | bytes 1048608 | tf_op jit(solution)/shard_map/all_to_all | solution.py:336
  76.9 1.3 shard_map.123
  78.2 7.9 %all-to-all-start.2 = ((f32[32,2,256]{2,1,0:T(2,128)}), f32[32,2,256]{2,1,0:T(2,128)S(1)}, u32[]{:S(2)}, u32[]{:S(2)}) async-start(f32[32,2,256]{2,1,0:T(2,128)} %get-tuple-element.37), calls=%async_computation.2 | async-start | bytes 131072 | tf_op jit(solution)/shard_map/all_to_all | solution.py:336
  86.2 15.1 %all_gather.7.column = bf16[8,144,256]{2,1,0:T(8,128)(2,1)S(1)} all-gather(bf16[2,144,256]{2,1,0:T(8,128)(2,1)S(1)} %get-tuple-element.36), channel_id=1, replica_groups=mesh['gx'=8,'gy_0'=2,'gy_1'=2,'gz_0'=4,'gz_1'=4] {'gz_1'}, dimensions={0}, use_global_device_ids=true | all-gather | bytes 737280 | tf_op jit(solution)/shard_map/all_gather | solution.py:339
  101.2 1.0 shard_map.124
  102.3 4.6 %all-to-all-start.3 = ((bf16[16,144,256]{2,1,0:T(8,128)(2,1)}), bf16[16,144,256]{2,1,0:T(8,128)(2,1)S(1)}, u32[]{:S(2)}, u32[]{:S(2)}) async-start(bf16[16,144,256]{2,1,0:T(8,128)(2,1)} %get-tuple-element.41), calls=%async_computation.3 | async-start | bytes 2359296 | tf_op jit(solution)/shard_map/all_to_all | solution.py:336
  106.9 5.9 %psum.14 = f32[2,256]{1,0:T(2,128)S(1)} all-reduce(f32[2,256]{1,0:T(2,128)S(1)} %get-tuple-element.38), channel_id=1, replica_groups=mesh['gx'=8,'gy_0'=2,'gy_1'=2,'gz_0'=4,'gz_1'=4] {'gy_0','gy_1'}, use_global_device_ids=true, to_apply=%region_0.0 | all-reduce | flops 512 | bytes 4096 | tf_op jit(solution)/shard_map/psum | solution.py:411
  112.8 10.3 %psum.15.sums = f32[2,256]{1,0:T(2,128)S(1)} all-reduce(f32[2,256]{1,0:T(2,128)S(1)} %psum.14), channel_id=1, replica_groups=mesh['gx'=8,'gy_0'=2,'gy_1'=2,'gz_0'=4,'gz_1'=4] {'gz_1'}, use_global_device_ids=true, to_apply=%region_1.0 | all-reduce | flops 512 | bytes 4096 | tf_op jit(solution)/shard_map/psum | solution.py:411
  123.1 2.9 %shard_map.125 = (bf16[16,128,256]{2,1,0:T(8,128)(2,1)}, bf16[15,128,256]{2,1,0:T(8,128)(2,1)S(1)}) custom-call(s32[136]{0:T(256)S(4)} %get-tuple-element.26.table, f32[2,256]{1,0:T(2,128)S(1)} %psum.15.sums, f32[1,256]{1,0:T(1,128)S(1)} %bitcast.6, f32[1,256]{1,0:T(1,128)S(1)} %bitcast.7, f32[4,128,256]{2,1,0:T(8,128)S(1)} %get-tuple-element.39.first_own, ...), custom_call_target="tpu_custom_call" | custom-call | flops 536870912 | bytes 5242880 | tf_op jit(solution)/shard_map/pallas_call | solution.py:413
  126.0 0.0 copy-start.2
  126.0 7.7 %all-to-all-start.4 = ((bf16[16,128,256]{2,1,0:T(8,128)(2,1)}), bf16[16,128,256]{2,1,0:T(8,128)(2,1)S(1)}, u32[]{:S(2)}, u32[]{:S(2)}) async-start(bf16[16,128,256]{2,1,0:T(8,128)(2,1)} %get-tuple-element.42), calls=%async_computation.4 | async-start | bytes 2097152 | tf_op jit(solution)/shard_map/all_to_all | solution.py:336
  133.8 3.8 %shard_map.126 = (bf16[6,128,256]{2,1,0:T(8,128)(2,1)}, f32[2,128,256]{2,1,0:T(8,128)S(1)}, f32[2,128,256]{2,1,0:T(8,128)S(1)}) custom-call(s32[136]{0:T(256)S(4)} %get-tuple-element.26.table, bf16[15,128,256]{2,1,0:T(8,128)(2,1)S(1)} %get-tuple-element.43.view, bf16[14,8,128,128]{3,2,1,0:T(8,128)(2,1)} %tiles.9, bf16[256,256]{1,0:T(8,128)(2,1)S(1)} %copy-done.4, ...), custom_call_target="tpu_custom_call" | custom-call | flops 503316480 | bytes 5242880 | tf_op jit(solution)/shard_map/pallas_call | solution.py:422
  137.6 23.6 %all-to-all-done.4.incoming = bf16[16,128,256]{2,1,0:T(8,128)(2,1)S(1)} async-done(((bf16[16,128,256]{2,1,0:T(8,128)(2,1)}), bf16[16,128,256]{2,1,0:T(8,128)(2,1)S(1)}, u32[]{:S(2)}, u32[]{:S(2)}) %all-to-all-start.4) | async-done | bytes 1048608 | tf_op jit(solution)/shard_map/all_to_all | solution.py:336
  161.2 1.2 shard_map.127
  (16 shorter events, 0.0 us)
Async XLA Ops:
  23.1 4.5 %copy-start.9 = (s32[14,8]{0,1:T(8,128)S(1)}, s32[14,8]{0,1:T(8,128)}, u32[]{:S(2)}) copy-start(s32[14,8]{0,1:T(8,128)} %param.14) | copy-start | bytes 1348
  23.1 4.6 %copy-start.10 = (s32[14,8]{0,1:T(8,128)S(1)}, s32[14,8]{0,1:T(8,128)}, u32[]{:S(2)}) copy-start(s32[14,8]{0,1:T(8,128)} %param.15) | copy-start | bytes 1348
  23.1 4.6 %copy-start = (bf16[768,256]{1,0:T(8,128)(2,1)S(1)}, bf16[768,256]{1,0:T(8,128)(2,1)}, u32[]{:S(2)}) copy-start(bf16[768,256]{1,0:T(8,128)(2,1)} %param.12) | copy-start | bytes 1179652
  23.1 4.6 %copy-start.5 = (s32[128]{0:T(128)S(1)}, s32[128]{0:T(128)}, u32[]{:S(2)}) copy-start(s32[128]{0:T(128)} %root.3) | copy-start | bytes 1540
  23.1 4.6 %copy-start.6 = (s32[128]{0:T(128)S(1)}, s32[128]{0:T(128)}, u32[]{:S(2)}) copy-start(s32[128]{0:T(128)} %block.3) | copy-start | bytes 1540
  23.2 19.2 %all-to-all-start = ((bf16[16,128,256]{2,1,0:T(8,128)(2,1)}), bf16[16,128,256]{2,1,0:T(8,128)(2,1)S(1)}, u32[]{:S(2)}, u32[]{:S(2)}) async-start(bf16[16,128,256]{2,1,0:T(8,128)(2,1)} %shard_map.120), calls=%async_computation | async-start | bytes 2097152 | tf_op jit(solution)/shard_map/all_to_all | solution.py:336
  45.4 4.8 %copy-start.1 = (bf16[256,256]{1,0:T(8,128)(2,1)S(1)}, bf16[256,256]{1,0:T(8,128)(2,1)}, u32[]{:S(2)}) copy-start(bf16[256,256]{1,0:T(8,128)(2,1)} %w_neigh.5) | copy-start | bytes 393220
  45.5 4.8 %copy-start.3 = (bf16[256,256]{1,0:T(8,128)(2,1)S(1)}, bf16[256,256]{1,0:T(8,128)(2,1)}, u32[]{:S(2)}) copy-start(bf16[256,256]{1,0:T(8,128)(2,1)} %w_self.2) | copy-start | bytes 393220
  45.5 31.4 %all-to-all-start.1 = ((bf16[16,128,256]{2,1,0:T(8,128)(2,1)}), bf16[16,128,256]{2,1,0:T(8,128)(2,1)S(1)}, u32[]{:S(2)}, u32[]{:S(2)}) async-start(bf16[16,128,256]{2,1,0:T(8,128)(2,1)} %get-tuple-element.31), calls=%async_computation.1 | async-start | bytes 2097152 | tf_op jit(solution)/shard_map/all_to_all | solution.py:336
  78.2 23.0 %all-to-all-start.2 = ((f32[32,2,256]{2,1,0:T(2,128)}), f32[32,2,256]{2,1,0:T(2,128)S(1)}, u32[]{:S(2)}, u32[]{:S(2)}) async-start(f32[32,2,256]{2,1,0:T(2,128)} %get-tuple-element.37), calls=%async_computation.2 | async-start | bytes 131072 | tf_op jit(solution)/shard_map/all_to_all | solution.py:336
  102.3 20.8 %copy-start.7 = (f32[256]{0:T(256)S(1)}, f32[256]{0:T(256)}, u32[]{:S(2)}) copy-start(f32[256]{0:T(256)} %param.20) | copy-start | bytes 3076
  102.3 20.8 %copy-start.8 = (f32[256]{0:T(256)S(1)}, f32[256]{0:T(256)}, u32[]{:S(2)}) copy-start(f32[256]{0:T(256)} %param.21) | copy-start | bytes 3076
  102.3 20.8 %all-to-all-start.3 = ((bf16[16,144,256]{2,1,0:T(8,128)(2,1)}), bf16[16,144,256]{2,1,0:T(8,128)(2,1)S(1)}, u32[]{:S(2)}, u32[]{:S(2)}) async-start(bf16[16,144,256]{2,1,0:T(8,128)(2,1)} %get-tuple-element.41), calls=%async_computation.3 | async-start | bytes 2359296 | tf_op jit(solution)/shard_map/all_to_all | solution.py:336
  126.0 7.8 %copy-start.2 = (bf16[256,256]{1,0:T(8,128)(2,1)S(1)}, bf16[256,256]{1,0:T(8,128)(2,1)}, u32[]{:S(2)}) copy-start(bf16[256,256]{1,0:T(8,128)(2,1)} %w_neigh.7) | copy-start | bytes 393220
  126.0 7.8 %copy-start.4 = (bf16[256,256]{1,0:T(8,128)(2,1)S(1)}, bf16[256,256]{1,0:T(8,128)(2,1)}, u32[]{:S(2)}) copy-start(bf16[256,256]{1,0:T(8,128)(2,1)} %w_self.3) | copy-start | bytes 393220
  126.0 35.1 %all-to-all-start.4 = ((bf16[16,128,256]{2,1,0:T(8,128)(2,1)}), bf16[16,128,256]{2,1,0:T(8,128)(2,1)S(1)}, u32[]{:S(2)}, u32[]{:S(2)}) async-start(bf16[16,128,256]{2,1,0:T(8,128)(2,1)} %get-tuple-element.42), calls=%async_computation.4 | async-start | bytes 2097152 | tf_op jit(solution)/shard_map/all_to_all | solution.py:336
